TPU v7x, 32 devices: a whole 2x2x4 slice. The times are simulated.
32 devices in a mesh: rep: 4 (over x, core), shard: 8 (over z, y).
Axes of the slice: x: 2, y: 2, z: 4, core: 2. Of those that a mesh axis runs over, the one named last changes fastest.
Arguments:
- decoder_states: bfloat16 [32768, 1024], P(('rep', 'shard')), may hold values from -6 to 6
- encoder_states: bfloat16 [8192, 1024], P(('rep', 'shard')), may hold values from -6 to 6
- piece_starts: int32 [32, 2], P(('rep', 'shard')), may hold values from 0 to 768, as said below
- out_cotangent: bfloat16 [32768, 1024], P(('rep', 'shard')), may hold values from -6 to 6
- self_query: bfloat16 [1024, 1024], P('shard'), may hold values from -0.1875 to 0.1875
- self_key: bfloat16 [1024, 1024], P('shard'), may hold values from -0.1875 to 0.1875
- self_value: bfloat16 [1024, 1024], P('shard'), may hold values from -0.1875 to 0.1875
- self_out: bfloat16 [1024, 1024], P('shard'), may hold values from -1 to 1
- cross_query: bfloat16 [1024, 1024], P('shard'), may hold values from -0.1875 to 0.1875
- cross_key: bfloat16 [1024, 1024], P('shard'), may hold values from -0.1875 to 0.1875
- cross_value: bfloat16 [1024, 1024], P('shard'), may hold values from -0.1875 to 0.1875
- cross_out: bfloat16 [1024, 1024], P('shard'), may hold values from -1 to 1
- expand_weight: bfloat16 [1024, 4096], P('shard'), may hold values from -0.1875 to 0.1875
- contract_weight: bfloat16 [4096, 1024], P('shard'), may hold values from -0.125 to 0.125
- self_gain: bfloat16 [1024], P('shard'), may hold values from 0.25 to 1.75
- self_shift: bfloat16 [1024], P('shard'), may hold values from -1.5 to 1.5
- cross_gain: bfloat16 [1024], P('shard'), may hold values from 0.25 to 1.75
- cross_shift: bfloat16 [1024], P('shard'), may hold values from -1.5 to 1.5
- mlp_gain: bfloat16 [1024], P('shard'), may hold values from 0.25 to 1.75
- mlp_shift: bfloat16 [1024], P('shard'), may hold values from -1.5 to 1.5
Outputs:
- layer_out: bfloat16 [32768, 1024], P(('rep', 'shard'))
- grad_decoder: float32 [32768, 1024], P(('rep', 'shard'))
- grad_encoder: float32 [8192, 1024], P(('rep', 'shard'))
- grad_self_query: float32 [1024, 1024], P('shard')
- grad_self_key: float32 [1024, 1024], P('shard')
- grad_self_value: float32 [1024, 1024], P('shard')
- grad_self_out: float32 [1024, 1024], P('shard')
- grad_cross_query: float32 [1024, 1024], P('shard')
- grad_cross_key: float32 [1024, 1024], P('shard')
- grad_cross_value: float32 [1024, 1024], P('shard')
- grad_cross_out: float32 [1024, 1024], P('shard')
- grad_expand: float32 [1024, 4096], P('shard')
- grad_contract: float32 [4096, 1024], P('shard')
- grad_self_gain: float32 [1024], P('shard')
- grad_self_shift: float32 [1024], P('shard')
- grad_cross_gain: float32 [1024], P('shard')
- grad_cross_shift: float32 [1024], P('shard')
- grad_mlp_gain: float32 [1024], P('shard')
- grad_mlp_shift: float32 [1024], P('shard')
Inputs may be any that keep to these rules, and one draw needn't show every extreme that they name: `piece_starts`: row s holds the first positions of the 2 picture pieces of sequence s in increasing order; piece p starts within positions p * (512) to (p + 1) * 512 - 256, so pieces lie inside the sequence and never intersect.
All inputs are finite; a program needn't handle non-finite values.
Results may differ from a plain program's by a relative error of at most 0.025.
Values may be sent and summed in bfloat16 or wider, within the bound.
A program may use at most 320 MiB of HBM per device.

v0:
```python
import jax
import jax.numpy as jnp
from jax import lax
from jax.sharding import PartitionSpec as P

HD = 64
PIC = 256


EPS = 1e-05
NEGATIVE = -1e30
INV_ROOT_TWO = 0.7071067811865476
INV_ROOT_TWO_PI = 0.3989422804014327


def norm_forward(resid, gain, shift):
    mean = jnp.mean(resid, -1, keepdims=True)
    centred = resid - mean
    variance = jnp.mean(centred * centred, -1, keepdims=True)
    inverse = lax.rsqrt(variance + EPS)
    normed = centred * inverse
    return (normed * gain + shift, normed, inverse)


def norm_backward(grad_out, normed, inverse, gain):
    grad_gain = jnp.sum(grad_out * normed, 0)
    grad_shift = jnp.sum(grad_out, 0)
    grad_normed = grad_out * gain
    centre_term = jnp.mean(grad_normed, -1, keepdims=True)
    slope_term = jnp.mean(grad_normed * normed, -1, keepdims=True)
    return (inverse * (grad_normed - centre_term - normed * slope_term), grad_gain, grad_shift)


def attend_forward(queries, keys, values, allowed, block):
    rows = queries.shape[0]
    count = rows // block
    q_blocks = queries.reshape(count, block, -1, HD)
    k_heads = keys.reshape(keys.shape[0], -1, HD)
    v_heads = values.reshape(values.shape[0], -1, HD)
    firsts = jnp.arange(count, dtype=jnp.int32) * block

    def one_block(item):
        q_block, first = item
        scores = jnp.einsum("qhd,khd->hqk", q_block, k_heads, preferred_element_type=jnp.float32)
        scores = jnp.where(allowed(first, block)[None], scores, NEGATIVE)
        top = jnp.max(scores, -1, keepdims=True)
        expd = jnp.exp(scores - top)
        total = jnp.sum(expd, -1, keepdims=True)
        probs = (expd / total).astype(jnp.bfloat16)
        mixed = jnp.einsum("hqk,khd->qhd", probs, v_heads, preferred_element_type=jnp.float32)
        return (mixed, (top + jnp.log(total))[..., 0])

    mixed, logsum = lax.map(one_block, (q_blocks, firsts))
    return (mixed.reshape(rows, -1), logsum)


def attend_backward(queries, keys, values, grad_mixed, logsum, allowed, block):
    rows = queries.shape[0]
    count = rows // block
    q_blocks = queries.reshape(count, block, -1, HD)
    g_blocks = grad_mixed.reshape(count, block, -1, HD)
    k_heads = keys.reshape(keys.shape[0], -1, HD)
    v_heads = values.reshape(values.shape[0], -1, HD)
    firsts = jnp.arange(count, dtype=jnp.int32) * block

    def one_block(carry, item):
        grad_keys, grad_values = carry
        q_block, g_block, lse, first = item
        scores = jnp.einsum("qhd,khd->hqk", q_block, k_heads, preferred_element_type=jnp.float32)
        probs = jnp.where(allowed(first, block)[None], jnp.exp(scores - lse[..., None]), 0.0)
        grad_probs = jnp.einsum(
            "qhd,khd->hqk", g_block, v_heads, preferred_element_type=jnp.float32
        )
        delta = jnp.sum(probs * grad_probs, -1, keepdims=True)
        grad_scores = (probs * (grad_probs - delta)).astype(jnp.bfloat16)
        grad_q = jnp.einsum(
            "hqk,khd->qhd", grad_scores, k_heads, preferred_element_type=jnp.float32
        )
        grad_keys = grad_keys + jnp.einsum(
            "hqk,qhd->khd", grad_scores, q_block, preferred_element_type=jnp.float32
        )
        grad_values = grad_values + jnp.einsum(
            "hqk,qhd->khd", probs.astype(jnp.bfloat16), g_block, preferred_element_type=jnp.float32
        )
        return ((grad_keys, grad_values), grad_q)

    zeros = jnp.zeros(k_heads.shape, jnp.float32)
    (grad_keys, grad_values), grad_q = lax.scan(
        one_block, (zeros, zeros), (q_blocks, g_blocks, logsum, firsts)
    )
    return (
        grad_q.reshape(rows, -1),
        grad_keys.reshape(keys.shape[0], -1),
        grad_values.reshape(values.shape[0], -1),
    )


def matmul(left, right):
    return jnp.dot(left, right, preferred_element_type=jnp.float32)


def body(
    decoder_states,
    encoder_states,
    piece_starts,
    out_cotangent,
    self_query,
    self_key,
    self_value,
    self_out,
    cross_query,
    cross_key,
    cross_value,
    cross_out,
    expand_weight,
    contract_weight,
    self_gain,
    self_shift,
    cross_gain,
    cross_shift,
    mlp_gain,
    mlp_shift,
):
    rows = decoder_states.shape[0]
    enc_rows = encoder_states.shape[0]
    block = min(rows, 512)
    scale = HD ** (-0.5)
    (
        full_self_query,
        full_self_key,
        full_self_value,
        full_self_out,
        full_cross_query,
        full_cross_key,
        full_cross_value,
        full_cross_out,
        full_self_gain,
        full_self_shift,
        full_cross_gain,
        full_cross_shift,
    ) = (
        lax.all_gather(self_query, "shard", axis=0, tiled=True),
        lax.all_gather(self_key, "shard", axis=0, tiled=True),
        lax.all_gather(self_value, "shard", axis=0, tiled=True),
        lax.all_gather(self_out, "shard", axis=0, tiled=True),
        lax.all_gather(cross_query, "shard", axis=0, tiled=True),
        lax.all_gather(cross_key, "shard", axis=0, tiled=True),
        lax.all_gather(cross_value, "shard", axis=0, tiled=True),
        lax.all_gather(cross_out, "shard", axis=0, tiled=True),
        lax.all_gather(self_gain, "shard", axis=0, tiled=True),
        lax.all_gather(self_shift, "shard", axis=0, tiled=True),
        lax.all_gather(cross_gain, "shard", axis=0, tiled=True),
        lax.all_gather(cross_shift, "shard", axis=0, tiled=True),
    )
    full_expand, full_contract, full_mlp_gain, full_mlp_shift = (
        lax.all_gather(expand_weight, "shard", axis=0, tiled=True),
        lax.all_gather(contract_weight, "shard", axis=0, tiled=True),
        lax.all_gather(mlp_gain, "shard", axis=0, tiled=True),
        lax.all_gather(mlp_shift, "shard", axis=0, tiled=True),
    )
    positions = jnp.arange(rows, dtype=jnp.int32)
    starts_row = piece_starts[0]
    inside = (
        (positions[:, None] >= starts_row[None, :])
        & (positions[:, None] < starts_row[None, :] + PIC)
    ).astype(jnp.float32)

    def self_allowed(first, count):
        rows_here = first + jnp.arange(count, dtype=jnp.int32)
        inside_here = lax.dynamic_slice_in_dim(inside, first, count, 0)
        same_piece = jnp.dot(inside_here, inside.T) > 0.5
        return (positions[None, :] <= rows_here[:, None]) | same_piece

    def cross_allowed(first, count):
        return jnp.ones((count, enc_rows), dtype=bool)

    states_wide = decoder_states.astype(jnp.float32)
    query_self = (matmul(decoder_states, full_self_query) * scale).astype(jnp.bfloat16)
    key_self = matmul(decoder_states, full_self_key).astype(jnp.bfloat16)
    value_self = matmul(decoder_states, full_self_value).astype(jnp.bfloat16)
    mixed_self, logsum_self = attend_forward(query_self, key_self, value_self, self_allowed, block)
    mixed_self = mixed_self.astype(jnp.bfloat16)
    resid_one = states_wide + matmul(mixed_self, full_self_out)
    hidden_one, normed_one, inverse_one = norm_forward(
        resid_one, full_self_gain.astype(jnp.float32), full_self_shift.astype(jnp.float32)
    )
    hidden_one_low = hidden_one.astype(jnp.bfloat16)
    query_cross = (matmul(hidden_one_low, full_cross_query) * scale).astype(jnp.bfloat16)
    key_cross = matmul(encoder_states, full_cross_key).astype(jnp.bfloat16)
    value_cross = matmul(encoder_states, full_cross_value).astype(jnp.bfloat16)
    mixed_cross, logsum_cross = attend_forward(
        query_cross, key_cross, value_cross, cross_allowed, block
    )
    mixed_cross = mixed_cross.astype(jnp.bfloat16)
    resid_two = hidden_one + matmul(mixed_cross, full_cross_out)
    hidden_two, normed_two, inverse_two = norm_forward(
        resid_two, full_cross_gain.astype(jnp.float32), full_cross_shift.astype(jnp.float32)
    )
    hidden_two_low = hidden_two.astype(jnp.bfloat16)
    pre_act = matmul(hidden_two_low, full_expand)
    active = jax.nn.gelu(pre_act, approximate=False).astype(jnp.bfloat16)
    resid_three = hidden_two + matmul(active, full_contract)
    final, normed_three, inverse_three = norm_forward(
        resid_three, full_mlp_gain.astype(jnp.float32), full_mlp_shift.astype(jnp.float32)
    )
    back_expand, back_contract, back_mlp_gain = (
        lax.all_gather(expand_weight, "shard", axis=0, tiled=True),
        lax.all_gather(contract_weight, "shard", axis=0, tiled=True),
        lax.all_gather(mlp_gain, "shard", axis=0, tiled=True),
    )
    (
        back_self_query,
        back_self_key,
        back_self_value,
        back_self_out,
        back_cross_query,
        back_cross_key,
        back_cross_value,
        back_cross_out,
        back_self_gain,
        back_cross_gain,
    ) = (
        lax.all_gather(self_query, "shard", axis=0, tiled=True),
        lax.all_gather(self_key, "shard", axis=0, tiled=True),
        lax.all_gather(self_value, "shard", axis=0, tiled=True),
        lax.all_gather(self_out, "shard", axis=0, tiled=True),
        lax.all_gather(cross_query, "shard", axis=0, tiled=True),
        lax.all_gather(cross_key, "shard", axis=0, tiled=True),
        lax.all_gather(cross_value, "shard", axis=0, tiled=True),
        lax.all_gather(cross_out, "shard", axis=0, tiled=True),
        lax.all_gather(self_gain, "shard", axis=0, tiled=True),
        lax.all_gather(cross_gain, "shard", axis=0, tiled=True),
    )
    grad_top = out_cotangent.astype(jnp.float32)
    grad_resid_three, grad_mlp_gain, grad_mlp_shift = norm_backward(
        grad_top, normed_three, inverse_three, back_mlp_gain.astype(jnp.float32)
    )
    branch_three = grad_resid_three.astype(jnp.bfloat16)
    grad_contract = matmul(active.T, branch_three)
    grad_active = matmul(branch_three, back_contract.T)
    slope = (
        0.5 * (1.0 + lax.erf(pre_act * INV_ROOT_TWO))
        + pre_act * jnp.exp(-0.5 * pre_act * pre_act) * INV_ROOT_TWO_PI
    )
    grad_pre = (grad_active * slope).astype(jnp.bfloat16)
    grad_expand = matmul(hidden_two_low.T, grad_pre)
    grad_hidden_two = grad_resid_three + matmul(grad_pre, back_expand.T)
    grad_resid_two, grad_cross_gain, grad_cross_shift = norm_backward(
        grad_hidden_two, normed_two, inverse_two, back_cross_gain.astype(jnp.float32)
    )
    branch_two = grad_resid_two.astype(jnp.bfloat16)
    grad_cross_out = matmul(mixed_cross.T, branch_two)
    grad_mixed_cross = matmul(branch_two, back_cross_out.T).astype(jnp.bfloat16)
    grad_query, grad_key, grad_value = attend_backward(
        query_cross, key_cross, value_cross, grad_mixed_cross, logsum_cross, cross_allowed, block
    )
    grad_query = grad_query.astype(jnp.bfloat16) * scale
    grad_key = grad_key.astype(jnp.bfloat16)
    grad_value = grad_value.astype(jnp.bfloat16)
    grad_cross_query = matmul(hidden_one_low.T, grad_query)
    grad_cross_key = matmul(encoder_states.T, grad_key)
    grad_cross_value = matmul(encoder_states.T, grad_value)
    grad_encoder = matmul(grad_key, back_cross_key.T) + matmul(grad_value, back_cross_value.T)
    grad_hidden_one = grad_resid_two + matmul(grad_query, back_cross_query.T)
    grad_resid_one, grad_self_gain, grad_self_shift = norm_backward(
        grad_hidden_one, normed_one, inverse_one, back_self_gain.astype(jnp.float32)
    )
    branch_one = grad_resid_one.astype(jnp.bfloat16)
    grad_self_out = matmul(mixed_self.T, branch_one)
    grad_mixed_self = matmul(branch_one, back_self_out.T).astype(jnp.bfloat16)
    grad_query, grad_key, grad_value = attend_backward(
        query_self, key_self, value_self, grad_mixed_self, logsum_self, self_allowed, block
    )
    grad_query = grad_query.astype(jnp.bfloat16) * scale
    grad_key = grad_key.astype(jnp.bfloat16)
    grad_value = grad_value.astype(jnp.bfloat16)
    grad_self_query = matmul(decoder_states.T, grad_query)
    grad_self_key = matmul(decoder_states.T, grad_key)
    grad_self_value = matmul(decoder_states.T, grad_value)
    grad_decoder = (
        grad_resid_one
        + matmul(grad_query, back_self_query.T)
        + matmul(grad_key, back_self_key.T)
        + matmul(grad_value, back_self_value.T)
    )
    part_expand, part_contract, part_mlp_gain, part_mlp_shift = (
        lax.psum_scatter(grad_expand, "shard", scatter_dimension=0, tiled=True),
        lax.psum_scatter(grad_contract, "shard", scatter_dimension=0, tiled=True),
        lax.psum_scatter(grad_mlp_gain, "shard", scatter_dimension=0, tiled=True),
        lax.psum_scatter(grad_mlp_shift, "shard", scatter_dimension=0, tiled=True),
    )
    (
        part_sq,
        part_sk,
        part_sv,
        part_so,
        part_cq,
        part_ck,
        part_cv,
        part_co,
        part_self_gain,
        part_self_shift,
        part_cross_gain,
        part_cross_shift,
    ) = (
        lax.psum_scatter(grad_self_query, "shard", scatter_dimension=0, tiled=True),
        lax.psum_scatter(grad_self_key, "shard", scatter_dimension=0, tiled=True),
        lax.psum_scatter(grad_self_value, "shard", scatter_dimension=0, tiled=True),
        lax.psum_scatter(grad_self_out, "shard", scatter_dimension=0, tiled=True),
        lax.psum_scatter(grad_cross_query, "shard", scatter_dimension=0, tiled=True),
        lax.psum_scatter(grad_cross_key, "shard", scatter_dimension=0, tiled=True),
        lax.psum_scatter(grad_cross_value, "shard", scatter_dimension=0, tiled=True),
        lax.psum_scatter(grad_cross_out, "shard", scatter_dimension=0, tiled=True),
        lax.psum_scatter(grad_self_gain, "shard", scatter_dimension=0, tiled=True),
        lax.psum_scatter(grad_self_shift, "shard", scatter_dimension=0, tiled=True),
        lax.psum_scatter(grad_cross_gain, "shard", scatter_dimension=0, tiled=True),
        lax.psum_scatter(grad_cross_shift, "shard", scatter_dimension=0, tiled=True),
    )
    owned = (
        lax.psum(part_sq.astype(jnp.bfloat16), "rep").astype(jnp.float32),
        lax.psum(part_sk.astype(jnp.bfloat16), "rep").astype(jnp.float32),
        lax.psum(part_sv.astype(jnp.bfloat16), "rep").astype(jnp.float32),
        lax.psum(part_so.astype(jnp.bfloat16), "rep").astype(jnp.float32),
        lax.psum(part_cq.astype(jnp.bfloat16), "rep").astype(jnp.float32),
        lax.psum(part_ck.astype(jnp.bfloat16), "rep").astype(jnp.float32),
        lax.psum(part_cv.astype(jnp.bfloat16), "rep").astype(jnp.float32),
        lax.psum(part_co.astype(jnp.bfloat16), "rep").astype(jnp.float32),
        lax.psum(part_expand.astype(jnp.bfloat16), "rep").astype(jnp.float32),
        lax.psum(part_contract.astype(jnp.bfloat16), "rep").astype(jnp.float32),
        lax.psum(part_self_gain.astype(jnp.bfloat16), "rep").astype(jnp.float32),
        lax.psum(part_self_shift.astype(jnp.bfloat16), "rep").astype(jnp.float32),
        lax.psum(part_cross_gain.astype(jnp.bfloat16), "rep").astype(jnp.float32),
        lax.psum(part_cross_shift.astype(jnp.bfloat16), "rep").astype(jnp.float32),
        lax.psum(part_mlp_gain.astype(jnp.bfloat16), "rep").astype(jnp.float32),
        lax.psum(part_mlp_shift.astype(jnp.bfloat16), "rep").astype(jnp.float32),
    )
    return (
        final.astype(jnp.bfloat16),
        grad_decoder,
        grad_encoder,
        owned[0],
        owned[1],
        owned[2],
        owned[3],
        owned[4],
        owned[5],
        owned[6],
        owned[7],
        owned[8],
        owned[9],
        owned[10],
        owned[11],
        owned[12],
        owned[13],
        owned[14],
        owned[15],
    )


def solution(mesh):
    return jax.shard_map(
        body,
        mesh=mesh,
        in_specs=(
            P(("rep", "shard"), None),
            P(("rep", "shard"), None),
            P(("rep", "shard"), None),
            P(("rep", "shard"), None),
            P("shard", None),
            P("shard", None),
            P("shard", None),
            P("shard", None),
            P("shard", None),
            P("shard", None),
            P("shard", None),
            P("shard", None),
            P("shard", None),
            P("shard", None),
            P("shard"),
            P("shard"),
            P("shard"),
            P("shard"),
            P("shard"),
            P("shard"),
        ),
        out_specs=(
            P(("rep", "shard"), None),
            P(("rep", "shard"), None),
            P(("rep", "shard"), None),
            P("shard", None),
            P("shard", None),
            P("shard", None),
            P("shard", None),
            P("shard", None),
            P("shard", None),
            P("shard", None),
            P("shard", None),
            P("shard", None),
            P("shard", None),
            P("shard"),
            P("shard"),
            P("shard"),
            P("shard"),
            P("shard"),
            P("shard"),
        ),
        check_vma=False,
    )
```

profile of v0, /device:TPU:0, one launch (start us, length us, event | category | flops | bytes accessed | tf_op | source)
XLA Modules:
  0.0 2365.8 jit_solution(11785676272640436438)
XLA Ops:
  18.2 22.2 all-gather
  40.9 16.4 all-gather.1
  57.9 18.1 all-gather.2
  96.0 18.1 all-gather.4
  169.9 95.4 %while.56 = (s32[]{:T(128)}, bf16[2,512,16,64]{1,3,2,0:T(8,128)(2,1)}, f32[2,16,512]{2,1,0:T(8,128)S(1)}, s32[2]{0:T(128)S(1)}, bf16[1024,2]{0,1:T(2,128)(2,1)S(...) while((s32[]{:T(128)}, ...), condition=%wide.region_3.4_spmd.clone, body=%wide.region_0.3_spmd.clone.sunk | while | flops 2226643456 | bytes 127150816 | solution.py:53
  293.8 17.9 all-gather.27.cloned.1.call-done
  316.1 45.6 %all-gather.29.cloned.1.call-done = bf16[1024,1024]{1,0:T(8,128)(2,1)} async-done(((bf16[128,1024]{1,0:T(8,128)(2,1)}), bf16[1024,1024]{1,0:T(8,128)(2,1)}) %all-gather.29.cloned.1.call-update) | async-done | bytes 2097168 | tf_op jit(solution)/shard_map/all_gather | solution.py:148
  385.6 26.0 %all-gather.31.cloned.1.call-done = bf16[1024,1024]{1,0:T(8,128)(2,1)} async-done(((bf16[128,1024]{1,0:T(8,128)(2,1)}), bf16[1024,1024]{1,0:T(8,128)(2,1)}) %all-gather.31.cloned.1.call-update) | async-done | bytes 2097168 | tf_op jit(solution)/shard_map/all_gather | solution.py:149
  420.7 116.5 %all-gather.33.cloned.1.call-done = bf16[1024,4096]{1,0:T(8,128)(2,1)} async-done(((bf16[128,4096]{1,0:T(8,128)(2,1)}), bf16[1024,4096]{1,0:T(8,128)(2,1)}) %all-gather.33.cloned.1.call-update) | async-done | bytes 8388624 | tf_op jit(solution)/shard_map/all_gather | solution.py:156
  537.2 46.9 %fusion.73 = (bf16[1024,4096]{1,0:T(8,128)(2,1)}, f32[1024,4096]{1,0:T(8,128)}) fusion(bf16[1024,4096]{1,0:T(8,128)(2,1)} %all-gather.33.cloned.1.call-done, bf16[1024,1024]{0,1:T(8,128)(2,1)S(1)} %fusion.110.clone.4), kind=kOutput, calls=%fused_computation.91 | convolution fusion | flops 8862564352 | bytes 35651584 | tf_op jit(solution)/shard_map/dot_general | solution.py:99
  584.1 78.3 %all-gather.35.cloned.1.call-done = bf16[4096,1024]{1,0:T(8,128)(2,1)} async-done(((bf16[512,1024]{1,0:T(8,128)(2,1)}), bf16[4096,1024]{1,0:T(8,128)(2,1)}) %all-gather.35.cloned.1.call-update) | async-done | bytes 8388624 | tf_op jit(solution)/shard_map/all_gather | solution.py:157
  684.7 21.6 fusion.79
  706.3 17.3 multiply_reduce_fusion.2
  740.4 44.0 %while.57 = (s32[]{:T(128)}, f32[256,16,64]{0,2,1:T(8,128)}, f32[256,16,64]{0,2,1:T(8,128)}, bf16[2,512,16,64]{1,3,2,0:T(8,128)(2,1)}, bf16[2,512,16,64]{1,3,2,0...) while((s32[]{:T(128)}, f32[256,16,64]{0,2,1:T(8,128)}, ...), condition=%wide.region_20.21_spmd.clone, body=%wide.region_18.20_spmd.clone.sunk | while | flops 1362092032 | bytes 144409392 | solution.py:88
  817.5 216.9 %while.58 = (s32[]{:T(128)}, f32[1024,16,64]{0,2,1:T(8,128)}, f32[1024,16,64]{0,2,1:T(8,128)}, bf16[2,512,16,64]{1,3,2,0:T(8,128)(2,1)}, bf16[2,512,16,64]{1,3,2...) while((s32[]{:T(128)}, f32[1024,16,64]{0,2,1:T(8,128)}, ...), condition=%wide.region_25.26_spmd.clone, body=%wide.region_23.25_spmd.clone.sunk | while | flops 5477229056 | bytes 384151424 | solution.py:88
  836.2 24.5 %multiply_reduce_fusion.14 = (f32[16,512]{1,0:T(8,128)S(1)}, f32[16,512,1024]{2,1,0:T(8,128)}) fusion(f32[16,512,1024]{2,1,0:T(8,128)} %fusion.259, f32[16,512]{1,0:T(8,128)S(1)} %dynamic-slice_bitcast_fusion.5, pred[512,1024]{1,0:T(8,128)(4,1)S(1)} %fusion.260, bf16[1024,16,64]{0,2,1:T(8,128)(2,1)S(1)} %copy-done.14, ...), kind=kOutput, calls=%fused_computation.56.clone.1 | convolution fusion | flops 1107288064 | bytes 70844416 | tf_op jit(solution)/shard_map/while/body/eval_jaxpr/qhd,khd->hqk/dot_general | solution.py:71
  860.7 28.0 %multiply_convert_fusion.7 = bf16[16,512,1024]{2,1,0:T(8,128)(2,1)} fusion(f32[16,512,1024]{2,1,0:T(8,128)} %get-tuple-element.813, f32[16,512,1024]{2,1,0:T(8,128)} %fusion.259, f32[16,512]{1,0:T(8,128)S(1)} %get-tuple-element.814, f32[16,512]{1,0:T(8,128)S(1)} %dynamic-slice_bitcast_fusion.5, pred[512,1024]{1,0:T(8,128)(4,1)S(1)} %fusion.260), kind=kLoop, calls=%fused_computation.55.clone.1 | loop fusion | flops 41943040 | bytes 84475904 | tf_op jit(solution)/shard_map/while/body/eval_jaxpr/convert_element_type | solution.py:75
  943.1 24.5 %multiply_reduce_fusion.14 = (f32[16,512]{1,0:T(8,128)S(1)}, f32[16,512,1024]{2,1,0:T(8,128)}) fusion(f32[16,512,1024]{2,1,0:T(8,128)} %fusion.259, f32[16,512]{1,0:T(8,128)S(1)} %dynamic-slice_bitcast_fusion.5, pred[512,1024]{1,0:T(8,128)(4,1)S(1)} %fusion.260, bf16[1024,16,64]{0,2,1:T(8,128)(2,1)S(1)} %copy-done.14, ...), kind=kOutput, calls=%fused_computation.56.clone.1 | convolution fusion | flops 1107288064 | bytes 70844416 | tf_op jit(solution)/shard_map/while/body/eval_jaxpr/qhd,khd->hqk/dot_general | solution.py:71
  967.6 27.6 %multiply_convert_fusion.7 = bf16[16,512,1024]{2,1,0:T(8,128)(2,1)} fusion(f32[16,512,1024]{2,1,0:T(8,128)} %get-tuple-element.813, f32[16,512,1024]{2,1,0:T(8,128)} %fusion.259, f32[16,512]{1,0:T(8,128)S(1)} %get-tuple-element.814, f32[16,512]{1,0:T(8,128)S(1)} %dynamic-slice_bitcast_fusion.5, pred[512,1024]{1,0:T(8,128)(4,1)S(1)} %fusion.260), kind=kLoop, calls=%fused_computation.55.clone.1 | loop fusion | flops 41943040 | bytes 84475904 | tf_op jit(solution)/shard_map/while/body/eval_jaxpr/convert_element_type | solution.py:75
  1016.5 17.5 bitcast_add_fusion.5
  1087.4 17.3 fusion.104
  1105.4 16.7 fusion.107
  1124.0 36.1 %all-reduce.6 = (bf16[1024]{0:T(1024)(128)(2,1)S(1)}, bf16[1024]{0:T(1024)(128)(2,1)S(1)}, bf16[1024]{0:T(1024)(128)(2,1)S(1)}, bf16[1024]{0:T(1024)(128)(2,1)S(...) all-reduce(f32[1024]{0:T(1024)S(1)} %copy-done.91, ...), channel_id=12, replica_groups=mesh['rep'=4,'shard'=8] {'shard'}, use_global_device_ids=true, to_apply=%region_47.48.clone | all-reduce | flops 6144 | bytes 36864
  1179.3 44.5 %reduce-scatter.17.cloned.1.call-done = f32[128,1024]{1,0:T(8,128)} async-done(((f32[1024,1024]{1,0:T(8,128)}), f32[128,1024]{1,0:T(8,128)}) %reduce-scatter.17.cloned.1.call-update) | async-done | bytes 524304 | tf_op jit(solution)/shard_map/reduce_scatter | solution.py:309
  1225.5 90.4 %reduce-scatter.13.cloned.1.call-done = f32[128,1024]{0,1:T(8,128)} async-done(((f32[1024,1024]{0,1:T(8,128)}), f32[128,1024]{0,1:T(8,128)}) %reduce-scatter.13.cloned.1.call-update) | async-done | bytes 524304 | tf_op jit(solution)/shard_map/reduce_scatter | solution.py:307
  1317.7 89.9 %reduce-scatter.15.cloned.1.call-done = f32[128,1024]{0,1:T(8,128)} async-done(((f32[1024,1024]{0,1:T(8,128)}), f32[128,1024]{0,1:T(8,128)}) %reduce-scatter.15.cloned.1.call-update) | async-done | bytes 524304 | tf_op jit(solution)/shard_map/reduce_scatter | solution.py:308
  1409.4 89.8 %reduce-scatter.25.cloned.1.call-done = f32[128,1024]{1,0:T(8,128)} async-done(((f32[1024,1024]{1,0:T(8,128)}), f32[128,1024]{1,0:T(8,128)}) %reduce-scatter.25.cloned.1.call-update) | async-done | bytes 524304 | tf_op jit(solution)/shard_map/reduce_scatter | solution.py:313
  1501.0 90.0 %reduce-scatter.21.cloned.1.call-done = f32[128,1024]{0,1:T(8,128)} async-done(((f32[1024,1024]{0,1:T(8,128)}), f32[128,1024]{0,1:T(8,128)}) %reduce-scatter.21.cloned.1.call-update) | async-done | bytes 524304 | tf_op jit(solution)/shard_map/reduce_scatter | solution.py:311
  1592.7 90.4 %reduce-scatter.23.cloned.1.call-done = f32[128,1024]{0,1:T(8,128)} async-done(((f32[1024,1024]{0,1:T(8,128)}), f32[128,1024]{0,1:T(8,128)}) %reduce-scatter.23.cloned.1.call-update) | async-done | bytes 524304 | tf_op jit(solution)/shard_map/reduce_scatter | solution.py:312
  1684.9 284.5 %reduce-scatter.29.cloned.1.call-done = f32[512,1024]{1,0:T(8,128)} async-done(((f32[4096,1024]{1,0:T(8,128)}), f32[512,1024]{1,0:T(8,128)}) %reduce-scatter.29.cloned.1.call-update) | async-done | bytes 2097168 | tf_op jit(solution)/shard_map/reduce_scatter | solution.py:288
  1972.1 283.2 %reduce-scatter.27.cloned.1.call-done = f32[128,4096]{1,0:T(8,128)} async-done(((f32[1024,4096]{1,0:T(8,128)}), f32[128,4096]{1,0:T(8,128)}) %reduce-scatter.27.cloned.1.call-update) | async-done | bytes 2097168 | tf_op jit(solution)/shard_map/reduce_scatter | solution.py:287
  2281.2 64.6 %all-reduce.11.cloned.1.call-done = (bf16[128,1024]{0,1:T(8,128)(2,1)}, bf16[128,1024]{0,1:T(8,128)(2,1)}, bf16[128,1024]{0,1:T(8,128)(2,1)}, bf16[128,1024]{0,1...) async-done(((bf16[128,1024]{0,1:T(8,128)(2,1)}, ...) | async-done | bytes 4194320 | tf_op jit(solution)/shard_map/psum | solution.py:320
  (465 shorter events, 586.1 us)
Async XLA Ops:
  7.2 304.5 %copy-start = (bf16[256,1024]{1,0:T(8,128)(2,1)S(1)}, bf16[256,1024]{1,0:T(8,128)(2,1)}, u32[]{:S(2)}) copy-start(bf16[256,1024]{1,0:T(8,128)(2,1)} %param.29) | copy-start | bytes 1572868
  7.2 50.6 %copy-start.95 = (bf16[128]{0:T(256)(128)(2,1)S(1)}, bf16[128]{0:T(256)(128)(2,1)}, u32[]{:S(2)}) copy-start(bf16[128]{0:T(256)(128)(2,1)} %param.44) | copy-start | bytes 772
  7.2 69.3 %copy-start.96 = (bf16[128]{0:T(256)(128)(2,1)S(1)}, bf16[128]{0:T(256)(128)(2,1)}, u32[]{:S(2)}) copy-start(bf16[128]{0:T(256)(128)(2,1)} %param.45) | copy-start | bytes 772
  7.3 86.2 %copy-start.41 = (bf16[1024,1024]{1,0:T(8,128)(2,1)S(1)}, bf16[1024,1024]{1,0:T(8,128)(2,1)}, u32[]{:S(2)}) copy-start(bf16[1024,1024]{1,0:T(8,128)(2,1)} %param.31) | copy-start | bytes 6291460
  7.3 124.5 %all-gather.17.cloned.1.call-start = ((), (), s32[]{:S(2)}) async-start(), calls=%async_computation.10 | async-start | bytes 2359296 | tf_op jit(solution)/shard_map/all_gather | solution.py:142
  8.0 137.7 %all-gather.19.cloned.1.call-start = ((), (), s32[]{:S(2)}) async-start(), calls=%async_computation.11 | async-start | bytes 2359296 | tf_op jit(solution)/shard_map/all_gather | solution.py:143
  8.8 153.5 %all-gather.21.cloned.1.call-start = ((), (), s32[]{:S(2)}) async-start(), calls=%async_computation.12 | async-start | bytes 2359296 | tf_op jit(solution)/shard_map/all_gather | solution.py:144
  9.5 262.3 %all-gather.23.cloned.1.call-start = ((), (), s32[]{:S(2)}) async-start(), calls=%async_computation.13 | async-start | bytes 2359296 | tf_op jit(solution)/shard_map/all_gather | solution.py:145
  10.1 269.7 %all-gather.25.cloned.1.call-start = ((), (), s32[]{:S(2)}) async-start(), calls=%async_computation.14 | async-start | bytes 2359296 | tf_op jit(solution)/shard_map/all_gather | solution.py:146
  10.6 301.1 %all-gather.27.cloned.1.call-start = ((), (), s32[]{:S(2)}) async-start(), calls=%async_computation.15 | async-start | bytes 2359296 | tf_op jit(solution)/shard_map/all_gather | solution.py:147
  11.2 350.4 %all-gather.29.cloned.1.call-start = ((), (), s32[]{:S(2)}) async-start(), calls=%async_computation.16 | async-start | bytes 2359296 | tf_op jit(solution)/shard_map/all_gather | solution.py:148
  12.0 399.6 %all-gather.31.cloned.1.call-start = ((), (), s32[]{:S(2)}) async-start(), calls=%async_computation.17 | async-start | bytes 2359296 | tf_op jit(solution)/shard_map/all_gather | solution.py:149
  12.7 524.5 %all-gather.33.cloned.1.call-start = ((), (), s32[]{:S(2)}) async-start(), calls=%async_computation.18 | async-start | bytes 9437184 | tf_op jit(solution)/shard_map/all_gather | solution.py:156
  13.5 648.9 %all-gather.35.cloned.1.call-start = ((), (), s32[]{:S(2)}) async-start(), calls=%async_computation.19 | async-start | bytes 9437184 | tf_op jit(solution)/shard_map/all_gather | solution.py:157
  14.0 1161.6 %reduce-scatter.19.cloned.1.call-start = ((), (), s32[]{:S(2)}) async-start(), calls=%async_computation.24 | async-start | bytes 4718592 | tf_op jit(solution)/shard_map/reduce_scatter | solution.py:310
  14.2 81.8 %copy-start.97 = (bf16[128]{0:T(256)(128)(2,1)S(1)}, bf16[128]{0:T(256)(128)(2,1)}, u32[]{:S(2)}) copy-start(bf16[128]{0:T(256)(128)(2,1)} %param.46) | copy-start | bytes 772
  14.2 100.6 %copy-start.98 = (bf16[128]{0:T(256)(128)(2,1)S(1)}, bf16[128]{0:T(256)(128)(2,1)}, u32[]{:S(2)}) copy-start(bf16[128]{0:T(256)(128)(2,1)} %param.47) | copy-start | bytes 772
  277.3 134.3 %copy-start.66 = (f32[1024]{0:T(1024)}, f32[1024]{0:T(1024)S(1)}, u32[]{:S(2)}) copy-start(f32[1024]{0:T(1024)S(1)} %broadcast_multiply_fusion.8) | copy-start | bytes 12292
  279.8 131.8 %copy-start.76 = (f32[1024]{0:T(1024)}, f32[1024]{0:T(1024)S(1)}, u32[]{:S(2)}) copy-start(f32[1024]{0:T(1024)S(1)} %add_rsqrt_fusion.2) | copy-start | bytes 12292
  418.0 305.6 %copy-start.58 = (f32[1024]{0:T(1024)}, f32[1024]{0:T(1024)S(1)}, u32[]{:S(2)}) copy-start(f32[1024]{0:T(1024)S(1)} %broadcast_multiply_fusion.7) | copy-start | bytes 12292
  418.5 305.1 %copy-start.62 = (f32[1024]{0:T(1024)}, f32[1024]{0:T(1024)S(1)}, u32[]{:S(2)}) copy-start(f32[1024]{0:T(1024)S(1)} %add_rsqrt_fusion.1) | copy-start | bytes 12292
  793.5 384.0 %reduce-scatter.11.cloned.1.call-start = ((), (), s32[]{:S(2)}) async-start(), calls=%async_computation.20 | async-start | bytes 4718592 | tf_op jit(solution)/shard_map/reduce_scatter | solution.py:306
  1044.8 179.0 %reduce-scatter.17.cloned.1.call-start = ((), (), s32[]{:S(2)}) async-start(), calls=%async_computation.23 | async-start | bytes 4718592 | tf_op jit(solution)/shard_map/reduce_scatter | solution.py:309
  1052.0 263.9 %reduce-scatter.13.cloned.1.call-start = ((), (), s32[]{:S(2)}) async-start(), calls=%async_computation.21 | async-start | bytes 4718592 | tf_op jit(solution)/shard_map/reduce_scatter | solution.py:307
  1060.2 347.4 %reduce-scatter.15.cloned.1.call-start = ((), (), s32[]{:S(2)}) async-start(), calls=%async_computation.22 | async-start | bytes 4718592 | tf_op jit(solution)/shard_map/reduce_scatter | solution.py:308
  1068.5 430.7 %reduce-scatter.25.cloned.1.call-start = ((), (), s32[]{:S(2)}) async-start(), calls=%async_computation.27 | async-start | bytes 4718592 | tf_op jit(solution)/shard_map/reduce_scatter | solution.py:313
  1076.9 514.0 %reduce-scatter.21.cloned.1.call-start = ((), (), s32[]{:S(2)}) async-start(), calls=%async_computation.25 | async-start | bytes 4718592 | tf_op jit(solution)/shard_map/reduce_scatter | solution.py:311
  1080.9 602.2 %reduce-scatter.23.cloned.1.call-start = ((), (), s32[]{:S(2)}) async-start(), calls=%async_computation.26 | async-start | bytes 4718592 | tf_op jit(solution)/shard_map/reduce_scatter | solution.py:312
  1085.8 883.5 %reduce-scatter.29.cloned.1.call-start = ((), (), s32[]{:S(2)}) async-start(), calls=%async_computation.29 | async-start | bytes 18874368 | tf_op jit(solution)/shard_map/reduce_scatter | solution.py:288
  1104.8 1150.5 %reduce-scatter.27.cloned.1.call-start = ((), (), s32[]{:S(2)}) async-start(), calls=%async_computation.28 | async-start | bytes 18874368 | tf_op jit(solution)/shard_map/reduce_scatter | solution.py:287
  1122.2 1223.6 %all-reduce.11.cloned.1.call-start = ((), (), s32[]{:S(2)}) async-start(), calls=%async_computation.30 | async-start | bytes 8388608 | tf_op jit(solution)/shard_map/psum | solution.py:320
  1972.1 285.9 %copy-start.40 = (bf16[1024,16,64]{0,2,1:T(8,128)(2,1)S(1)}, bf16[1024,16,64]{0,2,1:T(8,128)(2,1)}, u32[]{:S(2)}) copy-start(bf16[1024,16,64]{0,2,1:T(8,128)(2,1)} %copy-done.39) | copy-start | bytes 6291460
  (108 other events, 748.8 us)
Sparse Core Ops, SparseCore 0:
  10.2 52.0 all-gather.16
  64.4 47.8 all-gather.18
  114.4 47.7 all-gather.20
  164.2 47.8 all-gather.22
  214.1 47.7 all-gather.24
  263.9 47.7 all-gather.26
  313.9 47.7 all-gather.28
  363.8 47.7 all-gather.30
  413.7 123.4 all-gather.32
  539.2 123.1 all-gather.34
  793.6 86.2 reduce-scatter.18
  1044.9 87.3 reduce-scatter.10
  1135.9 87.7 reduce-scatter.16
  1227.7 88.1 reduce-scatter.12
  1319.4 88.1 reduce-scatter.14
  1411.5 87.6 reduce-scatter.24
  1502.7 88.2 reduce-scatter.20
  1594.8 88.2 reduce-scatter.22
  1686.9 282.4 reduce-scatter.28
  1973.4 281.7 reduce-scatter.26
  2259.5 86.2 all-reduce.10
where the time goes:
time: 2380 us; the launch traced here: 2370 us
  waiting for transfers between devices  1430 us (60%)
  matrix products  491 us (21%)
  other arithmetic  150 us (6%)
  blocking collectives  149 us (6%)
  local copies, waits for them, and re-layouts  119 us (5%)
    reduce_scatter x1, waiting for transfers between devices, body(): lax.psum_scatter(grad_contract, 'shard', scatter_dimension=0, tiled=True)  284 us
    reduce_scatter x1, waiting for transfers between devices, body(): lax.psum_scatter(grad_expand, 'shard', scatter_dimension=0, tiled=True)  283 us
    dot_general x30, matrix products, matmul(): return jnp.dot(left, right, preferred_element_type=jnp.float32)  242 us
    all_gather x1, waiting for transfers between devices, body(): lax.all_gather(expand_weight, 'shard', axis=0, tiled=True)  117 us
    reduce_scatter x1, waiting for transfers between devices, body(): lax.psum_scatter(grad_cross_value, 'shard', scatter_dimension=0, tiled=True)  90.4 us
    reduce_scatter x1, waiting for transfers between devices, body(): lax.psum_scatter(grad_self_key, 'shard', scatter_dimension=0, tiled=True)  90.4 us
    reduce_scatter x1, waiting for transfers between devices, body(): lax.psum_scatter(grad_cross_key, 'shard', scatter_dimension=0, tiled=True)  90 us
    reduce_scatter x1, waiting for transfers between devices, body(): lax.psum_scatter(grad_self_value, 'shard', scatter_dimension=0, tiled=True)  89.9 us
  transfers between devices with their start and end apart: 21, of which 15 were waited for; matrix products, arithmetic and copies ran while one was open for 25% of the time, Pallas kernels for 0%

commit v1 on v0

v1 whole, which is shorter than its diff:
```python
import functools

import jax
import jax.numpy as jnp
from jax import lax
from jax.experimental import pallas as pl
from jax.experimental.pallas import tpu as pltpu
from jax.sharding import PartitionSpec as P

HD = 64
PIC = 256
EPS = 1e-05
NEGATIVE = -1e30
INV_ROOT_TWO = 0.7071067811865476
INV_ROOT_TWO_PI = 0.3989422804014327
MESH = pl.DeviceIdType.MESH
MIB = 1 << 20
HBM = pl.BlockSpec(memory_space=pltpu.HBM)
bf16 = jnp.bfloat16
f32 = jnp.float32


def dot(a, b, ca=1, cb=0):
    return lax.dot_general(a, b, (((ca,), (cb,)), ((), ())), preferred_element_type=f32)


def place(n):
    half = n // 2

    def shard_at(pos):
        pos = lax.rem(pos + 2 * n, n)
        back = pos // half
        return (1 - back) * 2 * pos + back * (2 * (n - 1 - pos) + 1)

    s = lax.axis_index("shard")
    odd = s % 2
    pos = (1 - odd) * (s // 2) + odd * (n - 1 - s // 2)
    return pos, shard_at


def greet(partners):
    barrier = pltpu.get_barrier_semaphore()
    for who in partners:
        pl.semaphore_signal(barrier, inc=1, device_id=who, device_id_type=MESH)
    pl.semaphore_wait(barrier, len(partners))


def send(src, dst, ssem, rsem, who):
    copy = pltpu.make_async_remote_copy(
        src_ref=src, dst_ref=dst, send_sem=ssem, recv_sem=rsem, device_id=who, device_id_type=MESH
    )
    copy.start()
    return copy


def load(src, dst, sem):
    copy = pltpu.make_async_copy(src, dst, sem)
    copy.start()
    return copy


def gather_kernel(n, ne, ns, rows, stack, vec, full, vecs, local, rs, rr, cs, cr, xs, xr, fs, fr, vs, vr):
    rep, shard = lax.axis_index("rep"), lax.axis_index("shard")
    x, c = rep // 2, rep % 2
    pos, shard_at = place(n)
    ways = (((rep, shard_at(pos + 1)), 1), ((rep, shard_at(pos - 1)), -1))
    sibling, across = (x * 2 + 1 - c, shard), ((1 - x) * 2 + c, shard)
    width = stack.shape[-1] // 4
    ring = pl.ds(x * ne, ne + ns)
    mine = pl.ds(x * (ne + ns), ne)
    theirs = pl.ds((1 - x) * (ne + ns), ne)

    def spot(units, owner, d):
        cols = pl.multiple_of(c * 2 * width + d * width, width)
        return full.at[units, pl.ds(pl.multiple_of(owner * rows, rows), rows), pl.ds(cols, width)]

    own = load(stack, full.at[:, pl.ds(pl.multiple_of(shard * rows, rows), rows), :], local.at[0])
    own_vec = load(vec, vecs.at[shard], local.at[1])
    greet((ways[0][0], ways[1][0], sibling, across))
    own.wait()
    own_vec.wait()
    on_ring, crossing, beside, forwarded, vec_sent = {}, {}, {}, {}, {}

    def forward(k):
        for d, (_, sign) in enumerate(ways):
            here = spot(theirs, shard_at(pos - sign * k), d)
            crossing[d, k].wait_recv()
            forwarded[d, k] = send(here, here, fs.at[d, k - 1], fr.at[d, k - 1], sibling)

    for k in range(n):
        for d, (who, sign) in enumerate(ways):
            owner = shard_at(pos - sign * k)
            here = spot(ring, owner, d)
            if k:
                on_ring[d, k - 1].wait_recv()
            if k < n - 1:
                on_ring[d, k] = send(here, here, rs.at[d, k], rr.at[d, k], who)
            if k:
                part = spot(mine, owner, d)
                crossing[d, k] = send(part, part, xs.at[d, k - 1], xr.at[d, k - 1], across)
                beside[d, k] = send(here, here, cs.at[d, k - 1], cr.at[d, k - 1], sibling)
        if k:
            vec_sent[k - 1].wait_recv()
        if k < n - 1:
            owner = shard_at(pos - k)
            vec_sent[k] = send(vecs.at[owner], vecs.at[owner], vs.at[k], vr.at[k], ways[0][0])
        if k >= 2:
            forward(k - 1)
    forward(n - 1)
    for copy in beside.values():
        copy.wait_recv()
    for copy in forwarded.values():
        copy.wait_recv()
    for group in (on_ring, crossing, beside, forwarded, vec_sent):
        for copy in group.values():
            copy.wait_send()


def gather(stack, vec, n, ne, ns):
    units, rows, width = stack.shape
    hops = pltpu.SemaphoreType.DMA((2, n - 1))
    return pl.pallas_call(
        functools.partial(gather_kernel, n, ne, ns, rows),
        out_shape=(
            jax.ShapeDtypeStruct((units, n * rows, width), stack.dtype),
            jax.ShapeDtypeStruct((n,) + vec.shape, vec.dtype),
        ),
        in_specs=[HBM, HBM],
        out_specs=[HBM, HBM],
        scratch_shapes=[pltpu.SemaphoreType.DMA((2,))]
        + [hops] * 8
        + [pltpu.SemaphoreType.DMA((n - 1,))] * 2,
        compiler_params=pltpu.CompilerParams(collective_id=0, has_side_effects=True, vmem_limit_bytes=16 * MIB),
        name="gather_weights",
    )(stack, vec)


def scatter_kernel(
    n, ne, ns, rows, grads, out, near, beside, cross, ring, swap_s, swap_e,
    local, cs, cr, xs, xr, rs, rr, ss, sr, os, orr, done,
):
    rep, shard = lax.axis_index("rep"), lax.axis_index("shard")
    x, c = rep // 2, rep % 2
    pos, shard_at = place(n)
    ways = (((rep, shard_at(pos + 1)), 1), ((rep, shard_at(pos - 1)), -1))
    sibling, across = (x * 2 + 1 - c, shard), ((1 - x) * 2 + c, shard)
    units = grads.shape[0]
    width = grads.shape[-1] // 4
    on_ring = ne + ns
    owners = {(d, k): shard_at(pos - sign * (1 + k)) for d, (_, sign) in enumerate(ways) for k in range(n)}

    def rows_of(owner):
        return pl.ds(pl.multiple_of(owner * rows, rows), rows)

    def cols(d):
        return pl.ds(d * width, width)

    loads, sides, crossing, hops = {}, {}, {}, {}
    for k in range(n):
        for d in range(2):
            at = rows_of(owners[d, k])
            half = pl.multiple_of(c * 2 * width + d * width, width)
            loads[d, k] = load(grads.at[:, at, pl.ds(half, width)], near.at[:, at, cols(d)], local.at[d, k])
    greet((ways[0][0], ways[1][0], sibling, across))
    for k in range(n):
        for d in range(2):
            at = rows_of(owners[d, k])
            half = pl.multiple_of((1 - c) * 2 * width + d * width, width)
            sides[d, k] = send(
                grads.at[:, at, pl.ds(half, width)], beside.at[:, at, cols(d)], cs.at[d, k], cr.at[d, k], sibling
            )

    def pair(k):
        for d in range(2):
            at = rows_of(owners[d, k])
            loads[d, k].wait()
            sides[d, k].wait_recv()

            def add(u, _):
                near[u, at, cols(d)] = (
                    near[u, at, cols(d)].astype(f32) + beside[u, at, cols(d)].astype(f32)
                ).astype(bf16)
                return 0

            lax.fori_loop(0, units, add, 0)
            theirs = pl.ds((1 - x) * on_ring, ne)
            crossing[d, k] = send(
                near.at[theirs, at, cols(d)], cross.at[:, at, cols(d)], xs.at[d, k], xr.at[d, k], across
            )

    def hop(k):
        for d, (who, _) in enumerate(ways):
            at = rows_of(owners[d, k])
            if k:
                hops[d, k - 1].wait_recv()

            def add_shared(i, _):
                u = ne + i
                value = near[u, at, cols(d)].astype(f32) + ring[d, k - 1, (1 - x) * ne + i].astype(f32)
                near[u, at, cols(d)] = value.astype(bf16)
                return 0

            if k:
                lax.fori_loop(0, ns, add_shared, 0)
            crossing[d, k].wait_recv()

            def add_mine(i, _):
                u = x * on_ring + i
                value = near[u, at, cols(d)].astype(f32) + cross[i, at, cols(d)].astype(f32)
                if k:
                    value = value + ring[d, k - 1, x * ns + i].astype(f32)
                near[u, at, cols(d)] = value.astype(bf16)
                return 0

            lax.fori_loop(0, ne, add_mine, 0)
            if k < n - 1:
                hops[d, k] = send(near.at[pl.ds(x * ne, on_ring), at, cols(d)], ring.at[d, k], rs.at[d, k], rr.at[d, k], who)

    pair(0)
    pair(1)
    for k in range(n):
        if k + 2 < n:
            pair(k + 2)
        hop(k)
    at = rows_of(shard)
    shared = pl.ds(ne, ns)
    mine = pl.ds(x * on_ring, ne)
    theirs = pl.ds((1 - x) * on_ring, ne)
    half = pl.ds(pl.multiple_of(c * 2 * width, 2 * width), 2 * width)
    swap = send(near.at[shared, at, :], swap_s, ss.at[0], sr.at[0], across)
    give = send(near.at[mine, at, :], swap_e, ss.at[1], sr.at[1], across)
    final = [send(near.at[mine, at, :], out.at[mine, :, half], os.at[0], orr.at[0], sibling)]
    keep = [load(near.at[mine, at, :], out.at[mine, :, half], done.at[0])]
    swap.wait_recv()

    def join(i, _):
        swap_s[i] = (swap_s[i].astype(f32) + near[ne + i, at, :].astype(f32)).astype(bf16)
        return 0

    lax.fori_loop(0, ns, join, 0)
    final.append(send(swap_s, out.at[shared, :, half], os.at[1], orr.at[1], sibling))
    keep.append(load(swap_s, out.at[shared, :, half], done.at[1]))
    give.wait_recv()
    final.append(send(swap_e, out.at[theirs, :, half], os.at[2], orr.at[2], sibling))
    keep.append(load(swap_e, out.at[theirs, :, half], done.at[2]))
    for copy in keep:
        copy.wait()
    for copy in final:
        copy.wait_recv()
    for copy in [*sides.values(), *crossing.values(), *hops.values(), swap, give, *final]:
        copy.wait_send()


def scatter(grads, n, ne, ns, collective_id):
    units, total, width = grads.shape
    rows = total // n
    dma = pltpu.SemaphoreType.DMA
    return pl.pallas_call(
        functools.partial(scatter_kernel, n, ne, ns, rows),
        out_shape=jax.ShapeDtypeStruct((units, rows, width), bf16),
        in_specs=[HBM],
        out_specs=HBM,
        scratch_shapes=[
            pltpu.VMEM((units, total, width // 2), bf16),
            pltpu.VMEM((units, total, width // 2), bf16),
            pltpu.VMEM((ne, total, width // 2), bf16),
            pltpu.VMEM((2, n - 1, ne + ns, rows, width // 4), bf16),
            pltpu.VMEM((ns, rows, width // 2), bf16),
            pltpu.VMEM((ne, rows, width // 2), bf16),
            dma((2, n)), dma((2, n)), dma((2, n)), dma((2, n)), dma((2, n)),
            dma((2, n - 1)), dma((2, n - 1)), dma((2,)), dma((2,)), dma((3,)), dma((3,)), dma((3,)),
        ],
        compiler_params=pltpu.CompilerParams(
            collective_id=collective_id, has_side_effects=True, vmem_limit_bytes=56 * MIB
        ),
        name="scatter_grads",
    )(grads)


def first_lanes(shape):
    return lax.broadcasted_iota(jnp.int32, shape, len(shape) - 1) < HD


def region_bias(starts_ref, region, size, transposed):
    first = region * size
    one = first + lax.broadcasted_iota(jnp.int32, (size, size), 0)
    two = first + lax.broadcasted_iota(jnp.int32, (size, size), 1)
    q_at, k_at = (two, one) if transposed else (one, two)
    start = starts_ref[0, region]
    q_in = (q_at >= start) & (q_at < start + PIC)
    k_in = (k_at >= start) & (k_at < start + PIC)
    return jnp.where((k_at <= q_at) | (q_in & k_in), 0.0, NEGATIVE)


def attend_forward_kernel(regions, starts_ref, q_ref, k_ref, v_ref, o_ref, lse_ref, bias_ref):
    rows = q_ref.shape[0]
    size = rows // regions

    if starts_ref is not None:
        @pl.when(pl.program_id(0) == 0)
        def _():
            for r in range(regions):
                bias_ref[r] = region_bias(starts_ref, r, size, False)

    low = first_lanes((1, 2 * HD))
    outs, lses = [[], []], [[], []]
    for h in range(2):
        pick = low if h == 0 else ~low
        keys = jnp.where(pick, k_ref[...], jnp.zeros((), bf16))
        for r in range(regions):
            span = slice(r * size, (r + 1) * size)
            q = q_ref[span, :]
            scores = []
            if starts_ref is None:
                scores.append((dot(q, keys, 1, 1), v_ref[...]))
            else:
                if r:
                    scores.append((dot(q, keys[: r * size], 1, 1), v_ref[: r * size, :]))
                scores.append((dot(q, keys[span], 1, 1) + bias_ref[r], v_ref[span, :]))
            top = functools.reduce(jnp.maximum, [jnp.max(s, -1, keepdims=True) for s, _ in scores])
            total, mixed = 0.0, 0.0
            for s, v in scores:
                e = jnp.exp(s - top)
                total = total + jnp.sum(e, -1, keepdims=True)
                mixed = mixed + dot(e.astype(bf16), v)
            outs[h].append(mixed / total)
            lses[h].append(top + jnp.log(total))
    for r in range(regions):
        span = slice(r * size, (r + 1) * size)
        o_ref[span, :] = jnp.where(low, outs[0][r], outs[1][r]).astype(bf16)
        turned = jnp.where(low, lses[0][r], lses[1][r]).T
        lse_ref[0, 0:1, span] = turned[0:1]
        lse_ref[0, 1:2, span] = turned[HD : HD + 1]


def attend_forward(q, k, v, starts):
    rows, width = q.shape
    regions = 1 if starts is None else starts.shape[1]
    pairs = width // (2 * HD)
    tall = lambda a: pl.BlockSpec((a.shape[0], 2 * HD), lambda i: (0, i))
    specs = [tall(q), tall(k), tall(v)]
    args = [q, k, v]
    if starts is None:
        kernel = lambda *refs: attend_forward_kernel(2, None, *refs, None)
        scratch = []
    else:
        kernel = functools.partial(attend_forward_kernel, regions)
        specs = [pl.BlockSpec(memory_space=pltpu.SMEM)] + specs
        args = [starts] + args
        scratch = [pltpu.VMEM((regions, rows // regions, rows // regions), f32)]
    return pl.pallas_call(
        kernel,
        grid=(pairs,),
        out_shape=(jax.ShapeDtypeStruct((rows, width), bf16), jax.ShapeDtypeStruct((pairs, 8, rows), f32)),
        in_specs=specs,
        out_specs=[tall(q), pl.BlockSpec((1, 8, rows), lambda i: (i, 0, 0))],
        scratch_shapes=scratch,
        compiler_params=pltpu.CompilerParams(vmem_limit_bytes=48 * MIB),
        name="self_forward" if starts is not None else "cross_forward",
    )(*args)


def attend_backward_kernel(
    regions, starts_ref, q_ref, k_ref, v_ref, g_ref, o_ref, lse_ref, gq_ref, gk_ref, gv_ref, bias_ref
):
    rows = q_ref.shape[0]
    size = rows // regions

    if starts_ref is not None:
        @pl.when(pl.program_id(0) == 0)
        def _():
            for r in range(regions):
                bias_ref[r] = region_bias(starts_ref, r, size, True)

    low = first_lanes((1, 2 * HD))
    product = g_ref[...].astype(f32) * o_ref[...].astype(f32)
    chooser = lax.broadcasted_iota(jnp.int32, (8, 2 * HD), 0)
    chooser = ((chooser == 0) & first_lanes((8, 2 * HD))) | ((chooser == 1) & ~first_lanes((8, 2 * HD)))
    chooser = chooser.astype(f32).astype(bf16)
    upper = product.astype(bf16)
    lower = (product - upper.astype(f32)).astype(bf16)
    deltas = dot(chooser, upper, 1, 1) + dot(chooser, lower, 1, 1)
    gq, gk, gv = {}, {}, {}
    key_spans = [slice(0, k_ref.shape[0])]
    if starts_ref is not None:
        key_spans = [slice(r * size, (r + 1) * size) for r in range(regions)]
    for h in range(2):
        pick = low if h == 0 else ~low
        zero = jnp.zeros((), bf16)
        keys = jnp.where(pick, k_ref[...], zero)
        values = jnp.where(pick, v_ref[...], zero)
        for r in range(regions):
            span = slice(r * size, (r + 1) * size)
            q, g = q_ref[span, :], g_ref[span, :]
            lse = lse_ref[0, h : h + 1, span]
            delta = deltas[h : h + 1, span]
            for j, keyed in enumerate(key_spans):
                if starts_ref is not None and j > r:
                    continue
                scores = dot(keys[keyed], q, 1, 1)
                if starts_ref is not None and j == r:
                    scores = scores + bias_ref[r]
                probs = jnp.exp(scores - lse)
                grad_probs = dot(values[keyed], g, 1, 1)
                grad_scores = (probs * (grad_probs - delta)).astype(bf16)
                gv[h, j] = gv.get((h, j), 0.0) + dot(probs.astype(bf16), g)
                gk[h, j] = gk.get((h, j), 0.0) + dot(grad_scores, q)
                gq[h, r] = gq.get((h, r), 0.0) + dot(grad_scores, k_ref[keyed, :], 0, 0)
    for r in range(regions):
        span = slice(r * size, (r + 1) * size)
        gq_ref[span, :] = jnp.where(low, gq[0, r], gq[1, r]).astype(bf16)
    for j, keyed in enumerate(key_spans):
        gk_ref[keyed, :] = jnp.where(low, gk[0, j], gk[1, j]).astype(bf16)
        gv_ref[keyed, :] = jnp.where(low, gv[0, j], gv[1, j]).astype(bf16)


def attend_backward(q, k, v, g, o, lse, starts):
    rows, width = q.shape
    regions = 1 if starts is None else starts.shape[1]
    pairs = width // (2 * HD)
    tall = lambda a: pl.BlockSpec((a.shape[0], 2 * HD), lambda i: (0, i))
    specs = [tall(a) for a in (q, k, v, g, o)] + [pl.BlockSpec((1, 8, rows), lambda i: (i, 0, 0))]
    args = [q, k, v, g, o, lse]
    if starts is None:
        kernel = lambda *refs: attend_backward_kernel(2, None, *refs, None)
        scratch = []
    else:
        kernel = functools.partial(attend_backward_kernel, regions)
        specs = [pl.BlockSpec(memory_space=pltpu.SMEM)] + specs
        args = [starts] + args
        scratch = [pltpu.VMEM((regions, rows // regions, rows // regions), f32)]
    like = lambda a: jax.ShapeDtypeStruct(a.shape, bf16)
    return pl.pallas_call(
        kernel,
        grid=(pairs,),
        out_shape=(like(q), like(k), like(v)),
        in_specs=specs,
        out_specs=[tall(q), tall(k), tall(v)],
        scratch_shapes=scratch,
        compiler_params=pltpu.CompilerParams(vmem_limit_bytes=48 * MIB),
        name="self_backward" if starts is not None else "cross_backward",
    )(*args)


def norm_forward(resid, gain, shift):
    mean = jnp.mean(resid, -1, keepdims=True)
    centred = resid - mean
    variance = jnp.mean(centred * centred, -1, keepdims=True)
    inverse = lax.rsqrt(variance + EPS)
    normed = centred * inverse
    return (normed * gain + shift, normed, inverse)


def norm_backward(grad_out, normed, inverse, gain):
    grad_gain = jnp.sum(grad_out * normed, 0)
    grad_shift = jnp.sum(grad_out, 0)
    grad_normed = grad_out * gain
    centre_term = jnp.mean(grad_normed, -1, keepdims=True)
    slope_term = jnp.mean(grad_normed * normed, -1, keepdims=True)
    return (inverse * (grad_normed - centre_term - normed * slope_term), grad_gain, grad_shift)


def body(n, states, encoded, starts, cotangent, *weights):
    matrices, vectors = weights[:10], weights[10:]
    expand, contract = matrices[8], matrices[9]
    rows, width = matrices[0].shape
    blocks = contract.shape[0] // rows
    scale = HD ** (-0.5)
    small = n <= 16
    stack = jnp.concatenate(
        [
            jnp.stack(matrices[:8]),
            expand.reshape(rows, n, blocks, rows).transpose(2, 0, 1, 3).reshape(blocks, rows, width),
            contract.reshape(blocks, rows, width),
        ]
    )
    vec = jnp.zeros((16, max(rows, 128)), bf16).at[: len(vectors), :rows].set(jnp.stack(vectors))
    if small:
        full, vecs = gather(stack, vec, n, 5, 6)
    else:
        full = lax.all_gather(stack, "shard", axis=1, tiled=True)
        vecs = lax.all_gather(vec, "shard", axis=0)
    vecs = vecs[:, : len(vectors), :rows].transpose(1, 0, 2).reshape(len(vectors), width).astype(f32)
    w_sq, w_sk, w_sv, w_so, w_cq, w_ck, w_cv, w_co = [full[i] for i in range(8)]
    gain_one, shift_one, gain_two, shift_two, gain_three, shift_three = vecs

    wide = states.astype(f32)
    q_self = (dot(states, w_sq) * scale).astype(bf16)
    k_self = dot(states, w_sk).astype(bf16)
    v_self = dot(states, w_sv).astype(bf16)
    k_cross = dot(encoded, w_ck).astype(bf16)
    v_cross = dot(encoded, w_cv).astype(bf16)
    mixed_self, lse_self = attend_forward(q_self, k_self, v_self, starts)
    hidden_one, normed_one, inverse_one = norm_forward(wide + dot(mixed_self, w_so), gain_one, shift_one)
    one_low = hidden_one.astype(bf16)
    q_cross = (dot(one_low, w_cq) * scale).astype(bf16)
    mixed_cross, lse_cross = attend_forward(q_cross, k_cross, v_cross, None)
    hidden_two, normed_two, inverse_two = norm_forward(hidden_one + dot(mixed_cross, w_co), gain_two, shift_two)
    two_low = hidden_two.astype(bf16)
    active, slopes = [], []
    resid_three = hidden_two
    for j in range(blocks):
        pre = dot(two_low, full[8 + j])
        phi = 0.5 * (1.0 + lax.erf(pre * INV_ROOT_TWO))
        active.append((pre * phi).astype(bf16))
        slopes.append((phi + pre * jnp.exp(-0.5 * pre * pre) * INV_ROOT_TWO_PI).astype(bf16))
        resid_three = resid_three + dot(active[j], full[8 + blocks + j])
    final, normed_three, inverse_three = norm_forward(resid_three, gain_three, shift_three)

    grad_three, g_gain_three, g_shift_three = norm_backward(cotangent.astype(f32), normed_three, inverse_three, gain_three)
    branch_three = grad_three.astype(bf16)
    grad_two = grad_three
    g_expand, g_contract = [], []
    for j in range(blocks):
        g_contract.append(dot(active[j], branch_three, 0, 0).astype(bf16))
        g_pre = (dot(branch_three, full[8 + blocks + j], 1, 1) * slopes[j]).astype(bf16)
        g_expand.append(dot(two_low, g_pre, 0, 0).astype(bf16))
        grad_two = grad_two + dot(g_pre, full[8 + j], 1, 1)
    grad_resid_two, g_gain_two, g_shift_two = norm_backward(grad_two, normed_two, inverse_two, gain_two)
    branch_two = grad_resid_two.astype(bf16)
    g_cross_out = dot(mixed_cross, branch_two, 0, 0)
    grad_mixed = dot(branch_two, w_co, 1, 1).astype(bf16)
    g_q, g_k, g_v = attend_backward(q_cross, k_cross, v_cross, grad_mixed, mixed_cross, lse_cross, None)
    g_q = g_q * scale
    g_cross_query = dot(one_low, g_q, 0, 0)
    g_cross_key = dot(encoded, g_k, 0, 0)
    g_cross_value = dot(encoded, g_v, 0, 0)
    grad_encoded = dot(g_k, w_ck, 1, 1) + dot(g_v, w_cv, 1, 1)
    grad_one = grad_resid_two + dot(g_q, w_cq, 1, 1)
    grad_resid_one, g_gain_one, g_shift_one = norm_backward(grad_one, normed_one, inverse_one, gain_one)
    branch_one = grad_resid_one.astype(bf16)
    g_self_out = dot(mixed_self, branch_one, 0, 0)
    grad_mixed = dot(branch_one, w_so, 1, 1).astype(bf16)
    g_q, g_k, g_v = attend_backward(q_self, k_self, v_self, grad_mixed, mixed_self, lse_self, starts)
    g_q = g_q * scale
    g_self_query = dot(states, g_q, 0, 0)
    g_self_key = dot(states, g_k, 0, 0)
    g_self_value = dot(states, g_v, 0, 0)
    grad_states = grad_resid_one + dot(g_q, w_sq, 1, 1) + dot(g_k, w_sk, 1, 1) + dot(g_v, w_sv, 1, 1)

    grads_ff = jnp.stack(g_expand + g_contract)
    grads_at = jnp.stack(
        [
            g.astype(bf16)
            for g in (
                g_self_query, g_self_key, g_self_value, g_self_out,
                g_cross_query, g_cross_key, g_cross_value, g_cross_out,
            )
        ]
    )
    grads_vec = jnp.stack([g_gain_one, g_shift_one, g_gain_two, g_shift_two, g_gain_three, g_shift_three])
    if small:
        own_ff = scatter(grads_ff, n, 2, 4, 1)
        own_at = scatter(grads_at, n, 2, 4, 2)
    else:
        total = lambda g: lax.psum(lax.psum_scatter(g, "shard", scatter_dimension=1, tiled=True), "rep")
        own_ff, own_at = total(grads_ff), total(grads_at)
    grads_vec = lax.psum(grads_vec, ("rep", "shard"))
    own_vec = lax.dynamic_slice_in_dim(grads_vec, lax.axis_index("shard") * rows, rows, 1)
    own_at = own_at.astype(f32)
    own_expand = own_ff[:blocks].reshape(blocks, rows, n, rows).transpose(1, 2, 0, 3).reshape(rows, blocks * width)
    own_contract = own_ff[blocks:].reshape(blocks * rows, width)
    return (
        final.astype(bf16),
        grad_states,
        grad_encoded,
        *[own_at[i] for i in range(8)],
        own_expand.astype(f32),
        own_contract.astype(f32),
        *[own_vec[i] for i in range(6)],
    )


def solution(mesh):
    many, few = P(("rep", "shard"), None), P("shard", None)
    return jax.shard_map(
        functools.partial(body, mesh.shape["shard"]),
        mesh=mesh,
        in_specs=(many,) * 4 + (few,) * 10 + (P("shard"),) * 6,
        out_specs=(many,) * 3 + (few,) * 10 + (P("shard"),) * 6,
        check_vma=False,
    )
```

time: 2380 us -> 768 us (0.32)
  waiting for transfers between devices: 1430 us -> 0 us
  Pallas kernels: 0 us -> 412 us
  matrix products: 491 us -> 227 us
  other arithmetic: 150 us -> 17.9 us
  blocking collectives: 149 us -> 39.5 us
  local copies, waits for them, and re-layouts: 119 us -> 60.6 us
    reduce_scatter x10 -> x0, waiting for transfers between devices: 1060 us -> none  [the longest x1 284 us: body(): lax.psum_scatter(grad_contract, 'shard', scatter_dimension=0, tiled=True)]
    pallas_call x0 -> x7, Pallas kernels: none -> 412 us  [the longest x2 181 us: scatter(): pl.pallas_call(functools.partial(scatter_kernel, n, ne, ns, rows), out_sh...]
    all_gather x10 -> x0, waiting for transfers between devices: 296 us -> none  [the longest x1 117 us: body(): lax.all_gather(expand_weight, 'shard', axis=0, tiled=True)]
    dot_general x62 -> x48, matrix products: 491 us -> 227 us  [dot(): lax.dot_general(a, b, (((ca,), (cb,)), ((), ())), preferred_element_type=...]
    all_gather x6 -> x0, blocking collectives: 107 us -> none  [the longest x1 22.2 us: body(): lax.all_gather(self_gain, 'shard', axis=0, tiled=True)]
    convert_element_type x37 -> x5, other arithmetic: 102 us -> 8.64 us  [the longest x1 3.15 us: body(): branch_three = grad_three.astype(bf16)]
    psum x1 -> x0, waiting for transfers between devices: 64.6 us -> none  [body(): lax.psum(part_sq.astype(jnp.bfloat16), 'rep').astype(jnp.float32)]
    unnamed x1 -> x0, blocking collectives: 36.1 us -> none
  transfers between devices with their start and end apart: 21 -> 0, of which waited for: 15 -> 0; matrix products, arithmetic and copies ran while one was open for 25% -> 0% of each run, Pallas kernels for 0% -> 0%
where the time goes in v1:
time: 768 us; the launch traced here: 759 us
  Pallas kernels  412 us (54%)
  matrix products  227 us (30%)
  local copies, waits for them, and re-layouts  60.6 us (8%)
  blocking collectives  39.5 us (5%)
  other arithmetic  17.9 us (2%)
    dot_general x48, matrix products, dot(): lax.dot_general(a, b, (((ca,), (cb,)), ((), ())), preferred_element_type=...  227 us
    pallas_call x2, Pallas kernels, scatter(): pl.pallas_call(functools.partial(scatter_kernel, n, ne, ns, rows), out_sh...  181 us
    pallas_call x1, Pallas kernels, gather(): pl.pallas_call(functools.partial(gather_kernel, n, ne, ns, rows), out_sha...  132 us
    pallas_call x2, Pallas kernels, attend_backward(): pl.pallas_call(kernel, grid=(pairs,), out_shape=(like(q), like(k), like(v...  63 us
    unnamed x166, local copies, waits for them, and re-layouts  47.7 us
    psum x1, blocking collectives, body(): grads_vec = lax.psum(grads_vec, ('rep', 'shard'))  39.5 us
    pallas_call x2, Pallas kernels, attend_forward(): pl.pallas_call(kernel, grid=(pairs,), out_shape=(jax.ShapeDtypeStruct((ro...  35.9 us

profile of v1, /device:TPU:0, one launch (start us, length us, event | category | flops | bytes accessed | tf_op | source)
XLA Modules:
  0.0 758.7 jit_solution(804826425893286400)
XLA Ops:
  16.6 132.0 %gather_weights.1 = (bf16[16,1024,1024]{2,1,0:T(8,128)(2,1)S(1)}, bf16[8,16,128]{2,1,0:T(8,128)(2,1)S(1)}) custom-call(bf16[16,128,1024]{2,1,0:T(8,128)(2,1)} %constant_dynamic-update-slice_fusion.stack, bf16[16,128]{1,0:T(8,128)(2,1)S(1)} %scatter.4.vec), custom_call_target="tpu_custom_call" | custom-call | tf_op jit(solution)/shard_map/gather_weights/pallas_call | solution.py:122
  148.6 11.1 %copy-done.11 = bf16[16,1024,1024]{2,1,0:T(8,128)(2,1)} copy-done((bf16[16,1024,1024]{2,1,0:T(8,128)(2,1)}, bf16[16,1024,1024]{2,1,0:T(8,128)(2,1)S(1)}, u32[]{:S(2)}) %copy-start.11) | copy-done | bytes 33554456
  163.6 6.0 convert_bitcast_fusion.1.k_ref
  169.6 5.3 convert_bitcast_fusion.v_ref
  174.9 25.4 %self_forward.1 = (bf16[1024,1024]{1,0:T(8,128)(2,1)S(1)}, f32[8,8,1024]{2,1,0:T(8,128)S(1)}) custom-call(s32[1,2]{1,0:T(1,128)S(1)} %copy-done.14, bf16[1024,1024]{1,0:T(8,128)(2,1)S(1)} %fusion.139.q_ref, bf16[1024,1024]{1,0:T(8,128)(2,1)} %convert_bitcast_fusion.1.k_ref, bf16[1024,1024]{1,0:T(8,128)(2,1)} %convert_bitcast_fusion.v_ref), custom_call_target="tpu_custom_call" | custom-call | tf_op jit(solution)/shard_map/self_forward/pallas_call | solution.py:351
  205.1 4.8 fusion.184
  212.0 5.7 multiply_convert_fusion.8
  226.2 10.6 %cross_forward.1 = (bf16[1024,1024]{1,0:T(8,128)(2,1)S(1)}, f32[8,8,1024]{2,1,0:T(8,128)S(1)}) custom-call(bf16[1024,1024]{1,0:T(8,128)(2,1)S(1)} %copy.47.refs_0_, bf16[256,1024]{1,0:T(8,128)(2,1)S(1)} %fusion.162.refs_1_, bf16[256,1024]{1,0:T(8,128)(2,1)S(1)} %fusion.159.refs_2_), custom_call_target="tpu_custom_call" | custom-call | tf_op jit(solution)/shard_map/cross_forward/pallas_call | solution.py:351
  236.8 5.4 fusion.185
  243.4 5.0 fusion.35
  248.4 5.6 fusion.31
  258.1 5.6 fusion.38
  270.0 5.6 fusion.45
  279.7 8.3 %fusion.186 = (f32[1024]{0:T(1024)S(1)}, f32[1024,1024]{0,1:T(8,128)S(1)}) fusion(f32[1024,1024]{0,1:T(8,128)S(1)} %fusion.31, f32[1024,1024]{0,1:T(8,128)S(1)} %fusion.38, f32[1024,1024]{0,1:T(8,128)} %fusion.45, bf16[16,1024,1024]{2,1,0:T(8,128)(2,1)} %copy-done.11, f32[1024,1024]{1,0:T(8,128)S(1)} %fusion.56, f32[1024]{0:T(1024)S(1)} %bitcast.321, ...), kind=kOutput, calls=%fused_computation.252 | convolution fusion | flops 2162162688 | bytes 27283456 | tf_op jit(solution)/shard_map/dot_general | solution.py:24
  301.0 6.4 multiply_convert_fusion
  312.2 4.9 multiply_convert_fusion.1
  317.2 6.8 fusion.40
  324.0 4.9 multiply_convert_fusion.2
  328.9 6.7 fusion.47
  335.7 6.7 multiply_convert_fusion.3
  342.4 9.5 %multiply_reduce_fusion = (f32[1024]{0:T(1024)S(1)}, f32[1024]{0:T(1024)S(1)}, f32[1024]{0:T(1024)S(1)}, f32[1024]{0:T(1024)S(1)}, f32[1024,1024]{0,1:T(8,128)S(1)}) fusion(f32[1024,1024]{0,1:T(8,128)S(1)} %copy-done.21, f32[1024]{0:T(1024)S(1)} %add_rsqrt_fusion.1, f32[1024]{0:T(1024)S(1)} %broadcast_multiply_fusion.7, f32[1024]{0:T(1024)S(1)} %bitcast.307, ...), kind=kOutput, calls=%fused_computation.34 | convolution fusion | flops 2169499648 | bytes 31506432 | tf_op jit(solution)/shard_map/dot_general | solution.py:24
  355.0 5.4 fusion.100.refs_3_
  360.5 19.2 %cross_backward.1 = (bf16[1024,1024]{1,0:T(8,128)(2,1)S(1)}, bf16[256,1024]{1,0:T(8,128)(2,1)S(1)}, bf16[256,1024]{1,0:T(8,128)(2,1)S(1)}) custom-call(bf16[1024,1024]{1,0:T(8,128)(2,1)} %copy-done.1, bf16[256,1024]{1,0:T(8,128)(2,1)S(1)} %copy-done.8, bf16[256,1024]{1,0:T(8,128)(2,1)S(1)} %copy-done.10, bf16[1024,1024]{1,0:T(8,128)(2,1)} %fusion.100.refs_3_, ...), custom_call_target="tpu_custom_call" | custom-call | tf_op jit(solution)/shard_map/cross_backward/pallas_call | solution.py:433
  379.7 7.2 multiply_reduce_fusion.1
  388.0 6.8 fusion.97.g_ref
  394.8 43.8 %self_backward.1 = (bf16[1024,1024]{1,0:T(8,128)(2,1)S(1)}, bf16[1024,1024]{1,0:T(8,128)(2,1)S(1)}, bf16[1024,1024]{1,0:T(8,128)(2,1)}) custom-call(s32[1,2]{1,0:T(1,128)S(1)} %copy-done.15, bf16[1024,1024]{1,0:T(8,128)(2,1)} %copy-done.2, bf16[1024,1024]{1,0:T(8,128)(2,1)} %convert_bitcast_fusion.1.k_ref, bf16[1024,1024]{1,0:T(8,128)(2,1)} %convert_bitcast_fusion.v_ref, ...), custom_call_target="tpu_custom_call" | custom-call | tf_op jit(solution)/shard_map/self_backward/pallas_call | solution.py:433
  438.6 5.3 fusion.77
  448.0 6.1 add_add_fusion
  454.1 5.7 copy.65
  492.6 89.8 %scatter_grads.2 = bf16[8,128,1024]{2,1,0:T(8,128)(2,1)} custom-call(bf16[8,1024,1024]{2,1,0:T(8,128)(2,1)} %bitcast_dynamic-update-slice_fusion.13.grads), custom_call_target="tpu_custom_call" | custom-call | tf_op jit(solution)/shard_map/scatter_grads/pallas_call | solution.py:258
  617.8 90.9 %scatter_grads.3 = bf16[8,128,1024]{2,1,0:T(8,128)(2,1)} custom-call(bf16[8,1024,1024]{2,1,0:T(8,128)(2,1)} %bitcast_dynamic-update-slice_fusion.5.grads), custom_call_target="tpu_custom_call" | custom-call | tf_op jit(solution)/shard_map/scatter_grads/pallas_call | solution.py:258
  718.2 39.5 %psum.7 = f32[6,1024]{1,0:T(8,128)S(1)} all-reduce(f32[6,1024]{1,0:T(8,128)S(1)} %stack.159), channel_id=1, replica_groups=mesh['rep'=4,'shard'=8] {'rep','shard'}, use_global_device_ids=true, to_apply=%region_18.0 | all-reduce | flops 6144 | bytes 49152 | tf_op jit(solution)/shard_map/psum | solution.py:558
  (228 shorter events, 154.3 us)
Async XLA Ops:
  0.7 219.9 %copy-start = (bf16[256,1024]{1,0:T(8,128)(2,1)S(1)}, bf16[256,1024]{1,0:T(8,128)(2,1)}, u32[]{:S(2)}) copy-start(bf16[256,1024]{1,0:T(8,128)(2,1)} %param.23) | copy-start | bytes 1572868
  0.7 6.3 copy-start.44
  0.7 7.0 copy-start.45
  0.7 7.7 %copy-start.46 = (bf16[128,1024]{1,0:T(8,128)(2,1)S(1)}, bf16[128,1024]{1,0:T(8,128)(2,1)}, u32[]{:S(2)}) copy-start(bf16[128,1024]{1,0:T(8,128)(2,1)} %param.31) | copy-start | bytes 786436
  0.7 8.5 %copy-start.47 = (bf16[128,1024]{1,0:T(8,128)(2,1)S(1)}, bf16[128,1024]{1,0:T(8,128)(2,1)}, u32[]{:S(2)}) copy-start(bf16[128,1024]{1,0:T(8,128)(2,1)} %param.32) | copy-start | bytes 786436
  0.7 10.8 %copy-start.40 = (bf16[128,4096]{1,0:T(8,128)(2,1)S(1)}, bf16[128,4096]{1,0:T(8,128)(2,1)}, u32[]{:S(2)}) copy-start(bf16[128,4096]{1,0:T(8,128)(2,1)} %param.34) | copy-start | bytes 3145732
  14.1 145.6 %copy-start.36 = (bf16[1024,1024]{1,0:T(8,128)(2,1)S(1)}, bf16[1024,1024]{1,0:T(8,128)(2,1)}, u32[]{:S(2)}) copy-start(bf16[1024,1024]{1,0:T(8,128)(2,1)} %param.22) | copy-start | bytes 6291460
  148.6 11.1 %copy-start.11 = (bf16[16,1024,1024]{2,1,0:T(8,128)(2,1)}, bf16[16,1024,1024]{2,1,0:T(8,128)(2,1)S(1)}, u32[]{:S(2)}) copy-start(bf16[16,1024,1024]{2,1,0:T(8,128)(2,1)S(1)} %get-tuple-element.43) | copy-start | bytes 100663296
  163.6 11.3 %copy-start.2 = (bf16[1024,1024]{1,0:T(8,128)(2,1)}, bf16[1024,1024]{1,0:T(8,128)(2,1)S(1)}, u32[]{:S(2)}) copy-start(bf16[1024,1024]{1,0:T(8,128)(2,1)S(1)} %fusion.139.q_ref) | copy-start | bytes 6291460
  200.3 9.6 %copy-start.3 = (bf16[1024,1024]{1,0:T(8,128)(2,1)}, bf16[1024,1024]{1,0:T(8,128)(2,1)S(1)}, u32[]{:S(2)}) copy-start(bf16[1024,1024]{1,0:T(8,128)(2,1)S(1)} %get-tuple-element.44.o_ref) | copy-start | bytes 6291460
  210.0 26.8 %copy-start.50 = (f32[1,8,128]{2,0,1:T(1,128)}, f32[1,8,128]{2,0,1:T(1,128)S(1)}, u32[]{:S(2)}) copy-start(f32[1,8,128]{2,0,1:T(1,128)S(1)} %get-tuple-element.102) | copy-start | bytes 12292
  223.6 18.6 %copy-start.7 = (bf16[256,1024]{1,0:T(8,128)(2,1)}, bf16[256,1024]{1,0:T(8,128)(2,1)S(1)}, u32[]{:S(2)}) copy-start(bf16[256,1024]{1,0:T(8,128)(2,1)S(1)} %fusion.162.refs_1_) | copy-start | bytes 1572868
  223.6 13.2 %copy-start.28 = (f32[1024,1024]{0,1:T(8,128)S(1)}, f32[1024,1024]{0,1:T(8,128)}, u32[]{:S(2)}) copy-start(f32[1024,1024]{0,1:T(8,128)} %copy-done.27) | copy-start | bytes 12582916
  226.2 16.0 %copy-start.9 = (bf16[256,1024]{1,0:T(8,128)(2,1)}, bf16[256,1024]{1,0:T(8,128)(2,1)S(1)}, u32[]{:S(2)}) copy-start(bf16[256,1024]{1,0:T(8,128)(2,1)S(1)} %fusion.159.refs_2_) | copy-start | bytes 1572868
  242.3 37.4 %copy-start.20 = (f32[1024,1024]{0,1:T(8,128)}, f32[1024,1024]{0,1:T(8,128)S(1)}, u32[]{:S(2)}) copy-start(f32[1024,1024]{0,1:T(8,128)S(1)} %get-tuple-element.113) | copy-start | bytes 12582916
  243.4 32.2 %copy-start.33 = (bf16[1024,1024]{0,1:T(8,128)(2,1)}, bf16[1024,1024]{0,1:T(8,128)(2,1)S(1)}, u32[]{:S(2)}) copy-start(bf16[1024,1024]{0,1:T(8,128)(2,1)S(1)} %fusion.29) | copy-start | bytes 6291460
  258.1 5.7 copy-start.64
  279.7 8.3 %copy-start.59 = (f32[1024,1024]{1,0:T(8,128)}, f32[1024,1024]{1,0:T(8,128)S(1)}, u32[]{:S(2)}) copy-start(f32[1024,1024]{1,0:T(8,128)S(1)} %fusion.56) | copy-start | bytes 12582916
  288.0 5.9 copy-start.22
  317.2 6.8 copy-start.72
  317.2 6.8 copy-start.68
  328.9 6.8 copy-start.74
  328.9 6.8 copy-start.60
  335.7 6.7 copy-start.21
  335.7 6.7 copy-start.23
  360.5 19.3 %copy-start.29 = (f32[1024,1024]{0,1:T(8,128)S(1)}, f32[1024,1024]{0,1:T(8,128)}, u32[]{:S(2)}) copy-start(f32[1024,1024]{0,1:T(8,128)} %copy-done.27) | copy-start | bytes 12582916
  379.7 7.2 copy-start.12
  379.7 7.2 copy-start.16
  388.0 60.0 %copy-start.25 = (f32[1024,1024]{0,1:T(8,128)}, f32[1024,1024]{0,1:T(8,128)S(1)}, u32[]{:S(2)}) copy-start(f32[1024,1024]{0,1:T(8,128)S(1)} %subtract_multiply_fusion) | copy-start | bytes 12582916
  388.0 6.9 copy-start.15
  459.8 6.0 copy-start.37
  480.8 6.1 copy-start.13
  (44 other events, 181.8 us)

commit v2 on v1

v2 whole, which is shorter than its diff:
```python
import functools

import jax
import jax.numpy as jnp
from jax import lax
from jax.experimental import pallas as pl
from jax.experimental.pallas import tpu as pltpu
from jax.sharding import PartitionSpec as P

HD = 64
PIC = 256
EPS = 1e-05
NEGATIVE = -1e30
INV_ROOT_TWO = 0.7071067811865476
INV_ROOT_TWO_PI = 0.3989422804014327
MESH = pl.DeviceIdType.MESH
MIB = 1 << 20
HBM = pl.BlockSpec(memory_space=pltpu.HBM)
bf16 = jnp.bfloat16
f32 = jnp.float32


def dot(a, b, ca=1, cb=0):
    return lax.dot_general(a, b, (((ca,), (cb,)), ((), ())), preferred_element_type=f32)


def place(n):
    half = n // 2

    def shard_at(pos):
        pos = lax.rem(pos + 2 * n, n)
        back = pos // half
        return (1 - back) * 2 * pos + back * (2 * (n - 1 - pos) + 1)

    s = lax.axis_index("shard")
    odd = s % 2
    pos = (1 - odd) * (s // 2) + odd * (n - 1 - s // 2)
    return pos, shard_at


def greet(partners):
    barrier = pltpu.get_barrier_semaphore()
    for who in partners:
        pl.semaphore_signal(barrier, inc=1, device_id=who, device_id_type=MESH)
    pl.semaphore_wait(barrier, len(partners))


def send(src, dst, ssem, rsem, who):
    copy = pltpu.make_async_remote_copy(
        src_ref=src, dst_ref=dst, send_sem=ssem, recv_sem=rsem, device_id=who, device_id_type=MESH
    )
    copy.start()
    return copy


def load(src, dst, sem):
    copy = pltpu.make_async_copy(src, dst, sem)
    copy.start()
    return copy


def neighbours(n):
    rep, shard = lax.axis_index("rep"), lax.axis_index("shard")
    x, c = rep // 2, rep % 2
    pos, shard_at = place(n)
    ways = (((rep, shard_at(pos + 1)), 1), ((rep, shard_at(pos - 1)), -1))
    sibling, across, corner = (x * 2 + 1 - c, shard), ((1 - x) * 2 + c, shard), ((1 - x) * 2 + 1 - c, shard)
    return x, c, shard, pos, shard_at, ways, sibling, across, corner


def remote(src, dst, ssem, rsem, who):
    return pltpu.make_async_remote_copy(
        src_ref=src, dst_ref=dst, send_sem=ssem, recv_sem=rsem, device_id=who, device_id_type=MESH
    )


def block_of(index, size):
    return pl.ds(pl.multiple_of(index * size, size), size)


class Gather:
    def __init__(self, n, width, shards, units, alone, owner_first=False, vec=None):
        self.n, self.shards, self.owner_first, self.vec = n, shards, owner_first, vec
        self.units, self.ne, self.ns = units, alone, units - 2 * alone
        self.rows, self.width = sum(s.size for s in shards) // (units * width), width
        self.arrays = list(shards) + ([] if vec is None else [vec])
        shape = (n, units, self.rows, self.width) if owner_first else (units, n * self.rows, self.width)
        self.out_shapes = [jax.ShapeDtypeStruct(shape, bf16)]
        dma = pltpu.SemaphoreType.DMA
        self.scratch = [pltpu.VMEM((units, self.rows, width), bf16), dma((2,))] + [dma((2, n - 1))] * 12
        if vec is not None:
            self.out_shapes.append(jax.ShapeDtypeStruct((n,) + vec.shape, vec.dtype))
            self.scratch += [dma((1,)), dma((n - 1,)), dma((n - 1,))]

    def bind(self, ins, outs, scratch):
        self.ins, self.full = ins, outs[0]
        self.own, self.local, *self.sems = scratch[:14]
        if self.vec is not None:
            self.vec_in, self.vecs, self.vec_sems = ins[-1], outs[1], scratch[14:]
            self.ins = ins[:-1]
        (self.x, self.c, self.shard, self.pos, self.shard_at, self.ways, self.sibling, self.across, _) = neighbours(self.n)
        on_ring = self.ne + self.ns
        self.mine = pl.ds(self.x * on_ring, self.ne)
        self.sets = (self.mine, pl.ds(self.ne, self.ns))
        self.theirs = pl.ds((1 - self.x) * on_ring, self.ne)

    def at(self, units, owner):
        if self.owner_first:
            return self.full.at[owner, units]
        return self.full.at[units, block_of(owner, self.rows), :]

    def spot(self, units, d, k):
        owner = self.shard_at(self.pos - self.ways[d][1] * k)
        quarter = self.rows // 4
        if self.owner_first:
            return self.full.at[owner, units, block_of(self.c * 2 + d, quarter), :]
        return self.full.at[units, block_of(owner * 4 + self.c * 2 + d, quarter), :]

    def moved(self, kind, units, d, k, hop, who):
        here = self.spot(units, d, k)
        return remote(here, here, self.sems[2 * kind].at[d, hop], self.sems[2 * kind + 1].at[d, hop], who)

    def first(self, e, d):
        src = self.own.at[self.sets[e], block_of(self.c * 2 + d, self.rows // 4), :]
        sems = self.sems[2 * e : 2 * e + 2]
        return remote(src, self.spot(self.sets[e], d, 0), sems[0].at[d, 0], sems[1].at[d, 0], self.ways[d][0])

    def stored(self):
        return pltpu.make_async_copy(self.own, self.at(pl.ds(0, self.units), self.shard), self.local.at[1])

    def ring(self, e, d, k):
        return self.moved(e, self.sets[e], d, k, k, self.ways[d][0])

    def side(self, e, d, k):
        return self.moved(2 + e, self.sets[e], d, k + 1, k, self.sibling)

    def cross(self, d, k):
        return self.moved(4, self.mine, d, k + 1, k, self.across)

    def forward(self, d, k):
        return self.moved(5, self.theirs, d, k + 1, k, self.sibling)

    def vec_hop(self, k):
        here = self.vecs.at[self.shard_at(self.pos - k)]
        return remote(here, here, self.vec_sems[1].at[k], self.vec_sems[2].at[k], self.ways[0][0])

    def begin(self):
        per = self.units // len(self.ins)
        for i, ref in enumerate(self.ins):
            for j in range(per):
                if ref.shape[1] > self.width:
                    part = ref.at[:, pl.ds(j * self.width, self.width)]
                else:
                    part = ref.at[pl.ds(j * self.rows, self.rows), :]
                pltpu.make_async_copy(part, self.own.at[i * per + j], self.local.at[0]).start()
        if self.vec is not None:
            pltpu.make_async_copy(self.vec_in, self.vecs.at[self.shard], self.vec_sems[0].at[0]).start()
        greet((self.ways[0][0], self.ways[1][0], self.sibling, self.across))
        pltpu.make_async_copy(self.own, self.own, self.local.at[0]).wait()
        for e in range(2):
            for d in range(2):
                self.first(e, d).start()
        self.stored().start()
        if self.vec is not None:
            pltpu.make_async_copy(self.vec_in, self.vecs.at[self.shard], self.vec_sems[0].at[0]).wait()

    def step(self, i):
        n = self.n
        pl.when(i == 0)(self.begin)

        for e in range(2):
            for d in range(2):

                @pl.when((i > 0) & (i < n))
                def _():
                    self.ring(e, d, i - 1).wait_recv()

                    @pl.when(i < n - 1)
                    def _():
                        self.ring(e, d, i).start()

                    if e == 0:
                        self.cross(d, i - 1).start()
                    self.side(e, d, i - 1).start()

        @pl.when((i > 1) & (i <= n))
        def _():
            for d in range(2):
                self.cross(d, i - 2).wait_recv()
                self.forward(d, i - 2).start()

        if self.vec is not None:
            @pl.when((i > 0) & (i < n))
            def _():
                self.vec_hop(i - 1).wait_recv()

            @pl.when(i < n - 1)
            def _():
                self.vec_hop(i).start()

    def finish(self, steps):
        n = self.n
        if steps <= n:
            for d in range(2):
                self.cross(d, n - 2).wait_recv()
                self.forward(d, n - 2).start()

        def drain(k, _):
            for d in range(2):
                for e in range(2):
                    self.ring(e, d, k).wait_send()
                    self.side(e, d, k).wait()
                self.cross(d, k).wait_send()
                self.forward(d, k).wait()
            if self.vec is not None:
                self.vec_hop(k).wait_send()
            return 0

        lax.fori_loop(0, n - 1, drain, 0)
        self.stored().wait()


class Scatter:
    def __init__(self, n, sources, alone, vec=None):
        self.n, self.arrays = n, list(sources) + ([] if vec is None else [vec])
        self.vec = vec
        self.counts = [1 if s.ndim == 2 else s.shape[s.ndim - 3] for s in sources]
        self.kinds = [s.ndim for s in sources]
        units = self.units = sum(self.counts)
        self.ne, self.ns = alone, units - 2 * alone
        first = sources[0].shape
        rows = self.rows = first[-2] if len(first) == 4 else first[-2] // n
        width = self.width = sources[0].shape[-1]
        half, self.quarter = rows // 2, rows // 4
        self.out_shapes = [jax.ShapeDtypeStruct((units, rows, width), bf16)]
        dma = pltpu.SemaphoreType.DMA
        self.scratch = [
            pltpu.VMEM((units, n * half, width), bf16),
            pltpu.VMEM((units, n * half, width), bf16),
            pltpu.VMEM((alone, n * half, width), bf16),
            pltpu.VMEM((2, n - 1, alone, half // 2, width), bf16),
            pltpu.VMEM((2, n - 1, self.ns, half // 2, width), bf16),
            pltpu.VMEM((self.ns, half, width), bf16),
            pltpu.VMEM((alone, half, width), bf16),
            dma((2, n)), dma((2, n)), dma((2, n)), dma((2, n)), dma((2, n)),
            dma((2, n - 1)), dma((2, n - 1)), dma((2, n - 1)), dma((2, n - 1)),
            dma((2,)), dma((2,)), dma((3,)), dma((3,)), dma((3,)),
        ]
        if vec is not None:
            self.out_shapes.append(jax.ShapeDtypeStruct((8, rows), f32))
            self.scratch += [
                pltpu.VMEM((n, 8, rows), f32), pltpu.VMEM((n - 1, 8, rows), f32), pltpu.VMEM((4, 8, rows), f32),
                pltpu.VMEM((8, rows), f32), dma((2,)), dma((n - 1,)), dma((n - 1,)), dma((3,)), dma((3,)),
            ]

    def bind(self, ins, outs, scratch):
        self.ins, self.out = ins, outs[0]
        (self.near, self.beside, self.over, slots_e, slots_s, self.swap_s, self.swap_e, self.local, self.cs, self.cr,
         self.xs, self.xr, *ring_sems, self.ss, self.sr, self.os, self.orr, self.done) = scratch[:21]
        self.slots, self.ring_sems = (slots_e, slots_s), (ring_sems[:2], ring_sems[2:])
        if self.vec is not None:
            self.vec_in, self.vec_out, self.ins = ins[-1], outs[1], ins[:-1]
            (self.v_near, self.v_ring, self.v_all, self.v_sum, self.v_local, self.v_rs, self.v_rr,
             self.v_ss, self.v_sr) = scratch[21:]
        (self.x, self.c, self.shard, self.pos, self.shard_at, self.ways, self.sibling, self.across,
         self.corner) = neighbours(self.n)
        self.on_ring = self.ne + self.ns
        self.theirs = pl.ds((1 - self.x) * self.on_ring, self.ne)
        self.mine = pl.ds(self.x * self.on_ring, self.ne)
        self.shared = pl.ds(self.ne, self.ns)
        self.sets = (self.mine, self.shared)

    def owner(self, d, k):
        return self.shard_at(self.pos - self.ways[d][1] * (1 + k))

    def span(self, d, k):
        return block_of(self.owner(d, k) * 2 + d, self.quarter)

    def region(self, ref, d, k):
        return ref.at[:, self.span(d, k), :]

    def pieces(self, d, k, core, target):
        owner = self.owner(d, k)
        u = 0
        for ref, count, kind in zip(self.ins, self.counts, self.kinds):
            rows = block_of(owner * 4 + core * 2 + d, self.quarter)
            if kind == 4:
                src = ref.at[owner, :, block_of(core * 2 + d, self.quarter), :]
            else:
                src = ref.at[rows, :] if kind == 2 else ref.at[:, rows, :]
            units = u if kind == 2 else pl.ds(u, count)
            yield src, target.at[units, self.span(d, k), :]
            u += count

    def crossing(self, d, k):
        rows = self.span(d, k)
        return remote(
            self.near.at[self.theirs, rows, :], self.over.at[:, rows, :], self.xs.at[d, k], self.xr.at[d, k], self.across
        )

    def hop(self, e, d, k):
        src = self.near.at[self.sets[e], self.span(d, k), :]
        sent, got = self.ring_sems[e]
        return remote(src, self.slots[e].at[d, k], sent.at[d, k], got.at[d, k], self.ways[d][0])

    def vec_hop(self, k):
        return remote(self.v_near.at[self.owner(0, k)], self.v_ring.at[k], self.v_rs.at[k], self.v_rr.at[k], self.ways[0][0])

    def begin(self):
        n = self.n

        def loads(k, _):
            for d in range(2):
                for src, dst in self.pieces(d, k, self.c, self.near):
                    pltpu.make_async_copy(src, dst, self.local.at[d, k]).start()
            return 0

        lax.fori_loop(0, n, loads, 0)
        if self.vec is not None:
            for s in range(n):
                pltpu.make_async_copy(
                    self.vec_in.at[:, pl.ds(s * self.rows, self.rows)], self.v_near.at[s], self.v_local.at[0]
                ).start()
        greet((self.ways[0][0], self.ways[1][0], self.sibling, self.across) + (() if self.vec is None else (self.corner,)))

        def sends(k, _):
            for d in range(2):
                for src, dst in self.pieces(d, k, 1 - self.c, self.beside):
                    remote(src, dst, self.cs.at[d, k], self.cr.at[d, k], self.sibling).start()
            return 0

        lax.fori_loop(0, n, sends, 0)
        if self.vec is not None:
            pltpu.make_async_copy(self.v_near, self.v_near, self.v_local.at[0]).wait()
        self.pair(0)
        self.pair(1)

    def arrived(self, ref, ssem, rsem, d, k):
        here = self.region(ref, d, k)
        return remote(here, here, ssem.at[d, k], rsem.at[d, k], self.sibling)

    def pair(self, k):
        for d in range(2):
            rows = self.span(d, k)
            here = self.region(self.near, d, k)
            pltpu.make_async_copy(here, here, self.local.at[d, k]).wait()
            self.arrived(self.beside, self.cs, self.cr, d, k).wait_recv()

            def add(u, _):
                self.near[u, rows, :] = self.near[u, rows, :] + self.beside[u, rows, :]
                return 0

            lax.fori_loop(0, self.units, add, 0)
            self.crossing(d, k).start()

    def combine(self, k, later):
        for e in (1, 0):
            for d in range(2):
                rows = self.span(d, k)
                if later:
                    self.hop(e, d, k - 1).wait_recv()
                if e == 0:
                    self.crossing(d, k).wait_recv()

                def add_shared(i, _):
                    u = self.ne + i
                    self.near[u, rows, :] = self.near[u, rows, :] + self.slots[1][d, k - 1, i]
                    return 0

                def add_mine(i, _):
                    u = self.x * self.on_ring + i
                    value = self.near[u, rows, :].astype(f32) + self.over[i, rows, :].astype(f32)
                    if later:
                        value = value + self.slots[0][d, k - 1, i].astype(f32)
                    self.near[u, rows, :] = value.astype(bf16)
                    return 0

                if e == 0:
                    lax.fori_loop(0, self.ne, add_mine, 0)
                elif later:
                    lax.fori_loop(0, self.ns, add_shared, 0)

                @pl.when(k < self.n - 1)
                def _():
                    self.hop(e, d, k).start()

        if self.vec is not None:
            if later:
                self.vec_hop(k - 1).wait_recv()
                self.v_near[self.owner(0, k)] = self.v_near[self.owner(0, k)] + self.v_ring[k - 1]

            @pl.when(k < self.n - 1)
            def _():
                self.vec_hop(k).start()

    def step(self, i):
        pl.when(i == 0)(self.begin)

        @pl.when(i == 0)
        def _():
            self.combine(i, False)

        @pl.when((i > 0) & (i < self.n))
        def _():
            self.combine(i, True)

        @pl.when(i + 2 < self.n)
        def _():
            self.pair(i + 2)

    def finish(self, steps):
        n = self.n
        at = block_of(self.shard, self.rows // 2)
        half = block_of(self.c, self.rows // 2)
        near, out = self.near, self.out
        swap = send(near.at[self.shared, at, :], self.swap_s, self.ss.at[0], self.sr.at[0], self.across)
        give = send(near.at[self.mine, at, :], self.swap_e, self.ss.at[1], self.sr.at[1], self.across)
        final = [send(near.at[self.mine, at, :], out.at[self.mine, half, :], self.os.at[0], self.orr.at[0], self.sibling)]
        keep = [load(near.at[self.mine, at, :], out.at[self.mine, half, :], self.done.at[0])]
        if self.vec is not None:
            sums = self.v_near.at[self.shard]
            rep = self.x * 2 + self.c
            shares = [
                send(sums, self.v_all.at[rep], self.v_ss.at[j], self.v_sr.at[j], who)
                for j, who in enumerate((self.sibling, self.across, self.corner))
            ]
            self.v_all[rep] = sums[...]
        swap.wait_recv()

        def join(i, _):
            self.swap_s[i] = (self.swap_s[i].astype(f32) + near[self.ne + i, at, :].astype(f32)).astype(bf16)
            return 0

        lax.fori_loop(0, self.ns, join, 0)
        final.append(send(self.swap_s, out.at[self.shared, half, :], self.os.at[1], self.orr.at[1], self.sibling))
        keep.append(load(self.swap_s, out.at[self.shared, half, :], self.done.at[1]))
        give.wait_recv()
        final.append(send(self.swap_e, out.at[self.theirs, half, :], self.os.at[2], self.orr.at[2], self.sibling))
        keep.append(load(self.swap_e, out.at[self.theirs, half, :], self.done.at[2]))
        if self.vec is not None:
            for copy in shares:
                copy.wait()
            self.v_sum[...] = (self.v_all[0] + self.v_all[1]) + (self.v_all[2] + self.v_all[3])
            keep.append(load(self.v_sum, self.vec_out, self.v_local.at[1]))
        for copy in keep:
            copy.wait()
        for copy in final:
            copy.wait()
        swap.wait_send()
        give.wait_send()

        def drain(k, _):
            for d in range(2):
                self.arrived(self.beside, self.cs, self.cr, d, k).wait_send()
                self.crossing(d, k).wait_send()
            return 0

        lax.fori_loop(0, n, drain, 0)

        def drain_ring(k, _):
            for d in range(2):
                self.hop(0, d, k).wait_send()
                self.hop(1, d, k).wait_send()
            if self.vec is not None:
                self.vec_hop(k).wait_send()
            return 0

        lax.fori_loop(0, n - 1, drain_ring, 0)


def hosted(kernel, steps, args, in_specs, out_shapes, out_specs, scratch, name, carry=None, collective_id=None, done_by=None, vmem=58):
    counts = [len(args), len(out_shapes), len(scratch)]
    extra = [0, 0, 0]
    params = dict(vmem_limit_bytes=vmem * MIB)
    if carry is not None:
        extra = [len(carry.arrays), len(carry.out_shapes), len(carry.scratch)]
        params.update(collective_id=collective_id, has_side_effects=True)

    def whole(*refs):
        main, other, first = [], [], 0
        for count, more in zip(counts, extra):
            main += refs[first : first + count]
            other.append(refs[first + count : first + count + more])
            first += count + more
        i = pl.program_id(0)
        if carry is not None:
            carry.bind(*other)
            carry.step(i)
            if done_by is not None:
                pl.when(i == done_by)(lambda: carry.finish(done_by + 1))
        if kernel is not None:
            kernel(*main)
        if carry is not None and done_by is None:
            pl.when(i == steps - 1)(lambda: carry.finish(steps))

    return pl.pallas_call(
        whole,
        grid=(steps,),
        out_shape=list(out_shapes) + (carry.out_shapes if carry else []),
        in_specs=list(in_specs) + [HBM] * extra[0],
        out_specs=list(out_specs) + [HBM] * extra[1],
        scratch_shapes=list(scratch) + (carry.scratch if carry else []),
        compiler_params=pltpu.CompilerParams(**params),
        name=name,
    )(*args, *(carry.arrays if carry else []))


def first_lanes(shape):
    return lax.broadcasted_iota(jnp.int32, shape, len(shape) - 1) < HD


def region_bias(starts_ref, region, size, transposed):
    first = region * size
    one = first + lax.broadcasted_iota(jnp.int32, (size, size), 0)
    two = first + lax.broadcasted_iota(jnp.int32, (size, size), 1)
    q_at, k_at = (two, one) if transposed else (one, two)
    start = starts_ref[0, region]
    q_in = (q_at >= start) & (q_at < start + PIC)
    k_in = (k_at >= start) & (k_at < start + PIC)
    return jnp.where((k_at <= q_at) | (q_in & k_in), 0.0, NEGATIVE)


def attend_forward_kernel(regions, starts_ref, q_ref, k_ref, v_ref, o_ref, lse_ref, bias_ref):
    rows = q_ref.shape[0]
    size = rows // regions

    if starts_ref is not None:
        @pl.when(pl.program_id(0) == 0)
        def _():
            for r in range(regions):
                bias_ref[r] = region_bias(starts_ref, r, size, False)

    low = first_lanes((1, 2 * HD))
    outs, lses = [[], []], [[], []]
    for h in range(2):
        pick = low if h == 0 else ~low
        keys = jnp.where(pick, k_ref[...], jnp.zeros((), bf16))
        for r in range(regions):
            span = slice(r * size, (r + 1) * size)
            q = q_ref[span, :]
            scores = []
            if starts_ref is None:
                scores.append((dot(q, keys, 1, 1), v_ref[...]))
            else:
                if r:
                    scores.append((dot(q, keys[: r * size], 1, 1), v_ref[: r * size, :]))
                scores.append((dot(q, keys[span], 1, 1) + bias_ref[r], v_ref[span, :]))
            top = functools.reduce(jnp.maximum, [jnp.max(s, -1, keepdims=True) for s, _ in scores])
            total, mixed = 0.0, 0.0
            for s, v in scores:
                e = jnp.exp(s - top)
                total = total + jnp.sum(e, -1, keepdims=True)
                mixed = mixed + dot(e.astype(bf16), v)
            outs[h].append(mixed / total)
            lses[h].append(top + jnp.log(total))
    for r in range(regions):
        span = slice(r * size, (r + 1) * size)
        o_ref[span, :] = jnp.where(low, outs[0][r], outs[1][r]).astype(bf16)
        turned = jnp.where(low, lses[0][r], lses[1][r]).T
        lse_ref[0, 0:1, span] = turned[0:1]
        lse_ref[0, 1:2, span] = turned[HD : HD + 1]


def attend_parts(kernel, regions_of, starts, arrays, rows):
    tall = [pl.BlockSpec((a.shape[0], 2 * HD), lambda i: (0, i)) if a.ndim == 2 else pl.BlockSpec((1, 8, rows), lambda i: (i, 0, 0)) for a in arrays]
    if starts is None:
        return lambda *refs: kernel(regions_of, None, *refs, None), list(arrays), tall, []
    size = rows // regions_of
    scratch = [pltpu.VMEM((regions_of, size, size), f32)]
    return functools.partial(kernel, regions_of), [starts, *arrays], [pl.BlockSpec(memory_space=pltpu.SMEM), *tall], scratch


def attend_forward(q, k, v, starts, carry, collective_id):
    rows, width = q.shape
    pairs = width // (2 * HD)
    kernel, args, specs, scratch = attend_parts(
        attend_forward_kernel, 2 if starts is None else starts.shape[1], starts, (q, k, v), rows
    )
    return hosted(
        kernel, pairs, args, specs,
        [jax.ShapeDtypeStruct((rows, width), bf16), jax.ShapeDtypeStruct((pairs, 8, rows), f32)],
        [pl.BlockSpec((rows, 2 * HD), lambda i: (0, i)), pl.BlockSpec((1, 8, rows), lambda i: (i, 0, 0))],
        scratch, "self_forward" if starts is not None else "cross_forward", carry, collective_id,
    )


def attend_backward_kernel(
    regions, starts_ref, q_ref, k_ref, v_ref, g_ref, o_ref, lse_ref, gq_ref, gk_ref, gv_ref, bias_ref
):
    rows = q_ref.shape[0]
    size = rows // regions

    if starts_ref is not None:
        @pl.when(pl.program_id(0) == 0)
        def _():
            for r in range(regions):
                bias_ref[r] = region_bias(starts_ref, r, size, True)

    low = first_lanes((1, 2 * HD))
    product = g_ref[...].astype(f32) * o_ref[...].astype(f32)
    chooser = lax.broadcasted_iota(jnp.int32, (8, 2 * HD), 0)
    chooser = ((chooser == 0) & first_lanes((8, 2 * HD))) | ((chooser == 1) & ~first_lanes((8, 2 * HD)))
    chooser = chooser.astype(f32).astype(bf16)
    upper = product.astype(bf16)
    lower = (product - upper.astype(f32)).astype(bf16)
    deltas = dot(chooser, upper, 1, 1) + dot(chooser, lower, 1, 1)
    gq, gk, gv = {}, {}, {}
    key_spans = [slice(0, k_ref.shape[0])]
    if starts_ref is not None:
        key_spans = [slice(r * size, (r + 1) * size) for r in range(regions)]
    for h in range(2):
        pick = low if h == 0 else ~low
        zero = jnp.zeros((), bf16)
        keys = jnp.where(pick, k_ref[...], zero)
        values = jnp.where(pick, v_ref[...], zero)
        for r in range(regions):
            span = slice(r * size, (r + 1) * size)
            q, g = q_ref[span, :], g_ref[span, :]
            lse = lse_ref[0, h : h + 1, span]
            delta = deltas[h : h + 1, span]
            for j, keyed in enumerate(key_spans):
                if starts_ref is not None and j > r:
                    continue
                scores = dot(keys[keyed], q, 1, 1)
                if starts_ref is not None and j == r:
                    scores = scores + bias_ref[r]
                probs = jnp.exp(scores - lse)
                grad_probs = dot(values[keyed], g, 1, 1)
                grad_scores = (probs * (grad_probs - delta)).astype(bf16)
                gv[h, j] = gv.get((h, j), 0.0) + dot(probs.astype(bf16), g)
                gk[h, j] = gk.get((h, j), 0.0) + dot(grad_scores, q)
                gq[h, r] = gq.get((h, r), 0.0) + dot(grad_scores, k_ref[keyed, :], 0, 0)
    for r in range(regions):
        span = slice(r * size, (r + 1) * size)
        gq_ref[span, :] = jnp.where(low, gq[0, r], gq[1, r]).astype(bf16)
    for j, keyed in enumerate(key_spans):
        gk_ref[keyed, :] = jnp.where(low, gk[0, j], gk[1, j]).astype(bf16)
        gv_ref[keyed, :] = jnp.where(low, gv[0, j], gv[1, j]).astype(bf16)


def attend_backward(q, k, v, g, o, lse, starts, carry, collective_id):
    rows, width = q.shape
    kernel, args, specs, scratch = attend_parts(
        attend_backward_kernel, 2 if starts is None else starts.shape[1], starts, (q, k, v, g, o, lse), rows
    )
    return hosted(
        kernel, width // (2 * HD), args, specs,
        [jax.ShapeDtypeStruct(a.shape, bf16) for a in (q, k, v)],
        [pl.BlockSpec((a.shape[0], 2 * HD), lambda i: (0, i)) for a in (q, k, v)],
        scratch, "self_backward" if starts is not None else "cross_backward", carry, collective_id,
    )


def norm_forward(resid, gain, shift):
    mean = jnp.mean(resid, -1, keepdims=True)
    centred = resid - mean
    variance = jnp.mean(centred * centred, -1, keepdims=True)
    inverse = lax.rsqrt(variance + EPS)
    normed = centred * inverse
    return (normed * gain + shift, normed, inverse)


def norm_backward(grad_out, normed, inverse, gain):
    grad_gain = jnp.sum(grad_out * normed, 0, keepdims=True)
    grad_shift = jnp.sum(grad_out, 0, keepdims=True)
    grad_normed = grad_out * gain
    centre_term = jnp.mean(grad_normed, -1, keepdims=True)
    slope_term = jnp.mean(grad_normed * normed, -1, keepdims=True)
    return (inverse * (grad_normed - centre_term - normed * slope_term), grad_gain, grad_shift)


def fixed(a):
    zeros = (0,) * a.ndim
    return pl.BlockSpec(a.shape, lambda i: zeros, pipeline_mode=pl.Buffered(1))


def slices(rows, count):
    size = rows // count
    return [slice(j * size, (j + 1) * size) for j in range(count)]


def ffn_forward_kernel(blocks, carry, low_ref, two_ref, cot_ref, vec_ref, w1_ref, *refs):
    refs = list(refs)
    w2_ref = refs.pop(0) if carry is None else carry.full
    final_ref, branch_ref, grad_ref, act_ref, slope_ref, sums_ref, acts, acc, w2_buf, sems = refs
    i = pl.program_id(0)
    spans = slices(low_ref.shape[0], 4)

    @pl.when(i < blocks)
    def _():
        for span in spans:
            pre = dot(low_ref[span, :], w1_ref[0])
            phi = 0.5 * (1.0 + lax.erf(pre * INV_ROOT_TWO))
            act = (pre * phi).astype(bf16)
            acts[i, span, :] = act
            act_ref[span, :] = act
            slope_ref[span, :] = (phi + pre * jnp.exp(-0.5 * pre * pre) * INV_ROOT_TWO_PI).astype(bf16)

    j = i - blocks

    def fetch(block, slot):
        return pltpu.make_async_copy(w2_ref.at[block], w2_buf.at[slot], sems.at[slot])

    @pl.when(j == 0)
    def _():
        fetch(0, 0).start()
        acc[...] = two_ref[...]

    @pl.when(j >= 0)
    def _():
        slot = lax.rem(j + blocks * 2, 2)

        @pl.when(j + 1 < blocks)
        def _():
            fetch(j + 1, 1 - slot).start()

        fetch(j, slot).wait()
        w2 = w2_buf[slot].reshape(-1, w2_buf.shape[-1])
        for span in spans:
            acc[span, :] += dot(acts[j, span, :], w2)

    @pl.when(j == blocks - 1)
    def _():
        gain, shift = vec_ref[4:5, :], vec_ref[5:6, :]
        sums = [0.0, 0.0]
        for span in slices(low_ref.shape[0], 8):
            final, normed, inverse = norm_forward(acc[span, :], gain, shift)
            final_ref[span, :] = final.astype(bf16)
            grad, *parts = norm_backward(cot_ref[span, :].astype(f32), normed, inverse, gain)
            grad_ref[span, :] = grad
            branch_ref[span, :] = grad.astype(bf16)
            sums = [a + b for a, b in zip(sums, parts)]
        sums_ref[...] = jnp.zeros_like(sums_ref)
        sums_ref[0:1, :] = sums[0]
        sums_ref[1:2, :] = sums[1]


def ffn_forward(low, two, cotangent, vecs, w1, w2, carry, collective_id):
    rows, width = low.shape
    if carry is not None:
        blocks, size = carry.n, carry.units * carry.rows
    else:
        blocks, size = w2.shape[0], w2.shape[1] * w2.shape[2]
    per = width // size
    last = blocks - 1
    args = [low, two, cotangent, vecs, w1]
    specs = [fixed(a) for a in args[:4]]
    specs.append(pl.BlockSpec((1, width, size), lambda i: (jnp.minimum(i, last) // per, 0, lax.rem(jnp.minimum(i, last), per))))
    if carry is None:
        args.append(w2)
        specs.append(HBM)
    tall = jax.ShapeDtypeStruct((rows, blocks * size), bf16)
    outs = [low, low, two, tall, tall, jax.ShapeDtypeStruct((8, width), f32)]
    out_specs = [fixed(a) for a in outs[:3]]
    out_specs += [pl.BlockSpec((rows, size), lambda i: (0, jnp.minimum(i, last)))] * 2 + [fixed(outs[5])]
    part = (width // 256, size // (width // 256), width) if carry is None else (carry.units, carry.rows, width)
    return hosted(
        functools.partial(ffn_forward_kernel, blocks, carry), 2 * blocks, args, specs,
        [jax.ShapeDtypeStruct(a.shape, a.dtype) for a in outs], out_specs,
        [
            pltpu.VMEM((blocks, rows, size), bf16), pltpu.VMEM((rows, width), f32),
            pltpu.VMEM((2,) + part, bf16), pltpu.SemaphoreType.DMA((2,)),
        ],
        "ffn_forward", carry, collective_id, done_by=blocks if carry else None, vmem=60,
    )


def ffn_backward_kernel(
    low_ref, branch_ref, g_ref, normed_ref, inverse_ref, vec_ref, w1_ref, w2_ref, act_ref, slope_ref,
    g_expand_ref, g_contract_ref, grad_ref, branch_two_ref, sums_ref, turned, acc,
):
    i = pl.program_id(0)
    rows = low_ref.shape[0]
    spans = slices(rows, 4)

    @pl.when(i == 0)
    def _():
        turned[...] = low_ref[...].T
        acc[...] = g_ref[...]

    w2 = w2_ref[0].reshape(-1, w2_ref.shape[-1])
    g_contract_ref[0] = dot(act_ref[...], branch_ref[...], 0, 0).astype(bf16).reshape(g_contract_ref.shape[1:])
    expand = 0.0
    for span in spans:
        g_pre = (dot(branch_ref[span, :], w2, 1, 1) * slope_ref[span, :].astype(f32)).astype(bf16)
        expand = expand + dot(turned[:, span], g_pre)
        acc[span, :] += dot(g_pre, w1_ref[0], 1, 1)
    g_expand_ref[0] = expand.astype(bf16)

    @pl.when(i == pl.num_programs(0) - 1)
    def _():
        gain = vec_ref[2:3, :]
        sums = [0.0, 0.0]
        for span in slices(rows, 8):
            grad, *parts = norm_backward(acc[span, :], normed_ref[span, :], inverse_ref[span, :], gain)
            grad_ref[span, :] = grad
            branch_two_ref[span, :] = grad.astype(bf16)
            sums = [a + b for a, b in zip(sums, parts)]
        sums_ref[...] = jnp.zeros_like(sums_ref)
        sums_ref[0:1, :] = sums[0]
        sums_ref[1:2, :] = sums[1]


def ffn_backward(low, branch, grad, normed, inverse, vecs, w1, w2, act, slope):
    rows, width = low.shape
    blocks, size = w2.shape[0], w2.shape[1] * w2.shape[2]
    per = width // size
    wide = pl.BlockSpec((1, width, size), lambda i: (i // per, 0, lax.rem(i, per)))
    deep = pl.BlockSpec((1,) + w2.shape[1:], lambda i: (i, 0, 0, 0))
    column = pl.BlockSpec((rows, size), lambda i: (0, i))
    args = [low, branch, grad, normed, inverse, vecs, w1, w2, act, slope]
    outs = [w1, w2, grad, low, jax.ShapeDtypeStruct((8, width), f32)]
    return hosted(
        ffn_backward_kernel, blocks, args, [fixed(a) for a in args[:6]] + [wide, deep, column, column],
        [jax.ShapeDtypeStruct(a.shape, a.dtype) for a in outs], [wide, deep] + [fixed(a) for a in outs[2:]],
        [pltpu.VMEM((width, rows), bf16), pltpu.VMEM((rows, width), f32)], "ffn_backward", vmem=60,
    )


def body(n, states, encoded, starts, cotangent, *weights):
    matrices, vectors = weights[:10], weights[10:]
    expand, contract = matrices[8], matrices[9]
    rows, width = matrices[0].shape
    blocks = contract.shape[0] // rows
    scale = HD ** (-0.5)
    small = n <= 16
    vec = jnp.zeros((16, max(rows, 128)), bf16).at[: len(vectors), :rows].set(jnp.stack(vectors))
    take = lambda shards, units, alone, **more: Gather(n, width, shards, units, alone, **more) if small else None
    if small:
        first, vecs = hosted(None, n, [], [], [], [], [], "gather_first", take(matrices[:3], 3, 1, vec=vec), 0)
    else:
        first = lax.all_gather(jnp.stack(matrices[:3]), "shard", axis=1, tiled=True)
        vecs = lax.all_gather(vec, "shard", axis=0)
    vecs = vecs[:, : len(vectors), :rows].transpose(1, 0, 2).reshape(len(vectors), width).astype(f32)
    vecs = jnp.concatenate([vecs, jnp.zeros((2, width), f32)])
    gain_one, shift_one, gain_two, shift_two = [vecs[i] for i in range(4)]
    w_sq, w_sk, w_sv = [first[i] for i in range(3)]

    wide = states.astype(f32)
    q_self = (dot(states, w_sq) * scale).astype(bf16)
    k_self = dot(states, w_sk).astype(bf16)
    v_self = dot(states, w_sv).astype(bf16)
    mixed_self, lse_self, *second = attend_forward(q_self, k_self, v_self, starts, take(matrices[3:8], 5, 2), 1)
    if not small:
        second = [lax.all_gather(jnp.stack(matrices[3:8]), "shard", axis=1, tiled=True)]
    w_so, w_cq, w_ck, w_cv, w_co = [second[0][i] for i in range(5)]
    hidden_one, normed_one, inverse_one = norm_forward(wide + dot(mixed_self, w_so), gain_one, shift_one)
    one_low = hidden_one.astype(bf16)
    q_cross = (dot(one_low, w_cq) * scale).astype(bf16)
    k_cross = dot(encoded, w_ck).astype(bf16)
    v_cross = dot(encoded, w_cv).astype(bf16)
    mixed_cross, lse_cross, *third = attend_forward(q_cross, k_cross, v_cross, None, take([expand], blocks, 1), 2)
    if not small:
        third = [lax.all_gather(expand.reshape(rows, blocks, width).transpose(1, 0, 2), "shard", axis=1, tiled=True)]
    w1 = third[0]
    hidden_two, normed_two, inverse_two = norm_forward(hidden_one + dot(mixed_cross, w_co), gain_two, shift_two)
    two_low = hidden_two.astype(bf16)
    w2 = None
    if not small:
        w2 = lax.all_gather(contract, "shard", axis=0, tiled=True).reshape(8, 4, -1, width)
    final, branch_three, grad_three, act, slope, sums_three, *fourth = ffn_forward(
        two_low, hidden_two, cotangent, vecs, w1, w2, take([contract], blocks, 1, owner_first=True), 3
    )
    if small:
        w2 = fourth[0]

    give = lambda sources, alone, **more: Scatter(n, sources, alone, **more) if small else None
    g_expand, g_contract, grad_resid_two, branch_two, sums_two = ffn_backward(
        two_low, branch_three, grad_three, normed_two, inverse_two, vecs, w1, w2, act, slope
    )
    g_cross_out = dot(mixed_cross, branch_two, 0, 0).astype(bf16)
    grad_mixed = dot(branch_two, w_co, 1, 1).astype(bf16)
    g_q, g_k, g_v, *own_contract = attend_backward(
        q_cross, k_cross, v_cross, grad_mixed, mixed_cross, lse_cross, None, give([g_contract], 1), 4
    )
    g_q = g_q * scale
    g_cross = [
        dot(one_low, g_q, 0, 0).astype(bf16), dot(encoded, g_k, 0, 0).astype(bf16), dot(encoded, g_v, 0, 0).astype(bf16),
        g_cross_out,
    ]
    grad_encoded = dot(g_k, w_ck, 1, 1) + dot(g_v, w_cv, 1, 1)
    grad_one = grad_resid_two + dot(g_q, w_cq, 1, 1)
    grad_resid_one, *sums_one = norm_backward(grad_one, normed_one, inverse_one, gain_one)
    branch_one = grad_resid_one.astype(bf16)
    g_self_out = dot(mixed_self, branch_one, 0, 0).astype(bf16)
    grad_mixed = dot(branch_one, w_so, 1, 1).astype(bf16)
    g_q, g_k, g_v, *own_middle = attend_backward(
        q_self, k_self, v_self, grad_mixed, mixed_self, lse_self, starts, give([g_expand, *g_cross], 2), 5
    )
    g_q = g_q * scale
    g_self = [dot(states, g, 0, 0).astype(bf16) for g in (g_q, g_k, g_v)] + [g_self_out]
    grad_states = grad_resid_one + dot(g_q, w_sq, 1, 1) + dot(g_k, w_sk, 1, 1) + dot(g_v, w_sv, 1, 1)
    grads_vec = jnp.concatenate([*sums_one, sums_two[:2], sums_three[:2], jnp.zeros((2, width), f32)])
    if small:
        own_self, own_vec = hosted(None, n, [], [], [], [], [], "scatter_last", give(g_self, 1, vec=grads_vec), 6)
        own_contract, own_middle = own_contract[0], own_middle[0]
    else:
        total = lambda g: lax.psum(lax.psum_scatter(g, "shard", scatter_dimension=1, tiled=True), "rep")
        own_self = total(jnp.stack(g_self))
        own_middle = total(jnp.concatenate([g_expand, jnp.stack(g_cross)]))
        own_contract = total(g_contract.reshape(1, -1, width))
        own_vec = lax.dynamic_slice_in_dim(
            lax.psum(grads_vec, ("rep", "shard")), lax.axis_index("shard") * rows, rows, 1
        )
    own_contract = own_contract.reshape(blocks * rows, width).astype(f32)
    own_expand = jnp.concatenate([own_middle[j] for j in range(blocks)], 1).astype(f32)
    attention = [own_self[j] for j in range(4)] + [own_middle[blocks + j] for j in range(4)]
    return (
        final,
        grad_states,
        grad_encoded,
        *[g.astype(f32) for g in attention],
        own_expand,
        own_contract,
        *[own_vec[i] for i in range(6)],
    )


def solution(mesh):
    many, few = P(("rep", "shard"), None), P("shard", None)
    return jax.shard_map(
        functools.partial(body, mesh.shape["shard"]),
        mesh=mesh,
        in_specs=(many,) * 4 + (few,) * 10 + (P("shard"),) * 6,
        out_specs=(many,) * 3 + (few,) * 10 + (P("shard"),) * 6,
        check_vma=False,
    )
```

time: 768 us -> 605 us (0.79)
  matrix products: 227 us -> 106 us
  local copies, waits for them, and re-layouts: 60.6 us -> 15.1 us
  Pallas kernels: 412 us -> 455 us
  blocking collectives: 39.5 us -> 0 us
    dot_general x48 -> x24, matrix products: 227 us -> 106 us  [dot(): lax.dot_general(a, b, (((ca,), (cb,)), ((), ())), preferred_element_type=...]
    pallas_call x7 -> x8, Pallas kernels: 412 us -> 455 us  [hosted(): pl.pallas_call(whole, grid=(steps,), out_shape=list(out_shapes) + (carry....]
    unnamed x166 -> x49, local copies, waits for them, and re-layouts: 47.7 us -> 5.88 us
    psum x1 -> x0, blocking collectives: 39.5 us -> none  [body(): grads_vec = lax.psum(grads_vec, ('rep', 'shard'))]
where the time goes in v2:
time: 605 us; the launch traced here: 597 us
  Pallas kernels  455 us (75%)
  matrix products  106 us (18%)
  other arithmetic  20.8 us (3%)
  local copies, waits for them, and re-layouts  15.1 us (2%)
    pallas_call x8, Pallas kernels, hosted(): pl.pallas_call(whole, grid=(steps,), out_shape=list(out_shapes) + (carry....  455 us
    dot_general x24, matrix products, dot(): lax.dot_general(a, b, (((ca,), (cb,)), ((), ())), preferred_element_type=...  106 us

profile of v2, /device:TPU:0, one launch (start us, length us, event | category | flops | bytes accessed | tf_op | source)
XLA Modules:
  0.0 597.4 jit_solution(13093470447626151879)
XLA Ops:
  2.1 38.5 %gather_first.1 = (bf16[3,1024,1024]{2,1,0:T(8,128)(2,1)}, bf16[8,16,128]{2,1,0:T(8,128)(2,1)}) custom-call(bf16[128,1024]{1,0:T(8,128)(2,1)} %refs_0_.3, bf16[128,1024]{1,0:T(8,128)(2,1)} %refs_1_.1, bf16[128,1024]{1,0:T(8,128)(2,1)} %refs_2_.2, bf16[16,128]{1,0:T(8,128)(2,1)} %scatter.4.refs_3_), custom_call_target="tpu_custom_call" | custom-call | tf_op jit(solution)/shard_map/gather_first/pallas_call | solution.py:496
  42.1 6.1 %convert_bitcast_fusion.5.refs_3_ = bf16[1024,1024]{1,0:T(8,128)(2,1)} fusion(bf16[1024,1024]{1,0:T(8,128)(2,1)} %param.22, bf16[3,1024,1024]{2,1,0:T(8,128)(2,1)} %get-tuple-element.61), kind=kOutput, calls=%fused_computation.51 | convolution fusion | flops 2148532224 | bytes 6291456 | tf_op jit(solution)/shard_map/dot_general | solution.py:24
  48.2 3.7 convert_bitcast_fusion.6.refs_2_
  51.9 3.7 fusion.67.refs_1_
  55.6 52.6 %self_forward.1 = (bf16[1024,1024]{1,0:T(8,128)(2,1)}, f32[8,8,1024]{2,1,0:T(8,128)}, bf16[5,1024,1024]{2,1,0:T(8,128)(2,1)}) custom-call(s32[1,2]{1,0:T(1,128)} %refs_0_.5, bf16[1024,1024]{1,0:T(8,128)(2,1)} %fusion.67.refs_1_, bf16[1024,1024]{1,0:T(8,128)(2,1)} %convert_bitcast_fusion.6.refs_2_, bf16[1024,1024]{1,0:T(8,128)(2,1)} %convert_bitcast_fusion.5.refs_3_, ...), custom_call_target="tpu_custom_call" | custom-call | tf_op jit(solution)/shard_map/self_forward/pallas_call | solution.py:496
  108.2 3.1 fusion.85.refs_2_
  111.3 3.2 fusion.88.refs_1_
  114.5 4.0 fusion.105
  120.6 4.8 multiply_convert_fusion
  127.9 44.0 %cross_forward.1 = (bf16[1024,1024]{1,0:T(8,128)(2,1)}, f32[8,8,1024]{2,1,0:T(8,128)}, bf16[4,1024,1024]{2,1,0:T(8,128)(2,1)}) custom-call(bf16[1024,1024]{1,0:T(8,128)(2,1)} %copy.61.refs_0_, bf16[256,1024]{1,0:T(8,128)(2,1)} %fusion.88.refs_1_, bf16[256,1024]{1,0:T(8,128)(2,1)} %fusion.85.refs_2_, bf16[128,4096]{1,0:T(8,128)(2,1)} %refs_3_.1), custom_call_target="tpu_custom_call" | custom-call | tf_op jit(solution)/shard_map/cross_forward/pallas_call | solution.py:496
  172.0 4.8 fusion.106
  180.5 7.0 %fusion.103 = (bf16[1024,1024]{1,0:T(8,128)(2,1)}, f32[1024,1024]{1,0:T(8,128)}, f32[1024,1024]{1,0:T(8,128)}) fusion(f32[1024]{0:T(1024)S(1)} %bitcast.191, f32[1024]{0:T(1024)S(1)} %bitcast.192, f32[1024]{0:T(1024)S(1)} %add_rsqrt_fusion, f32[1024,1024]{1,0:T(8,128)} %copy-done.4, f32[1024]{0:T(1024)S(1)} %broadcast_multiply_fusion.2), kind=kLoop, calls=%fused_computation.123 | loop fusion | flops 5242880 | bytes 14696448 | tf_op jit(solution)/shard_map/convert_element_type | solution.py:857
  187.5 66.1 %ffn_forward.1 = (bf16[1024,1024]{1,0:T(8,128)(2,1)}, bf16[1024,1024]{1,0:T(8,128)(2,1)}, f32[1024,1024]{1,0:T(8,128)}, bf16[1024,4096]{1,0:T(8,128)(2,1)}, bf16...) custom-call(bf16[1024,1024]{1,0:T(8,128)(2,1)} %get-tuple-element.95.refs_0_, ...), custom_call_target="tpu_custom_call" | custom-call | tf_op jit(solution)/shard_map/ffn_forward/pallas_call | solution.py:496
  254.4 53.8 %ffn_backward.1 = (bf16[4,1024,1024]{2,1,0:T(8,128)(2,1)}, bf16[8,4,128,1024]{3,2,1,0:T(8,128)(2,1)}, f32[1024,1024]{1,0:T(8,128)}, bf16[1024,1024]{1,0:T(8,128)(2,1)}, f32[8,1024]{1,0:T(8,128)}) custom-call(bf16[1024,1024]{1,0:T(8,128)(2,1)} %get-tuple-element.95.refs_0_, bf16[1024,1024]{1,0:T(8,128)(2,1)} %get-tuple-element.68.refs_1_, ...), custom_call_target="tpu_custom_call" | custom-call | tf_op jit(solution)/shard_map/ffn_backward/pallas_call | solution.py:496
  308.9 5.5 convolution_convert_fusion.1.refs_11_
  314.4 5.3 fusion.44.refs_3_
  319.8 52.8 %cross_backward.1 = (bf16[1024,1024]{1,0:T(8,128)(2,1)}, bf16[256,1024]{1,0:T(8,128)(2,1)}, bf16[256,1024]{1,0:T(8,128)(2,1)}, bf16[4,128,1024]{2,1,0:T(8,128)(2,1)}) custom-call(bf16[1024,1024]{1,0:T(8,128)(2,1)} %copy.61.refs_0_, bf16[256,1024]{1,0:T(8,128)(2,1)} %fusion.88.refs_1_, bf16[256,1024]{1,0:T(8,128)(2,1)} %fusion.85.refs_2_, ...), custom_call_target="tpu_custom_call" | custom-call | tf_op jit(solution)/shard_map/cross_backward/pallas_call | solution.py:496
  372.6 8.6 %multiply_reduce_fusion = (f32[1024]{0:T(1024)S(1)}, f32[1024]{0:T(1024)S(1)}, f32[1024]{0:T(1024)S(1)}, f32[1024]{0:T(1024)S(1)}, f32[1024,1024]{1,0:T(8,128)}) fusion(f32[1024,1024]{1,0:T(8,128)S(1)} %copy-done.3, f32[1024]{0:T(1024)S(1)} %add_rsqrt_fusion.1, f32[1024]{0:T(1024)S(1)} %broadcast_multiply_fusion.3, f32[1024]{0:T(1024)S(1)} %bitcast.188, ...), kind=kOutput, calls=%fused_computation | convolution fusion | flops 2159013888 | bytes 16805888 | tf_op jit(solution)/shard_map/dot_general | solution.py:24
  381.2 4.1 convolution_convert_fusion.2.refs_8_
  386.0 4.6 subtract_multiply_fusion
  394.6 3.3 fusion.76
  398.0 5.3 fusion.41.refs_4_
  407.5 97.7 %self_backward.1 = (bf16[1024,1024]{1,0:T(8,128)(2,1)}, bf16[1024,1024]{1,0:T(8,128)(2,1)}, bf16[1024,1024]{1,0:T(8,128)(2,1)}, bf16[8,128,1024]{2,1,0:T(8,128)(2,1)}) custom-call(s32[1,2]{1,0:T(1,128)} %refs_0_.5, bf16[1024,1024]{1,0:T(8,128)(2,1)} %fusion.67.refs_1_, bf16[1024,1024]{1,0:T(8,128)(2,1)} %convert_bitcast_fusion.6.refs_2_, ...), custom_call_target="tpu_custom_call" | custom-call | tf_op jit(solution)/shard_map/self_backward/pallas_call | solution.py:496
  505.2 5.5 convolution_convert_fusion.refs_3_
  514.7 3.7 convert_bitcast_fusion.2.refs_0_
  518.4 3.7 convert_bitcast_fusion.1.refs_1_
  522.1 6.1 %fusion.25 = f32[1024,1024]{1,0:T(8,128)} fusion(bf16[1024,1024]{1,0:T(8,128)(2,1)S(1)} %copy-done.19, bf16[3,1024,1024]{2,1,0:T(8,128)(2,1)} %get-tuple-element.61), kind=kOutput, calls=%fused_computation.39 | convolution fusion | flops 2147483648 | bytes 8388608 | tf_op jit(solution)/shard_map/dot_general | solution.py:24
  528.3 3.8 convert_bitcast_fusion.refs_2_
  532.0 49.0 %scatter_last.1 = (bf16[4,128,1024]{2,1,0:T(8,128)(2,1)}, f32[8,128]{1,0:T(8,128)}) custom-call(bf16[1024,1024]{1,0:T(8,128)(2,1)} %convert_bitcast_fusion.2.refs_0_, bf16[1024,1024]{1,0:T(8,128)(2,1)} %convert_bitcast_fusion.1.refs_1_, bf16[1024,1024]{1,0:T(8,128)(2,1)} %convert_bitcast_fusion.refs_2_, bf16[1024,1024]{1,0:T(8,128)(2,1)} %convolution_convert_fusion.refs_3_, ...), custom_call_target="tpu_custom_call" | custom-call | tf_op jit(solution)/shard_map/scatter_last/pallas_call | solution.py:496
  582.5 2.6 bitcast_convert_fusion.5
  585.1 4.2 fusion.21
  589.3 6.5 %add_add_fusion = f32[1024,1024]{1,0:T(8,128)} fusion(f32[1024,1024]{1,0:T(8,128)S(1)} %fusion.21, f32[1024,1024]{1,0:T(8,128)S(1)} %copy-done.5, f32[1024,1024]{1,0:T(8,128)S(1)} %subtract_multiply_fusion, bf16[3,1024,1024]{2,1,0:T(8,128)(2,1)} %get-tuple-element.61, bf16[1024,1024]{1,0:T(8,128)(2,1)S(1)} %copy-done.9), kind=kOutput, calls=%fused_computation.1 | convolution fusion | flops 2151677952 | bytes 20971520 | tf_op jit(solution)/shard_map/dot_general | solution.py:24
  (75 shorter events, 28.4 us)
Async XLA Ops:
  0.7 107.5 %copy-start = (bf16[256,1024]{1,0:T(8,128)(2,1)S(1)}, bf16[256,1024]{1,0:T(8,128)(2,1)}, u32[]{:S(2)}) copy-start(bf16[256,1024]{1,0:T(8,128)(2,1)} %param.23) | copy-start | bytes 1572868
  40.6 7.6 %slice-start = ((s8[6291456]{0:T(1024)(128)(4,1)}), s8[4194304]{0:T(1024)(128)(4,1)S(1)}, s32[]{:S(2)}) async-start(s8[6291456]{0:T(1024)(128)(4,1)} %bitcast.183), calls=%async_computation | async-start | bytes 8388608
  42.1 6.1 %slice-start.1 = ((s8[6291456]{0:T(1024)(128)(4,1)}), s8[2097152]{0:T(1024)(128)(4,1)S(1)}, s32[]{:S(2)}) async-start(s8[6291456]{0:T(1024)(128)(4,1)} %bitcast.183), calls=%async_computation.1 | async-start | bytes 4194304
  42.1 6.1 %copy-start.15 = (bf16[1024,1024]{1,0:T(8,128)(2,1)S(1)}, bf16[1024,1024]{1,0:T(8,128)(2,1)}, u32[]{:S(2)}) copy-start(bf16[1024,1024]{1,0:T(8,128)(2,1)} %param.22) | copy-start | bytes 6291460
  111.3 3.2 copy-start.6
  118.5 2.0 copy-start.1
  127.9 44.1 %copy-start.2 = (f32[1024,1024]{1,0:T(8,128)S(1)}, f32[1024,1024]{1,0:T(8,128)}, u32[]{:S(2)}) copy-start(f32[1024,1024]{1,0:T(8,128)} %copy-done.1) | copy-start | bytes 12582916
  176.8 2.1 copy-start.4
  254.4 54.5 %copy-start.7 = (bf16[1024,1024]{1,0:T(8,128)(2,1)S(1)}, bf16[1024,1024]{1,0:T(8,128)(2,1)}, u32[]{:S(2)}) copy-start(bf16[1024,1024]{1,0:T(8,128)(2,1)} %get-tuple-element.65.refs_4_) | copy-start | bytes 6291460
  308.9 5.5 copy-start.21
  319.8 52.8 %copy-start.3 = (f32[1024,1024]{1,0:T(8,128)S(1)}, f32[1024,1024]{1,0:T(8,128)}, u32[]{:S(2)}) copy-start(f32[1024,1024]{1,0:T(8,128)} %copy-done.1) | copy-start | bytes 12582916
  372.6 8.6 %copy-start.20 = (bf16[1024,1024]{1,0:T(8,128)(2,1)S(1)}, bf16[1024,1024]{1,0:T(8,128)(2,1)}, u32[]{:S(2)}) copy-start(bf16[1024,1024]{1,0:T(8,128)(2,1)} %get-tuple-element.77) | copy-start | bytes 6291460
  386.0 4.6 copy-start.13
  390.6 1.6 copy-start.14
  392.2 2.4 copy-start.12
  505.2 5.5 copy-start.11
  510.7 3.0 copy-start.16
  512.2 2.5 copy-start.8
  514.7 3.7 copy-start.19
  522.1 6.1 %copy-start.17 = (bf16[1024,1024]{1,0:T(8,128)(2,1)S(1)}, bf16[1024,1024]{1,0:T(8,128)(2,1)}, u32[]{:S(2)}) copy-start(bf16[1024,1024]{1,0:T(8,128)(2,1)} %get-tuple-element.84) | copy-start | bytes 6291460
  581.1 4.0 copy-start.18
  585.1 4.2 copy-start.5
  585.1 4.2 copy-start.9
  589.3 6.6 %copy-start.10 = (bf16[1024,1024]{1,0:T(8,128)(2,1)S(1)}, bf16[1024,1024]{1,0:T(8,128)(2,1)}, u32[]{:S(2)}) copy-start(bf16[1024,1024]{1,0:T(8,128)(2,1)} %get-tuple-element.148) | copy-start | bytes 6291460

commit v3 on v2

--- a/solution.py
+++ b/solution.py
@@ -80,7 +80,7 @@
 
 class Gather:
     def __init__(self, n, width, shards, units, alone, owner_first=False, vec=None):
-        self.n, self.shards, self.owner_first, self.vec = n, shards, owner_first, vec
+        self.n, self.shards, self.owner_first, self.vec, self.follows = n, shards, owner_first, vec, False
         self.units, self.ne, self.ns = units, alone, units - 2 * alone
         self.rows, self.width = sum(s.size for s in shards) // (units * width), width
         self.arrays = list(shards) + ([] if vec is None else [vec])
@@ -155,7 +155,8 @@
                 pltpu.make_async_copy(part, self.own.at[i * per + j], self.local.at[0]).start()
         if self.vec is not None:
             pltpu.make_async_copy(self.vec_in, self.vecs.at[self.shard], self.vec_sems[0].at[0]).start()
-        greet((self.ways[0][0], self.ways[1][0], self.sibling, self.across))
+        if not self.follows:
+            greet((self.ways[0][0], self.ways[1][0], self.sibling, self.across))
         pltpu.make_async_copy(self.own, self.own, self.local.at[0]).wait()
         for e in range(2):
             for d in range(2):
@@ -220,10 +221,32 @@
         self.stored().wait()
 
 
+class Chain:
+    def __init__(self, first, second):
+        self.first, self.second, self.n = first, second, first.n
+        second.follows = True
+        self.arrays = first.arrays + second.arrays
+        self.out_shapes = first.out_shapes + second.out_shapes
+        self.scratch = first.scratch + second.scratch
+
+    def bind(self, ins, outs, scratch):
+        a, b, c = len(self.first.arrays), len(self.first.out_shapes), len(self.first.scratch)
+        self.first.bind(ins[:a], outs[:b], scratch[:c])
+        self.second.bind(ins[a:], outs[b:], scratch[c:])
+
+    def step(self, t):
+        self.first.step(t)
+        pl.when(t == self.n)(lambda: self.first.finish(self.n + 1))
+        self.second.step(t - (self.n - 2))
+
+    def finish(self, ticks):
+        self.second.finish(ticks - (self.n - 2))
+
+
 class Scatter:
-    def __init__(self, n, sources, alone, vec=None):
+    def __init__(self, n, sources, alone, vec=None, start=1, every=1):
         self.n, self.arrays = n, list(sources) + ([] if vec is None else [vec])
-        self.vec = vec
+        self.vec, self.start, self.every = vec, start, every
         self.counts = [1 if s.ndim == 2 else s.shape[s.ndim - 3] for s in sources]
         self.kinds = [s.ndim for s in sources]
         units = self.units = sum(self.counts)
@@ -332,8 +355,6 @@
         lax.fori_loop(0, n, sends, 0)
         if self.vec is not None:
             pltpu.make_async_copy(self.v_near, self.v_near, self.v_local.at[0]).wait()
-        self.pair(0)
-        self.pair(1)
 
     def arrived(self, ref, ssem, rsem, d, k):
         here = self.region(ref, d, k)
@@ -393,61 +414,96 @@
             def _():
                 self.vec_hop(k).start()
 
-    def step(self, i):
-        pl.when(i == 0)(self.begin)
-
-        @pl.when(i == 0)
+    def step(self, t):
+        n = self.n
+        pl.when(t == 0)(self.begin)
+        since = t - self.start
+        if self.every > 1:
+            k, on = (since + n * self.every) // self.every - n, lax.rem(since + n * self.every, self.every) == 0
+        else:
+            k, on = since, since >= 0
+
+        @pl.when(since == 0)
         def _():
-            self.combine(i, False)
-
-        @pl.when((i > 0) & (i < self.n))
+            self.pair(0)
+            self.pair(1)
+            self.combine(0, False)
+
+        @pl.when(on & (k > 0) & (k < n))
         def _():
-            self.combine(i, True)
-
-        @pl.when(i + 2 < self.n)
+            self.combine(k, True)
+
+        @pl.when(on & (k >= 0) & (k + 2 < n))
         def _():
-            self.pair(i + 2)
-
-    def finish(self, steps):
+            self.pair(k + 2)
+
+        pl.when(since == (n - 1) * self.every)(self.exchange)
+        pl.when(since == (n - 1) * self.every + max(2, self.every))(self.join)
+
+    def swap(self, e):
+        src = self.near.at[self.sets[e], block_of(self.shard, self.rows // 2), :]
+        return remote(src, (self.swap_e, self.swap_s)[e], self.ss.at[e], self.sr.at[e], self.across)
+
+    def result(self, j, away):
+        half = block_of(self.c, self.rows // 2)
+        src = (self.near.at[self.mine, block_of(self.shard, self.rows // 2), :], self.swap_s, self.swap_e)[j]
+        dst = self.out.at[(self.mine, self.shared, self.theirs)[j], half, :]
+        if away:
+            return remote(src, dst, self.os.at[j], self.orr.at[j], self.sibling)
+        return pltpu.make_async_copy(src, dst, self.done.at[j])
+
+    def shares(self):
+        sums, rep = self.v_near.at[self.shard], self.x * 2 + self.c
+        return [
+            remote(sums, self.v_all.at[rep], self.v_ss.at[j], self.v_sr.at[j], who)
+            for j, who in enumerate((self.sibling, self.across, self.corner))
+        ]
+
+    def put(self, j):
+        self.result(j, True).start()
+        self.result(j, False).start()
+
+    def exchange(self):
+        self.swap(1).start()
+        self.swap(0).start()
+        self.put(0)
+        if self.vec is not None:
+            for copy in self.shares():
+                copy.start()
+            self.v_all[self.x * 2 + self.c] = self.v_near[self.shard]
+
+    def join(self):
+        at = block_of(self.shard, self.rows // 2)
+        self.swap(1).wait_recv()
+
+        def add(i, _):
+            self.swap_s[i] = self.swap_s[i] + self.near[self.ne + i, at, :]
+            return 0
+
+        lax.fori_loop(0, self.ns, add, 0)
+        self.put(1)
+        self.swap(0).wait_recv()
+        self.put(2)
+
+    def finish(self, ticks):
         n = self.n
-        at = block_of(self.shard, self.rows // 2)
-        half = block_of(self.c, self.rows // 2)
-        near, out = self.near, self.out
-        swap = send(near.at[self.shared, at, :], self.swap_s, self.ss.at[0], self.sr.at[0], self.across)
-        give = send(near.at[self.mine, at, :], self.swap_e, self.ss.at[1], self.sr.at[1], self.across)
-        final = [send(near.at[self.mine, at, :], out.at[self.mine, half, :], self.os.at[0], self.orr.at[0], self.sibling)]
-        keep = [load(near.at[self.mine, at, :], out.at[self.mine, half, :], self.done.at[0])]
+        last = self.start + (n - 1) * self.every
+        assert ticks > last - self.every
+        if ticks <= last:
+            self.combine(n - 1, True)
+            self.exchange()
+        if ticks <= last + max(2, self.every):
+            self.join()
         if self.vec is not None:
-            sums = self.v_near.at[self.shard]
-            rep = self.x * 2 + self.c
-            shares = [
-                send(sums, self.v_all.at[rep], self.v_ss.at[j], self.v_sr.at[j], who)
-                for j, who in enumerate((self.sibling, self.across, self.corner))
-            ]
-            self.v_all[rep] = sums[...]
-        swap.wait_recv()
-
-        def join(i, _):
-            self.swap_s[i] = (self.swap_s[i].astype(f32) + near[self.ne + i, at, :].astype(f32)).astype(bf16)
-            return 0
-
-        lax.fori_loop(0, self.ns, join, 0)
-        final.append(send(self.swap_s, out.at[self.shared, half, :], self.os.at[1], self.orr.at[1], self.sibling))
-        keep.append(load(self.swap_s, out.at[self.shared, half, :], self.done.at[1]))
-        give.wait_recv()
-        final.append(send(self.swap_e, out.at[self.theirs, half, :], self.os.at[2], self.orr.at[2], self.sibling))
-        keep.append(load(self.swap_e, out.at[self.theirs, half, :], self.done.at[2]))
-        if self.vec is not None:
-            for copy in shares:
+            for copy in self.shares():
                 copy.wait()
             self.v_sum[...] = (self.v_all[0] + self.v_all[1]) + (self.v_all[2] + self.v_all[3])
-            keep.append(load(self.v_sum, self.vec_out, self.v_local.at[1]))
-        for copy in keep:
-            copy.wait()
-        for copy in final:
-            copy.wait()
-        swap.wait_send()
-        give.wait_send()
+            load(self.v_sum, self.vec_out, self.v_local.at[1]).wait()
+        for j in range(3):
+            self.result(j, False).wait()
+            self.result(j, True).wait()
+        for e in range(2):
+            self.swap(e).wait_send()
 
         def drain(k, _):
             for d in range(2):
@@ -468,7 +524,9 @@
         lax.fori_loop(0, n - 1, drain_ring, 0)
 
 
-def hosted(kernel, steps, args, in_specs, out_shapes, out_specs, scratch, name, carry=None, collective_id=None, done_by=None, vmem=58):
+def hosted(
+    kernel, steps, args, in_specs, out_shapes, out_specs, scratch, name, carry=None, collective_id=None, done_by=None, ticks=1, vmem=58
+):
     counts = [len(args), len(out_shapes), len(scratch)]
     extra = [0, 0, 0]
     params = dict(vmem_limit_bytes=vmem * MIB)
@@ -483,15 +541,23 @@
             other.append(refs[first + count : first + count + more])
             first += count + more
         i = pl.program_id(0)
+
+        def tick(j):
+            if carry is not None:
+                carry.step(i * ticks + j)
+
         if carry is not None:
             carry.bind(*other)
-            carry.step(i)
+        if ticks == 1:
+            tick(0)
             if done_by is not None:
                 pl.when(i == done_by)(lambda: carry.finish(done_by + 1))
-        if kernel is not None:
-            kernel(*main)
+            if kernel is not None:
+                kernel(*main)
+        else:
+            kernel(tick, *main)
         if carry is not None and done_by is None:
-            pl.when(i == steps - 1)(lambda: carry.finish(steps))
+            pl.when(i == steps - 1)(lambda: carry.finish(steps * ticks))
 
     return pl.pallas_call(
         whole,
@@ -505,6 +571,34 @@
     )(*args, *(carry.arrays if carry else []))
 
 
+def norm_forward(resid, gain, shift):
+    mean = jnp.mean(resid, -1, keepdims=True)
+    centred = resid - mean
+    variance = jnp.mean(centred * centred, -1, keepdims=True)
+    inverse = lax.rsqrt(variance + EPS)
+    normed = centred * inverse
+    return (normed * gain + shift, normed, inverse)
+
+
+def norm_backward(grad_out, normed, inverse, gain):
+    grad_gain = jnp.sum(grad_out * normed, 0, keepdims=True)
+    grad_shift = jnp.sum(grad_out, 0, keepdims=True)
+    grad_normed = grad_out * gain
+    centre_term = jnp.mean(grad_normed, -1, keepdims=True)
+    slope_term = jnp.mean(grad_normed * normed, -1, keepdims=True)
+    return (inverse * (grad_normed - centre_term - normed * slope_term), grad_gain, grad_shift)
+
+
+def fixed(a):
+    zeros = (0,) * a.ndim
+    return pl.BlockSpec(a.shape, lambda i: zeros, pipeline_mode=pl.Buffered(1))
+
+
+def slices(rows, count):
+    size = rows // count
+    return [slice(j * size, (j + 1) * size) for j in range(count)]
+
+
 def first_lanes(shape):
     return lax.broadcasted_iota(jnp.int32, shape, len(shape) - 1) < HD
 
@@ -520,169 +614,329 @@
     return jnp.where((k_at <= q_at) | (q_in & k_in), 0.0, NEGATIVE)
 
 
-def attend_forward_kernel(regions, starts_ref, q_ref, k_ref, v_ref, o_ref, lse_ref, bias_ref):
-    rows = q_ref.shape[0]
-    size = rows // regions
-
-    if starts_ref is not None:
-        @pl.when(pl.program_id(0) == 0)
+def self_forward_kernel(regions, lead, scale, carry, starts_ref, x_ref, *refs):
+    refs = list(refs)
+    w_ref = refs.pop(0) if carry is None else carry.first.full
+    q_ref, k_ref, v_ref, o_ref, lse_ref, bias_ref, w_buf, sems = refs
+    rows, size = x_ref.shape[0], x_ref.shape[0] // regions
+    i = pl.program_id(0)
+    j = i - lead
+    pairs = pl.num_programs(0) - lead
+
+    @pl.when(i == 0)
+    def _():
+        for r in range(regions):
+            bias_ref[r] = region_bias(starts_ref, r, size, False)
+
+    def fetch(pair, slot):
+        return pltpu.make_async_copy(w_ref.at[:, :, block_of(pair, 2 * HD)], w_buf.at[slot], sems.at[slot])
+
+    @pl.when(j == 0)
+    def _():
+        fetch(0, 0).start()
+
+    @pl.when(j >= 0)
+    def _():
+        slot = lax.rem(i - lead + 2, 2)
+
+        @pl.when(j + 1 < pairs)
         def _():
+            fetch(j + 1, 1 - slot).start()
+
+        fetch(j, slot).wait()
+        made = dot(x_ref[...], jnp.concatenate([w_buf[slot, u] for u in range(3)], 1))
+        q_ref[...] = (made[:, : 2 * HD] * scale).astype(bf16)
+        k_ref[...] = made[:, 2 * HD : 4 * HD].astype(bf16)
+        v_ref[...] = made[:, 4 * HD :].astype(bf16)
+        low = first_lanes((1, 2 * HD))
+        outs, lses = [[], []], [[], []]
+        for h in range(2):
+            keys = jnp.where(low if h == 0 else ~low, k_ref[...], jnp.zeros((), bf16))
             for r in range(regions):
-                bias_ref[r] = region_bias(starts_ref, r, size, False)
-
-    low = first_lanes((1, 2 * HD))
-    outs, lses = [[], []], [[], []]
-    for h in range(2):
-        pick = low if h == 0 else ~low
-        keys = jnp.where(pick, k_ref[...], jnp.zeros((), bf16))
-        for r in range(regions):
-            span = slice(r * size, (r + 1) * size)
-            q = q_ref[span, :]
-            scores = []
-            if starts_ref is None:
-                scores.append((dot(q, keys, 1, 1), v_ref[...]))
-            else:
+                span = slice(r * size, (r + 1) * size)
+                q = q_ref[span, :]
+                scores = []
                 if r:
                     scores.append((dot(q, keys[: r * size], 1, 1), v_ref[: r * size, :]))
                 scores.append((dot(q, keys[span], 1, 1) + bias_ref[r], v_ref[span, :]))
-            top = functools.reduce(jnp.maximum, [jnp.max(s, -1, keepdims=True) for s, _ in scores])
-            total, mixed = 0.0, 0.0
-            for s, v in scores:
-                e = jnp.exp(s - top)
-                total = total + jnp.sum(e, -1, keepdims=True)
-                mixed = mixed + dot(e.astype(bf16), v)
-            outs[h].append(mixed / total)
-            lses[h].append(top + jnp.log(total))
-    for r in range(regions):
-        span = slice(r * size, (r + 1) * size)
-        o_ref[span, :] = jnp.where(low, outs[0][r], outs[1][r]).astype(bf16)
-        turned = jnp.where(low, lses[0][r], lses[1][r]).T
-        lse_ref[0, 0:1, span] = turned[0:1]
-        lse_ref[0, 1:2, span] = turned[HD : HD + 1]
-
-
-def attend_parts(kernel, regions_of, starts, arrays, rows):
-    tall = [pl.BlockSpec((a.shape[0], 2 * HD), lambda i: (0, i)) if a.ndim == 2 else pl.BlockSpec((1, 8, rows), lambda i: (i, 0, 0)) for a in arrays]
-    if starts is None:
-        return lambda *refs: kernel(regions_of, None, *refs, None), list(arrays), tall, []
-    size = rows // regions_of
-    scratch = [pltpu.VMEM((regions_of, size, size), f32)]
-    return functools.partial(kernel, regions_of), [starts, *arrays], [pl.BlockSpec(memory_space=pltpu.SMEM), *tall], scratch
-
-
-def attend_forward(q, k, v, starts, carry, collective_id):
-    rows, width = q.shape
-    pairs = width // (2 * HD)
-    kernel, args, specs, scratch = attend_parts(
-        attend_forward_kernel, 2 if starts is None else starts.shape[1], starts, (q, k, v), rows
-    )
-    return hosted(
-        kernel, pairs, args, specs,
-        [jax.ShapeDtypeStruct((rows, width), bf16), jax.ShapeDtypeStruct((pairs, 8, rows), f32)],
-        [pl.BlockSpec((rows, 2 * HD), lambda i: (0, i)), pl.BlockSpec((1, 8, rows), lambda i: (i, 0, 0))],
-        scratch, "self_forward" if starts is not None else "cross_forward", carry, collective_id,
-    )
-
-
-def attend_backward_kernel(
-    regions, starts_ref, q_ref, k_ref, v_ref, g_ref, o_ref, lse_ref, gq_ref, gk_ref, gv_ref, bias_ref
-):
-    rows = q_ref.shape[0]
-    size = rows // regions
-
-    if starts_ref is not None:
-        @pl.when(pl.program_id(0) == 0)
-        def _():
-            for r in range(regions):
-                bias_ref[r] = region_bias(starts_ref, r, size, True)
-
-    low = first_lanes((1, 2 * HD))
-    product = g_ref[...].astype(f32) * o_ref[...].astype(f32)
-    chooser = lax.broadcasted_iota(jnp.int32, (8, 2 * HD), 0)
-    chooser = ((chooser == 0) & first_lanes((8, 2 * HD))) | ((chooser == 1) & ~first_lanes((8, 2 * HD)))
-    chooser = chooser.astype(f32).astype(bf16)
-    upper = product.astype(bf16)
-    lower = (product - upper.astype(f32)).astype(bf16)
-    deltas = dot(chooser, upper, 1, 1) + dot(chooser, lower, 1, 1)
-    gq, gk, gv = {}, {}, {}
-    key_spans = [slice(0, k_ref.shape[0])]
-    if starts_ref is not None:
-        key_spans = [slice(r * size, (r + 1) * size) for r in range(regions)]
-    for h in range(2):
-        pick = low if h == 0 else ~low
-        zero = jnp.zeros((), bf16)
-        keys = jnp.where(pick, k_ref[...], zero)
-        values = jnp.where(pick, v_ref[...], zero)
+                top = functools.reduce(jnp.maximum, [jnp.max(s, -1, keepdims=True) for s, _ in scores])
+                total, mixed = 0.0, 0.0
+                for s, v in scores:
+                    e = jnp.exp(s - top)
+                    total = total + jnp.sum(e, -1, keepdims=True)
+                    mixed = mixed + dot(e.astype(bf16), v)
+                outs[h].append(mixed / total)
+                lses[h].append(top + jnp.log(total))
         for r in range(regions):
             span = slice(r * size, (r + 1) * size)
-            q, g = q_ref[span, :], g_ref[span, :]
-            lse = lse_ref[0, h : h + 1, span]
-            delta = deltas[h : h + 1, span]
-            for j, keyed in enumerate(key_spans):
-                if starts_ref is not None and j > r:
-                    continue
-                scores = dot(keys[keyed], q, 1, 1)
-                if starts_ref is not None and j == r:
-                    scores = scores + bias_ref[r]
-                probs = jnp.exp(scores - lse)
-                grad_probs = dot(values[keyed], g, 1, 1)
-                grad_scores = (probs * (grad_probs - delta)).astype(bf16)
-                gv[h, j] = gv.get((h, j), 0.0) + dot(probs.astype(bf16), g)
-                gk[h, j] = gk.get((h, j), 0.0) + dot(grad_scores, q)
-                gq[h, r] = gq.get((h, r), 0.0) + dot(grad_scores, k_ref[keyed, :], 0, 0)
-    for r in range(regions):
-        span = slice(r * size, (r + 1) * size)
-        gq_ref[span, :] = jnp.where(low, gq[0, r], gq[1, r]).astype(bf16)
-    for j, keyed in enumerate(key_spans):
-        gk_ref[keyed, :] = jnp.where(low, gk[0, j], gk[1, j]).astype(bf16)
-        gv_ref[keyed, :] = jnp.where(low, gv[0, j], gv[1, j]).astype(bf16)
-
-
-def attend_backward(q, k, v, g, o, lse, starts, carry, collective_id):
+            o_ref[span, :] = jnp.where(low, outs[0][r], outs[1][r]).astype(bf16)
+            turned = jnp.where(low, lses[0][r], lses[1][r]).T
+            lse_ref[0, 0:1, span] = turned[0:1]
+            lse_ref[0, 1:2, span] = turned[HD : HD + 1]
+
+
+def self_forward(states, weights, starts, scale, carry, collective_id):
+    rows, width = states.shape
+    regions = starts.shape[1]
+    size = rows // regions
+    pairs = width // (2 * HD)
+    lead = 0 if carry is None else carry.n
+    args, specs = [starts, states], [pl.BlockSpec(memory_space=pltpu.SMEM), fixed(states)]
+    if carry is None:
+        args.append(weights)
+        specs.append(HBM)
+    column = pl.BlockSpec((rows, 2 * HD), lambda i: (0, jnp.maximum(i - lead, 0)))
+    return hosted(
+        functools.partial(self_forward_kernel, regions, lead, scale, carry), lead + pairs, args, specs,
+        [jax.ShapeDtypeStruct((rows, width), bf16)] * 4 + [jax.ShapeDtypeStruct((pairs, 8, rows), f32)],
+        [column] * 4 + [pl.BlockSpec((1, 8, rows), lambda i: (jnp.maximum(i - lead, 0), 0, 0))],
+        [pltpu.VMEM((regions, size, size), f32), pltpu.VMEM((2, 3, width, 2 * HD), bf16), pltpu.SemaphoreType.DMA((2,))],
+        "self_forward", carry, collective_id,
+    )
+
+
+def self_backward_kernel(
+    regions, scale, pairs, starts_ref, q_ref, k_ref, v_ref, g_ref, o_ref, lse_ref, x_ref, w_ref, resid_ref,
+    g_query_ref, g_key_ref, g_value_ref, grad_ref, bias_ref, grads,
+):
+    rows, width = x_ref.shape
+    size = rows // regions
+    i = pl.program_id(0)
+    spans = slices(rows, regions)
+    low = first_lanes((1, 2 * HD))
+
+    @pl.when(i == 0)
+    def _():
+        for r in range(regions):
+            bias_ref[r] = region_bias(starts_ref, r, size, True)
+
+    @pl.when(i < pairs)
+    def _():
+        product = g_ref[...].astype(f32) * o_ref[...].astype(f32)
+        chooser = lax.broadcasted_iota(jnp.int32, (8, 2 * HD), 0)
+        chooser = ((chooser == 0) & first_lanes((8, 2 * HD))) | ((chooser == 1) & ~first_lanes((8, 2 * HD)))
+        chooser = chooser.astype(f32).astype(bf16)
+        upper = product.astype(bf16)
+        lower = (product - upper.astype(f32)).astype(bf16)
+        deltas = dot(chooser, upper, 1, 1) + dot(chooser, lower, 1, 1)
+        gq, gk, gv = {}, {}, {}
+        for h in range(2):
+            pick = low if h == 0 else ~low
+            zero = jnp.zeros((), bf16)
+            keys = jnp.where(pick, k_ref[...], zero)
+            values = jnp.where(pick, v_ref[...], zero)
+            for r, span in enumerate(spans):
+                q, g = q_ref[span, :], g_ref[span, :]
+                lse = lse_ref[0, h : h + 1, span]
+                delta = deltas[h : h + 1, span]
+                for j, keyed in enumerate(spans[: r + 1]):
+                    scores = dot(keys[keyed], q, 1, 1)
+                    if j == r:
+                        scores = scores + bias_ref[r]
+                    probs = jnp.exp(scores - lse)
+                    grad_probs = dot(values[keyed], g, 1, 1)
+                    grad_scores = (probs * (grad_probs - delta)).astype(bf16)
+                    gv[h, j] = gv.get((h, j), 0.0) + dot(probs.astype(bf16), g)
+                    gk[h, j] = gk.get((h, j), 0.0) + dot(grad_scores, q)
+                    gq[h, r] = gq.get((h, r), 0.0) + dot(grad_scores, k_ref[keyed, :], 0, 0)
+        cols = block_of(i, 2 * HD)
+        for r, span in enumerate(spans):
+            grads[0, span, cols] = jnp.where(low, gq[0, r], gq[1, r]).astype(bf16) * scale
+            grads[1, span, cols] = jnp.where(low, gk[0, r], gk[1, r]).astype(bf16)
+            grads[2, span, cols] = jnp.where(low, gv[0, r], gv[1, r]).astype(bf16)
+
+    for u, out in enumerate((g_query_ref, g_key_ref, g_value_ref)):
+
+        @pl.when(i == pairs + u)
+        def _():
+            for span in slices(width, 4):
+                out[span, :] = dot(x_ref[:, span], grads[u], 0, 0).astype(bf16)
+
+    @pl.when(i >= pairs + 3)
+    def _():
+        at = block_of(i - pairs - 3, grad_ref.shape[0])
+        total = resid_ref[...]
+        for u in range(3):
+            total = total + dot(grads[u, at, :], w_ref[u], 1, 1)
+        grad_ref[...] = total
+
+
+def self_backward(q, k, v, g, o, lse, starts, states, weights, resid, scale, carry, collective_id):
     rows, width = q.shape
-    kernel, args, specs, scratch = attend_parts(
-        attend_backward_kernel, 2 if starts is None else starts.shape[1], starts, (q, k, v, g, o, lse), rows
-    )
+    regions = starts.shape[1]
+    size = rows // regions
+    pairs, parts = width // (2 * HD), 4
+    last = pairs - 1
+    column = pl.BlockSpec((rows, 2 * HD), lambda i: (0, jnp.minimum(i, last)))
+    some = pl.BlockSpec((rows // parts, width), lambda i: (jnp.maximum(i - pairs - 3, 0), 0))
+    square = jax.ShapeDtypeStruct((width, width), bf16)
     return hosted(
-        kernel, width // (2 * HD), args, specs,
-        [jax.ShapeDtypeStruct(a.shape, bf16) for a in (q, k, v)],
-        [pl.BlockSpec((a.shape[0], 2 * HD), lambda i: (0, i)) for a in (q, k, v)],
-        scratch, "self_backward" if starts is not None else "cross_backward", carry, collective_id,
-    )
-
-
-def norm_forward(resid, gain, shift):
-    mean = jnp.mean(resid, -1, keepdims=True)
-    centred = resid - mean
-    variance = jnp.mean(centred * centred, -1, keepdims=True)
-    inverse = lax.rsqrt(variance + EPS)
-    normed = centred * inverse
-    return (normed * gain + shift, normed, inverse)
-
-
-def norm_backward(grad_out, normed, inverse, gain):
-    grad_gain = jnp.sum(grad_out * normed, 0, keepdims=True)
-    grad_shift = jnp.sum(grad_out, 0, keepdims=True)
-    grad_normed = grad_out * gain
-    centre_term = jnp.mean(grad_normed, -1, keepdims=True)
-    slope_term = jnp.mean(grad_normed * normed, -1, keepdims=True)
-    return (inverse * (grad_normed - centre_term - normed * slope_term), grad_gain, grad_shift)
-
-
-def fixed(a):
-    zeros = (0,) * a.ndim
-    return pl.BlockSpec(a.shape, lambda i: zeros, pipeline_mode=pl.Buffered(1))
-
-
-def slices(rows, count):
-    size = rows // count
-    return [slice(j * size, (j + 1) * size) for j in range(count)]
+        functools.partial(self_backward_kernel, regions, scale, pairs), pairs + 3 + parts,
+        [starts, q, k, v, g, o, lse, states, weights, resid],
+        [pl.BlockSpec(memory_space=pltpu.SMEM)] + [column] * 5
+        + [pl.BlockSpec((1, 8, rows), lambda i: (jnp.minimum(i, last), 0, 0)), fixed(states), fixed(weights), some],
+        [square] * 3 + [jax.ShapeDtypeStruct((rows, width), f32)], [fixed(square)] * 3 + [some],
+        [pltpu.VMEM((regions, size, size), f32), pltpu.VMEM((3, rows, width), bf16)],
+        "self_backward", carry, collective_id, vmem=60,
+    )
+
+
+def cross_forward_kernel(
+    scale, tick, x_ref, mixed_in, enc_ref, w_ref, vec_ref, low_ref, n1_ref, i1_ref, q_ref, k_ref, v_ref, mixed_ref,
+    lse_ref, two_ref, n2_ref, i2_ref, low_two_ref,
+):
+    tick(0)
+
+    @pl.when(pl.program_id(0) == 0)
+    def _():
+        k_ref[...] = dot(enc_ref[...], w_ref[2]).astype(bf16)
+        v_ref[...] = dot(enc_ref[...], w_ref[3]).astype(bf16)
+
+    one, n1_ref[...], i1_ref[...] = norm_forward(
+        x_ref[...].astype(f32) + dot(mixed_in[...], w_ref[0]), vec_ref[0:1, :], vec_ref[1:2, :]
+    )
+    low_ref[...] = one.astype(bf16)
+    q_ref[...] = (dot(low_ref[...], w_ref[1]) * scale).astype(bf16)
+    rows, width = x_ref.shape
+    low = first_lanes((1, 2 * HD))
+    lane = lax.broadcasted_iota(jnp.int32, (1, 2 * HD), 1)
+    lses = jnp.zeros((rows, 2 * HD), f32)
+    for pair in range(width // (2 * HD)):
+        if pair == 2:
+            tick(1)
+        cols = slice(pair * 2 * HD, (pair + 1) * 2 * HD)
+        parts = []
+        for h in range(2):
+            keys = jnp.where(low if h == 0 else ~low, k_ref[:, cols], jnp.zeros((), bf16))
+            scores = dot(q_ref[:, cols], keys, 1, 1)
+            top = jnp.max(scores, -1, keepdims=True)
+            e = jnp.exp(scores - top)
+            total = jnp.sum(e, -1, keepdims=True)
+            parts.append(dot(e.astype(bf16), v_ref[:, cols]) / total)
+            lses = jnp.where(lane == 8 * pair + h, top + jnp.log(total), lses)
+        mixed_ref[:, cols] = jnp.where(low, *parts).astype(bf16)
+    lse_ref[...] = lses.T[: lse_ref.shape[0]]
+    two, n2_ref[...], i2_ref[...] = norm_forward(one + dot(mixed_ref[...], w_ref[4]), vec_ref[2:3, :], vec_ref[3:4, :])
+    two_ref[...] = two
+    low_two_ref[...] = two.astype(bf16)
+
+
+def cross_forward(states, mixed, encoded, weights, vecs, scale, carry, collective_id):
+    rows, width = states.shape
+    steps = 4
+    block = pl.BlockSpec((rows // steps, width), lambda i: (i, 0))
+    thin = pl.BlockSpec((rows // steps, 1), lambda i: (i, 0))
+    heads = width // HD * 4
+    tall = lambda kind: jax.ShapeDtypeStruct((rows, width), kind)
+    column = jax.ShapeDtypeStruct((rows, 1), f32)
+    outs = [
+        (tall(bf16), block), (tall(f32), block), (column, thin), (tall(bf16), block), (encoded, fixed(encoded)),
+        (encoded, fixed(encoded)), (tall(bf16), block),
+        (jax.ShapeDtypeStruct((heads, rows), f32), pl.BlockSpec((heads, rows // steps), lambda i: (0, i))),
+        (tall(f32), block), (tall(f32), block), (column, thin), (tall(bf16), block),
+    ]
+    return hosted(
+        functools.partial(cross_forward_kernel, scale), steps, [states, mixed, encoded, weights, vecs],
+        [block, block, fixed(encoded), fixed(weights), fixed(vecs)],
+        [jax.ShapeDtypeStruct(o.shape, o.dtype) for o, _ in outs], [spec for _, spec in outs], [],
+        "cross_forward", carry, collective_id, ticks=2,
+    )
+
+
+def cross_backward_kernel(
+    scale, pairs, parts, b2_ref, mixed_ref, low_ref, mixed_one_ref, q_ref, lse_ref, k_ref, v_ref, w_ref, vec_ref, g2_ref,
+    n1_ref, i1_ref, g_out_ref, g_query_ref, g_self_out_ref, gk_ref, gv_ref, g1_ref, gm_ref, sums_ref,
+    g_mixed, gq_all, b1_all,
+):
+    i = pl.program_id(0)
+    rows, width = b2_ref.shape
+
+    @pl.when(i == 0)
+    def _():
+        for span in slices(rows, 4):
+            g_mixed[span, :] = dot(b2_ref[span, :], w_ref[4], 1, 1).astype(bf16)
+        sums_ref[...] = jnp.zeros_like(sums_ref)
+
+    j = i - 1
+
+    @pl.when((j >= 0) & (j < pairs))
+    def _():
+        cols = block_of(j, 2 * HD)
+        low = first_lanes((1, 2 * HD))
+        chooser = lax.broadcasted_iota(jnp.int32, (8, 2 * HD), 0)
+        chooser = ((chooser == 0) & first_lanes((8, 2 * HD))) | ((chooser == 1) & ~first_lanes((8, 2 * HD)))
+        chooser = chooser.astype(f32).astype(bf16)
+        gks, gvs = [0.0, 0.0], [0.0, 0.0]
+        for span in slices(rows, 2):
+            g, q = g_mixed[span, cols], q_ref[span, :]
+            product = g.astype(f32) * mixed_ref[span, cols].astype(f32)
+            upper = product.astype(bf16)
+            lower = (product - upper.astype(f32)).astype(bf16)
+            deltas = dot(chooser, upper, 1, 1) + dot(chooser, lower, 1, 1)
+            gqs = []
+            for h in range(2):
+                pick = low if h == 0 else ~low
+                keys = jnp.where(pick, k_ref[...], jnp.zeros((), bf16))
+                values = jnp.where(pick, v_ref[...], jnp.zeros((), bf16))
+                probs = jnp.exp(dot(keys, q, 1, 1) - lse_ref[h : h + 1, span])
+                grad_scores = (probs * (dot(values, g, 1, 1) - deltas[h : h + 1, :])).astype(bf16)
+                gvs[h] = gvs[h] + dot(probs.astype(bf16), g)
+                gks[h] = gks[h] + dot(grad_scores, q)
+                gqs.append(dot(grad_scores, k_ref[...], 0, 0))
+            gq_all[span, cols] = jnp.where(low, *gqs).astype(bf16) * scale
+        gk_ref[...] = jnp.where(low, *gks).astype(bf16)
+        gv_ref[...] = jnp.where(low, *gvs).astype(bf16)
+
+    m = j - pairs
+
+    @pl.when((m >= 0) & (m < parts))
+    def _():
+        at = block_of(m, rows // parts)
+        grad_one = g2_ref[...] + dot(gq_all[at, :], w_ref[1], 1, 1)
+        grad, g_gain, g_shift = norm_backward(grad_one, n1_ref[...], i1_ref[...], vec_ref[0:1, :])
+        sums_ref[0:1, :] += g_gain
+        sums_ref[1:2, :] += g_shift
+        g1_ref[...] = grad
+        b1_all[at, :] = grad.astype(bf16)
+        gm_ref[...] = dot(b1_all[at, :], w_ref[0], 1, 1).astype(bf16)
+
+    for u, (left, right, out) in enumerate(
+        ((mixed_ref, b2_ref, g_out_ref), (low_ref, gq_all, g_query_ref), (mixed_one_ref, b1_all, g_self_out_ref))
+    ):
+
+        @pl.when(m == parts + u)
+        def _():
+            for span in slices(width, 4):
+                out[span, :] = dot(left[:, span], right[...], 0, 0).astype(bf16)
+
+
+def cross_backward(
+    branch, mixed, low, mixed_one, grad, normed, inverse, q, lse, k, v, weights, vecs, scale, carry, collective_id
+):
+    rows, width = q.shape
+    pairs, parts = width // (2 * HD), 4
+    column = lambda a: pl.BlockSpec((a.shape[0], 2 * HD), lambda i: (0, jnp.clip(i - 1, 0, pairs - 1)))
+    some = lambda cols: pl.BlockSpec((rows // parts, cols), lambda i: (jnp.clip(i - 1 - pairs, 0, parts - 1), 0))
+    square = jax.ShapeDtypeStruct((width, width), bf16)
+    outs = [
+        (square, fixed(square)), (square, fixed(square)), (square, fixed(square)), (k, column(k)), (v, column(v)),
+        (grad, some(width)), (q, some(width)), (vecs, fixed(vecs)),
+    ]
+    args = [branch, mixed, low, mixed_one, q, lse, k, v, weights, vecs, grad, normed, inverse]
+    lse_spec = pl.BlockSpec((8, rows), lambda i: (jnp.clip(i - 1, 0, pairs - 1), 0))
+    return hosted(
+        functools.partial(cross_backward_kernel, scale, pairs, parts), 1 + pairs + parts + 3, args,
+        [fixed(a) for a in args[:4]] + [column(q), lse_spec, column(k), column(v), fixed(weights), fixed(vecs)]
+        + [some(width), some(width), some(1)],
+        [jax.ShapeDtypeStruct(o.shape, o.dtype) for o, _ in outs], [spec for _, spec in outs],
+        [pltpu.VMEM((rows, width), bf16)] * 3, "cross_backward", carry, collective_id, vmem=60,
+    )
 
 
 def ffn_forward_kernel(blocks, carry, low_ref, two_ref, cot_ref, vec_ref, w1_ref, *refs):
     refs = list(refs)
     w2_ref = refs.pop(0) if carry is None else carry.full
-    final_ref, branch_ref, grad_ref, act_ref, slope_ref, sums_ref, acts, acc, w2_buf, sems = refs
+    final_ref, branch_ref, grad_ref, slope_ref, g_contract_ref, sums_ref, acts, acc, w2_buf, sems = refs
     i = pl.program_id(0)
     spans = slices(low_ref.shape[0], 4)
 
@@ -691,9 +945,7 @@
         for span in spans:
             pre = dot(low_ref[span, :], w1_ref[0])
             phi = 0.5 * (1.0 + lax.erf(pre * INV_ROOT_TWO))
-            act = (pre * phi).astype(bf16)
-            acts[i, span, :] = act
-            act_ref[span, :] = act
+            acts[i, span, :] = (pre * phi).astype(bf16)
             slope_ref[span, :] = (phi + pre * jnp.exp(-0.5 * pre * pre) * INV_ROOT_TWO_PI).astype(bf16)
 
     j = i - blocks
@@ -706,7 +958,7 @@
         fetch(0, 0).start()
         acc[...] = two_ref[...]
 
-    @pl.when(j >= 0)
+    @pl.when((j >= 0) & (j < blocks))
     def _():
         slot = lax.rem(j + blocks * 2, 2)
 
@@ -733,6 +985,11 @@
         sums_ref[...] = jnp.zeros_like(sums_ref)
         sums_ref[0:1, :] = sums[0]
         sums_ref[1:2, :] = sums[1]
+
+    @pl.when(j >= blocks)
+    def _():
+        made = dot(acts[j - blocks], branch_ref[...], 0, 0).astype(bf16)
+        g_contract_ref[0] = made.reshape(g_contract_ref.shape[1:])
 
 
 def ffn_forward(low, two, cotangent, vecs, w1, w2, carry, collective_id):
@@ -750,12 +1007,14 @@
         args.append(w2)
         specs.append(HBM)
     tall = jax.ShapeDtypeStruct((rows, blocks * size), bf16)
-    outs = [low, low, two, tall, tall, jax.ShapeDtypeStruct((8, width), f32)]
+    part = w2.shape[1:] if carry is None else (carry.units, carry.rows, width)
+    outs = [low, low, two, tall, jax.ShapeDtypeStruct((blocks,) + part, bf16), jax.ShapeDtypeStruct((8, width), f32)]
     out_specs = [fixed(a) for a in outs[:3]]
-    out_specs += [pl.BlockSpec((rows, size), lambda i: (0, jnp.minimum(i, last)))] * 2 + [fixed(outs[5])]
-    part = (width // 256, size // (width // 256), width) if carry is None else (carry.units, carry.rows, width)
+    out_specs.append(pl.BlockSpec((rows, size), lambda i: (0, jnp.minimum(i, last))))
+    out_specs.append(pl.BlockSpec((1,) + part, lambda i: (jnp.maximum(i - 2 * blocks, 0), 0, 0, 0)))
+    out_specs.append(fixed(outs[5]))
     return hosted(
-        functools.partial(ffn_forward_kernel, blocks, carry), 2 * blocks, args, specs,
+        functools.partial(ffn_forward_kernel, blocks, carry), 3 * blocks, args, specs,
         [jax.ShapeDtypeStruct(a.shape, a.dtype) for a in outs], out_specs,
         [
             pltpu.VMEM((blocks, rows, size), bf16), pltpu.VMEM((rows, width), f32),
@@ -766,54 +1025,60 @@
 
 
 def ffn_backward_kernel(
-    low_ref, branch_ref, g_ref, normed_ref, inverse_ref, vec_ref, w1_ref, w2_ref, act_ref, slope_ref,
-    g_expand_ref, g_contract_ref, grad_ref, branch_two_ref, sums_ref, turned, acc,
+    blocks, low_ref, branch_ref, vec_ref, w1_ref, w2_ref, slope_ref, normed_ref, inverse_ref, g_ref,
+    g_expand_ref, grad_ref, branch_two_ref, sums_ref, turned, acc, g_pre, sem,
 ):
     i = pl.program_id(0)
     rows = low_ref.shape[0]
     spans = slices(rows, 4)
+    start = pltpu.make_async_copy(g_ref, acc, sem.at[0])
 
     @pl.when(i == 0)
     def _():
+        start.start()
         turned[...] = low_ref[...].T
-        acc[...] = g_ref[...]
-
-    w2 = w2_ref[0].reshape(-1, w2_ref.shape[-1])
-    g_contract_ref[0] = dot(act_ref[...], branch_ref[...], 0, 0).astype(bf16).reshape(g_contract_ref.shape[1:])
-    expand = 0.0
-    for span in spans:
-        g_pre = (dot(branch_ref[span, :], w2, 1, 1) * slope_ref[span, :].astype(f32)).astype(bf16)
-        expand = expand + dot(turned[:, span], g_pre)
-        acc[span, :] += dot(g_pre, w1_ref[0], 1, 1)
-    g_expand_ref[0] = expand.astype(bf16)
-
-    @pl.when(i == pl.num_programs(0) - 1)
-    def _():
-        gain = vec_ref[2:3, :]
-        sums = [0.0, 0.0]
-        for span in slices(rows, 8):
-            grad, *parts = norm_backward(acc[span, :], normed_ref[span, :], inverse_ref[span, :], gain)
-            grad_ref[span, :] = grad
-            branch_two_ref[span, :] = grad.astype(bf16)
-            sums = [a + b for a, b in zip(sums, parts)]
         sums_ref[...] = jnp.zeros_like(sums_ref)
-        sums_ref[0:1, :] = sums[0]
-        sums_ref[1:2, :] = sums[1]
-
-
-def ffn_backward(low, branch, grad, normed, inverse, vecs, w1, w2, act, slope):
+
+    @pl.when(i < blocks)
+    def _():
+        w2 = w2_ref[0].reshape(-1, w2_ref.shape[-1])
+        for span in spans:
+            g_pre[span, :] = (dot(branch_ref[span, :], w2, 1, 1) * slope_ref[span, :].astype(f32)).astype(bf16)
+        for span in slices(turned.shape[0], 4):
+            g_expand_ref[0, span, :] = dot(turned[span, :], g_pre[...]).astype(bf16)
+        pl.when(i == 0)(start.wait)
+        for span in spans:
+            acc[span, :] += dot(g_pre[span, :], w1_ref[0], 1, 1)
+
+    @pl.when(i >= blocks)
+    def _():
+        at = block_of(i - blocks, grad_ref.shape[0])
+        grad, g_gain, g_shift = norm_backward(acc[at, :], normed_ref[...], inverse_ref[...], vec_ref[2:3, :])
+        grad_ref[...] = grad
+        branch_two_ref[...] = grad.astype(bf16)
+        sums_ref[0:1, :] += g_gain
+        sums_ref[1:2, :] += g_shift
+
+
+def ffn_backward(low, branch, grad, normed, inverse, vecs, w1, w2, slope, carry, collective_id):
     rows, width = low.shape
     blocks, size = w2.shape[0], w2.shape[1] * w2.shape[2]
-    per = width // size
-    wide = pl.BlockSpec((1, width, size), lambda i: (i // per, 0, lax.rem(i, per)))
-    deep = pl.BlockSpec((1,) + w2.shape[1:], lambda i: (i, 0, 0, 0))
-    column = pl.BlockSpec((rows, size), lambda i: (0, i))
-    args = [low, branch, grad, normed, inverse, vecs, w1, w2, act, slope]
-    outs = [w1, w2, grad, low, jax.ShapeDtypeStruct((8, width), f32)]
+    per, last, parts = width // size, w2.shape[0] - 1, 4
+    wide = pl.BlockSpec((1, width, size), lambda i: (jnp.minimum(i, last) // per, 0, lax.rem(jnp.minimum(i, last), per)))
+    deep = pl.BlockSpec((1,) + w2.shape[1:], lambda i: (jnp.minimum(i, last), 0, 0, 0))
+    column = pl.BlockSpec((rows, size), lambda i: (0, jnp.minimum(i, last)))
+    some = lambda cols: pl.BlockSpec((rows // parts, cols), lambda i: (jnp.maximum(i - blocks, 0), 0))
+    args = [low, branch, vecs, w1, w2, slope, normed, inverse, grad]
+    outs = [w1, grad, low, vecs]
     return hosted(
-        ffn_backward_kernel, blocks, args, [fixed(a) for a in args[:6]] + [wide, deep, column, column],
-        [jax.ShapeDtypeStruct(a.shape, a.dtype) for a in outs], [wide, deep] + [fixed(a) for a in outs[2:]],
-        [pltpu.VMEM((width, rows), bf16), pltpu.VMEM((rows, width), f32)], "ffn_backward", vmem=60,
+        functools.partial(ffn_backward_kernel, blocks), blocks + parts, args,
+        [fixed(a) for a in args[:3]] + [wide, deep, column, some(width), some(1), HBM],
+        [jax.ShapeDtypeStruct(a.shape, a.dtype) for a in outs], [wide, some(width), some(width), fixed(vecs)],
+        [
+            pltpu.VMEM((width, rows), bf16), pltpu.VMEM((rows, width), f32), pltpu.VMEM((rows, size), bf16),
+            pltpu.SemaphoreType.DMA((1,)),
+        ],
+        "ffn_backward", carry, collective_id, vmem=60,
     )
 
 
@@ -827,84 +1092,60 @@
     vec = jnp.zeros((16, max(rows, 128)), bf16).at[: len(vectors), :rows].set(jnp.stack(vectors))
     take = lambda shards, units, alone, **more: Gather(n, width, shards, units, alone, **more) if small else None
     if small:
-        first, vecs = hosted(None, n, [], [], [], [], [], "gather_first", take(matrices[:3], 3, 1, vec=vec), 0)
+        chain = Chain(take(matrices[:3], 3, 1, vec=vec), take(matrices[3:8], 5, 2))
+        q_self, k_self, v_self, mixed_self, lse_self, first, vecs, second = self_forward(states, None, starts, scale, chain, 0)
     else:
         first = lax.all_gather(jnp.stack(matrices[:3]), "shard", axis=1, tiled=True)
         vecs = lax.all_gather(vec, "shard", axis=0)
+        second = lax.all_gather(jnp.stack(matrices[3:8]), "shard", axis=1, tiled=True)
+        q_self, k_self, v_self, mixed_self, lse_self = self_forward(states, first, starts, scale, None, None)
     vecs = vecs[:, : len(vectors), :rows].transpose(1, 0, 2).reshape(len(vectors), width).astype(f32)
     vecs = jnp.concatenate([vecs, jnp.zeros((2, width), f32)])
-    gain_one, shift_one, gain_two, shift_two = [vecs[i] for i in range(4)]
-    w_sq, w_sk, w_sv = [first[i] for i in range(3)]
-
-    wide = states.astype(f32)
-    q_self = (dot(states, w_sq) * scale).astype(bf16)
-    k_self = dot(states, w_sk).astype(bf16)
-    v_self = dot(states, w_sv).astype(bf16)
-    mixed_self, lse_self, *second = attend_forward(q_self, k_self, v_self, starts, take(matrices[3:8], 5, 2), 1)
-    if not small:
-        second = [lax.all_gather(jnp.stack(matrices[3:8]), "shard", axis=1, tiled=True)]
-    w_so, w_cq, w_ck, w_cv, w_co = [second[0][i] for i in range(5)]
-    hidden_one, normed_one, inverse_one = norm_forward(wide + dot(mixed_self, w_so), gain_one, shift_one)
-    one_low = hidden_one.astype(bf16)
-    q_cross = (dot(one_low, w_cq) * scale).astype(bf16)
-    k_cross = dot(encoded, w_ck).astype(bf16)
-    v_cross = dot(encoded, w_cv).astype(bf16)
-    mixed_cross, lse_cross, *third = attend_forward(q_cross, k_cross, v_cross, None, take([expand], blocks, 1), 2)
+    (one_low, normed_one, inverse_one, q_cross, k_cross, v_cross, mixed_cross, lse_cross, hidden_two, normed_two, inverse_two,
+     two_low, *third) = cross_forward(states, mixed_self, encoded, second, vecs, scale, take([expand], blocks, 1), 2)
     if not small:
         third = [lax.all_gather(expand.reshape(rows, blocks, width).transpose(1, 0, 2), "shard", axis=1, tiled=True)]
     w1 = third[0]
-    hidden_two, normed_two, inverse_two = norm_forward(hidden_one + dot(mixed_cross, w_co), gain_two, shift_two)
-    two_low = hidden_two.astype(bf16)
     w2 = None
     if not small:
         w2 = lax.all_gather(contract, "shard", axis=0, tiled=True).reshape(8, 4, -1, width)
-    final, branch_three, grad_three, act, slope, sums_three, *fourth = ffn_forward(
+    final, branch_three, grad_three, slope, g_contract, sums_three, *fourth = ffn_forward(
         two_low, hidden_two, cotangent, vecs, w1, w2, take([contract], blocks, 1, owner_first=True), 3
     )
     if small:
         w2 = fourth[0]
 
     give = lambda sources, alone, **more: Scatter(n, sources, alone, **more) if small else None
-    g_expand, g_contract, grad_resid_two, branch_two, sums_two = ffn_backward(
-        two_low, branch_three, grad_three, normed_two, inverse_two, vecs, w1, w2, act, slope
-    )
-    g_cross_out = dot(mixed_cross, branch_two, 0, 0).astype(bf16)
-    grad_mixed = dot(branch_two, w_co, 1, 1).astype(bf16)
-    g_q, g_k, g_v, *own_contract = attend_backward(
-        q_cross, k_cross, v_cross, grad_mixed, mixed_cross, lse_cross, None, give([g_contract], 1), 4
-    )
-    g_q = g_q * scale
-    g_cross = [
-        dot(one_low, g_q, 0, 0).astype(bf16), dot(encoded, g_k, 0, 0).astype(bf16), dot(encoded, g_v, 0, 0).astype(bf16),
-        g_cross_out,
-    ]
-    grad_encoded = dot(g_k, w_ck, 1, 1) + dot(g_v, w_cv, 1, 1)
-    grad_one = grad_resid_two + dot(g_q, w_cq, 1, 1)
-    grad_resid_one, *sums_one = norm_backward(grad_one, normed_one, inverse_one, gain_one)
-    branch_one = grad_resid_one.astype(bf16)
-    g_self_out = dot(mixed_self, branch_one, 0, 0).astype(bf16)
-    grad_mixed = dot(branch_one, w_so, 1, 1).astype(bf16)
-    g_q, g_k, g_v, *own_middle = attend_backward(
-        q_self, k_self, v_self, grad_mixed, mixed_self, lse_self, starts, give([g_expand, *g_cross], 2), 5
-    )
-    g_q = g_q * scale
-    g_self = [dot(states, g, 0, 0).astype(bf16) for g in (g_q, g_k, g_v)] + [g_self_out]
-    grad_states = grad_resid_one + dot(g_q, w_sq, 1, 1) + dot(g_k, w_sk, 1, 1) + dot(g_v, w_sv, 1, 1)
-    grads_vec = jnp.concatenate([*sums_one, sums_two[:2], sums_three[:2], jnp.zeros((2, width), f32)])
+    g_expand, grad_resid_two, branch_two, sums_two, *own_contract = ffn_backward(
+        two_low, branch_three, grad_three, normed_two, inverse_two, vecs, w1, w2, slope, give([g_contract], 1), 4
+    )
+    g_cross_out, g_cross_query, g_self_out, g_k, g_v, grad_resid_one, grad_mixed, sums_one, *own_expand = cross_backward(
+        branch_two, mixed_cross, one_low, mixed_self, grad_resid_two, normed_one, inverse_one, q_cross, lse_cross, k_cross,
+        v_cross, second, vecs, scale, give([g_expand], 1, start=1, every=2), 5
+    )
+    g_cross = [g_cross_query, dot(encoded, g_k, 0, 0).astype(bf16), dot(encoded, g_v, 0, 0).astype(bf16), g_cross_out]
+    grad_encoded = dot(g_k, second[2], 1, 1) + dot(g_v, second[3], 1, 1)
+    g_query, g_key, g_value, grad_states, *own_middle = self_backward(
+        q_self, k_self, v_self, grad_mixed, mixed_self, lse_self, starts, states, first, grad_resid_one, scale,
+        give([*g_cross, g_self_out], 1), 6
+    )
+    g_self = [g_query, g_key, g_value]
+    grads_vec = jnp.concatenate([sums_one[:2], sums_two[:2], sums_three[:2], jnp.zeros((2, width), f32)])
     if small:
-        own_self, own_vec = hosted(None, n, [], [], [], [], [], "scatter_last", give(g_self, 1, vec=grads_vec), 6)
-        own_contract, own_middle = own_contract[0], own_middle[0]
+        own_self, own_vec = hosted(None, n + 3, [], [], [], [], [], "scatter_last", give(g_self, 1, vec=grads_vec), 7)
+        own_contract, own_expand, own_middle = own_contract[0], own_expand[0], own_middle[0]
     else:
         total = lambda g: lax.psum(lax.psum_scatter(g, "shard", scatter_dimension=1, tiled=True), "rep")
         own_self = total(jnp.stack(g_self))
-        own_middle = total(jnp.concatenate([g_expand, jnp.stack(g_cross)]))
+        own_middle = total(jnp.stack([*g_cross, g_self_out]))
+        own_expand = total(g_expand)
         own_contract = total(g_contract.reshape(1, -1, width))
         own_vec = lax.dynamic_slice_in_dim(
             lax.psum(grads_vec, ("rep", "shard")), lax.axis_index("shard") * rows, rows, 1
         )
     own_contract = own_contract.reshape(blocks * rows, width).astype(f32)
-    own_expand = jnp.concatenate([own_middle[j] for j in range(blocks)], 1).astype(f32)
-    attention = [own_self[j] for j in range(4)] + [own_middle[blocks + j] for j in range(4)]
+    own_expand = jnp.concatenate([own_expand[j] for j in range(blocks)], 1).astype(f32)
+    attention = [own_self[0], own_self[1], own_self[2], own_middle[4]] + [own_middle[j] for j in range(4)]
     return (
         final,
         grad_states,

time: 605 us -> 519 us (0.86)
  matrix products: 106 us -> 10.1 us
  Pallas kernels: 455 us -> 481 us
  other arithmetic: 20.8 us -> 6.6 us
    dot_general x24 -> x4, matrix products: 106 us -> 10.1 us  [dot(): lax.dot_general(a, b, (((ca,), (cb,)), ((), ())), preferred_element_type=...]
    pallas_call x8 -> x7, Pallas kernels: 455 us -> 481 us  [hosted(): pl.pallas_call(whole, grid=(steps,), out_shape=list(out_shapes) + (carry....]
    convert_element_type x3 -> x1, other arithmetic: 9.4 us -> 1.52 us  [body(): jnp.concatenate([own_expand[j] for j in range(blocks)], 1).astype(f32)]
where the time goes in v3:
time: 519 us; the launch traced here: 510 us
  Pallas kernels  481 us (93%)
  local copies, waits for them, and re-layouts  11.8 us (2%)
  matrix products  10.1 us (2%)
  other arithmetic  6.6 us (1%)
    pallas_call x7, Pallas kernels, hosted(): pl.pallas_call(whole, grid=(steps,), out_shape=list(out_shapes) + (carry....  481 us

profile of v3, /device:TPU:0, one launch (start us, length us, event | category | flops | bytes accessed | tf_op | source)
XLA Modules:
  0.0 510.2 jit_solution(16147839751606673799)
XLA Ops:
  0.7 0.1 pad.12.clone
  0.7 0.8 stack.27
  1.5 0.6 scatter.4.refs_5_
  2.1 91.1 %self_forward.1 = (bf16[1024,1024]{1,0:T(8,128)(2,1)}, bf16[1024,1024]{1,0:T(8,128)(2,1)}, bf16[1024,1024]{1,0:T(8,128)(2,1)}, bf16[1024,1024]{1,0:T(8,128)(2,1)...) custom-call(s32[1,2]{1,0:T(1,128)} %refs_0_.5, ...), custom_call_target="tpu_custom_call" | custom-call | tf_op jit(solution)/shard_map/self_forward/pallas_call | solution.py:562
  93.2 0.7 slice_bitcast_fusion.4
  93.9 0.6 pad_convert_fusion.refs_4_.refs_3_.refs_2_.refs_9_
  94.5 50.7 %cross_forward.1 = (bf16[1024,1024]{1,0:T(8,128)(2,1)}, f32[1024,1024]{1,0:T(8,128)}, f32[1024,1]{1,0:T(8,128)}, bf16[1024,1024]{1,0:T(8,128)(2,1)}, bf16[256,10...) custom-call(bf16[1024,1024]{1,0:T(8,128)(2,1)} %refs_7_.3, ...), custom_call_target="tpu_custom_call" | custom-call | tf_op jit(solution)/shard_map/cross_forward/pallas_call | solution.py:562
  145.3 78.9 %ffn_forward.1 = (bf16[1024,1024]{1,0:T(8,128)(2,1)}, bf16[1024,1024]{1,0:T(8,128)(2,1)}, f32[1024,1024]{1,0:T(8,128)}, bf16[1024,4096]{1,0:T(8,128)(2,1)}, bf16...) custom-call(bf16[1024,1024]{1,0:T(8,128)(2,1)} %get-tuple-element.83.refs_0_, ...), custom_call_target="tpu_custom_call" | custom-call | tf_op jit(solution)/shard_map/ffn_forward/pallas_call | solution.py:562
  224.1 0.8 slice.93
  224.9 58.9 %ffn_backward.1 = (bf16[4,1024,1024]{2,1,0:T(8,128)(2,1)}, f32[1024,1024]{1,0:T(8,128)}, bf16[1024,1024]{1,0:T(8,128)(2,1)}, f32[8,1024]{1,0:T(8,128)}, bf16[4,128,1024]{2,1,0:T(8,128)(2,1)}) custom-call(bf16[1024,1024]{1,0:T(8,128)(2,1)} %get-tuple-element.83.refs_0_, bf16[1024,1024]{1,0:T(8,128)(2,1)} %get-tuple-element.90.refs_1_, ...), custom_call_target="tpu_custom_call" | custom-call | tf_op jit(solution)/shard_map/ffn_backward/pallas_call | solution.py:562
  283.8 76.7 %cross_backward.1 = (bf16[1024,1024]{1,0:T(8,128)(2,1)}, bf16[1024,1024]{1,0:T(8,128)(2,1)}, bf16[1024,1024]{1,0:T(8,128)(2,1)}, bf16[256,1024]{1,0:T(8,128)(2,1...) custom-call(bf16[1024,1024]{1,0:T(8,128)(2,1)} %get-tuple-element.97, ...), custom_call_target="tpu_custom_call" | custom-call | tf_op jit(solution)/shard_map/cross_backward/pallas_call | solution.py:562
  360.5 0.0 copy-start.3
  360.5 0.8 slice.91
  361.3 0.8 slice.92
  362.1 0.7 maximum_maximum_fusion.refs_3_
  362.8 2.5 fusion
  365.3 0.0 copy-done.3
  365.3 3.4 fusion.6
  368.7 0.1 slice_bitcast_fusion.3
  368.8 0.0 copy-start
  368.8 1.5 maximum_convert_fusion
  370.3 2.1 convert_bitcast_fusion.1.refs_11_
  372.4 2.1 convert_bitcast_fusion.refs_12_
  374.5 83.8 %self_backward.1 = (bf16[1024,1024]{1,0:T(8,128)(2,1)}, bf16[1024,1024]{1,0:T(8,128)(2,1)}, bf16[1024,1024]{1,0:T(8,128)(2,1)}, f32[1024,1024]{1,0:T(8,128)}, bf16[5,128,1024]{2,1,0:T(8,128)(2,1)}) custom-call(s32[1,2]{1,0:T(1,128)} %refs_0_.5, bf16[1024,1024]{1,0:T(8,128)(2,1)} %get-tuple-element.87.refs_1_, bf16[1024,1024]{1,0:T(8,128)(2,1)} %get-tuple-element.88.refs_2_, ...), custom_call_target="tpu_custom_call" | custom-call | tf_op jit(solution)/shard_map/self_backward/pallas_call | solution.py:562
  458.3 40.5 %scatter_last.1 = (bf16[3,128,1024]{2,1,0:T(8,128)(2,1)}, f32[8,128]{1,0:T(8,128)}) custom-call(bf16[1024,1024]{1,0:T(8,128)(2,1)} %get-tuple-element.118.refs_0_, bf16[1024,1024]{1,0:T(8,128)(2,1)} %get-tuple-element.119.refs_1_, bf16[1024,1024]{1,0:T(8,128)(2,1)} %get-tuple-element.120.refs_2_, f32[8,1024]{1,0:T(8,128)} %maximum_maximum_fusion.refs_3_), custom_call_target="tpu_custom_call" | custom-call | tf_op jit(solution)/shard_map/scatter_last/pallas_call | solution.py:562
  498.8 1.4 slice_bitcast_fusion.5
  500.3 1.6 bitcast_convert_fusion
  501.9 2.1 bitcast_convert_fusion.1
  504.0 0.9 copy-done.2
  504.9 1.3 copy.45
  506.2 1.6 copy-done.1
  507.8 2.0 copy.46
  (14 shorter events, 0.0 us)
Async XLA Ops:
  360.5 4.8 copy-start.3
  365.3 3.4 copy-start.6
  368.8 1.5 copy-start
  370.3 2.1 copy-start.8
  458.3 41.9 %copy-start.5 = (bf16[4,128,1024]{2,1,0:T(8,128)(2,1)S(1)}, bf16[4,128,1024]{2,1,0:T(8,128)(2,1)}, u32[]{:S(2)}) copy-start(bf16[4,128,1024]{2,1,0:T(8,128)(2,1)} %get-tuple-element.127) | copy-start | bytes 3145732
  498.8 3.1 copy-start.4
  498.8 3.1 copy-start.7
  501.9 3.0 copy-start.2
  504.9 2.9 copy-start.1

commit v4 on v3

--- a/solution.py
+++ b/solution.py
@@ -87,16 +87,17 @@
         shape = (n, units, self.rows, self.width) if owner_first else (units, n * self.rows, self.width)
         self.out_shapes = [jax.ShapeDtypeStruct(shape, bf16)]
         dma = pltpu.SemaphoreType.DMA
-        self.scratch = [pltpu.VMEM((units, self.rows, width), bf16), dma((2,))] + [dma((2, n - 1))] * 12
+        self.scratch = [pltpu.VMEM((units, self.rows, width), bf16), dma((2,)), dma((6, 2)), dma((3, 2))]
+        self.scratch += [dma((2, n - 1))] * 3
         if vec is not None:
             self.out_shapes.append(jax.ShapeDtypeStruct((n,) + vec.shape, vec.dtype))
             self.scratch += [dma((1,)), dma((n - 1,)), dma((n - 1,))]
 
     def bind(self, ins, outs, scratch):
         self.ins, self.full = ins, outs[0]
-        self.own, self.local, *self.sems = scratch[:14]
+        self.own, self.local, self.sent, self.got, *self.came = scratch[:7]
         if self.vec is not None:
-            self.vec_in, self.vecs, self.vec_sems = ins[-1], outs[1], scratch[14:]
+            self.vec_in, self.vecs, self.vec_sems = ins[-1], outs[1], scratch[7:]
             self.ins = ins[:-1]
         (self.x, self.c, self.shard, self.pos, self.shard_at, self.ways, self.sibling, self.across, _) = neighbours(self.n)
         on_ring = self.ne + self.ns
@@ -118,12 +119,20 @@
 
     def moved(self, kind, units, d, k, hop, who):
         here = self.spot(units, d, k)
-        return remote(here, here, self.sems[2 * kind].at[d, hop], self.sems[2 * kind + 1].at[d, hop], who)
+        came = self.came[kind].at[d, hop] if kind < 3 else self.got.at[kind - 3, d]
+        return remote(here, here, self.sent.at[kind, d], came, who)
+
+    def every(self, units, sem):
+        size = self.rows // 4
+        if self.owner_first:
+            hops = self.full.at[pl.ds(0, self.n - 1), units, pl.ds(0, size), :]
+        else:
+            hops = self.full.at[units, pl.ds(0, (self.n - 1) * size), :]
+        pltpu.make_async_copy(hops, hops, sem).wait()
 
     def first(self, e, d):
         src = self.own.at[self.sets[e], block_of(self.c * 2 + d, self.rows // 4), :]
-        sems = self.sems[2 * e : 2 * e + 2]
-        return remote(src, self.spot(self.sets[e], d, 0), sems[0].at[d, 0], sems[1].at[d, 0], self.ways[d][0])
+        return remote(src, self.spot(self.sets[e], d, 0), self.sent.at[e, d], self.came[e].at[d, 0], self.ways[d][0])
 
     def stored(self):
         return pltpu.make_async_copy(self.own, self.at(pl.ds(0, self.units), self.shard), self.local.at[1])
@@ -132,10 +141,10 @@
         return self.moved(e, self.sets[e], d, k, k, self.ways[d][0])
 
     def side(self, e, d, k):
-        return self.moved(2 + e, self.sets[e], d, k + 1, k, self.sibling)
+        return self.moved(3 + e, self.sets[e], d, k + 1, k, self.sibling)
 
     def cross(self, d, k):
-        return self.moved(4, self.mine, d, k + 1, k, self.across)
+        return self.moved(2, self.mine, d, k + 1, k, self.across)
 
     def forward(self, d, k):
         return self.moved(5, self.theirs, d, k + 1, k, self.sibling)
@@ -206,18 +215,13 @@
                 self.cross(d, n - 2).wait_recv()
                 self.forward(d, n - 2).start()
 
-        def drain(k, _):
-            for d in range(2):
-                for e in range(2):
-                    self.ring(e, d, k).wait_send()
-                    self.side(e, d, k).wait()
-                self.cross(d, k).wait_send()
-                self.forward(d, k).wait()
-            if self.vec is not None:
-                self.vec_hop(k).wait_send()
-            return 0
-
-        lax.fori_loop(0, n - 1, drain, 0)
+        for d in range(2):
+            for kind, units in enumerate((*self.sets, self.mine, *self.sets, self.theirs)):
+                self.every(units, self.sent.at[kind, d])
+                if kind > 2:
+                    self.every(units, self.got.at[kind - 3, d])
+        if self.vec is not None:
+            lax.fori_loop(0, n - 1, lambda k, _: (self.vec_hop(k).wait_send(), 0)[1], 0)
         self.stored().wait()
 
 
@@ -265,8 +269,8 @@
             pltpu.VMEM((2, n - 1, self.ns, half // 2, width), bf16),
             pltpu.VMEM((self.ns, half, width), bf16),
             pltpu.VMEM((alone, half, width), bf16),
-            dma((2, n)), dma((2, n)), dma((2, n)), dma((2, n)), dma((2, n)),
-            dma((2, n - 1)), dma((2, n - 1)), dma((2, n - 1)), dma((2, n - 1)),
+            dma((2, n)), dma((2,)), dma((2, n)), dma((2,)), dma((2, n)),
+            dma((2,)), dma((2, n - 1)), dma((2,)), dma((2, n - 1)),
             dma((2,)), dma((2,)), dma((3,)), dma((3,)), dma((3,)),
         ]
         if vec is not None:
@@ -318,13 +322,13 @@
     def crossing(self, d, k):
         rows = self.span(d, k)
         return remote(
-            self.near.at[self.theirs, rows, :], self.over.at[:, rows, :], self.xs.at[d, k], self.xr.at[d, k], self.across
+            self.near.at[self.theirs, rows, :], self.over.at[:, rows, :], self.xs.at[d], self.xr.at[d, k], self.across
         )
 
     def hop(self, e, d, k):
         src = self.near.at[self.sets[e], self.span(d, k), :]
         sent, got = self.ring_sems[e]
-        return remote(src, self.slots[e].at[d, k], sent.at[d, k], got.at[d, k], self.ways[d][0])
+        return remote(src, self.slots[e].at[d, k], sent.at[d], got.at[d, k], self.ways[d][0])
 
     def vec_hop(self, k):
         return remote(self.v_near.at[self.owner(0, k)], self.v_ring.at[k], self.v_rs.at[k], self.v_rr.at[k], self.ways[0][0])
@@ -349,7 +353,7 @@
         def sends(k, _):
             for d in range(2):
                 for src, dst in self.pieces(d, k, 1 - self.c, self.beside):
-                    remote(src, dst, self.cs.at[d, k], self.cr.at[d, k], self.sibling).start()
+                    remote(src, dst, self.cs.at[d], self.cr.at[d, k], self.sibling).start()
             return 0
 
         lax.fori_loop(0, n, sends, 0)
@@ -358,7 +362,7 @@
 
     def arrived(self, ref, ssem, rsem, d, k):
         here = self.region(ref, d, k)
-        return remote(here, here, ssem.at[d, k], rsem.at[d, k], self.sibling)
+        return remote(here, here, ssem.at[d], rsem.at[d, k], self.sibling)
 
     def pair(self, k):
         for d in range(2):
@@ -505,28 +509,26 @@
         for e in range(2):
             self.swap(e).wait_send()
 
-        def drain(k, _):
-            for d in range(2):
-                self.arrived(self.beside, self.cs, self.cr, d, k).wait_send()
-                self.crossing(d, k).wait_send()
-            return 0
-
-        lax.fori_loop(0, n, drain, 0)
-
-        def drain_ring(k, _):
-            for d in range(2):
-                self.hop(0, d, k).wait_send()
-                self.hop(1, d, k).wait_send()
-            if self.vec is not None:
-                self.vec_hop(k).wait_send()
-            return 0
-
-        lax.fori_loop(0, n - 1, drain_ring, 0)
+        span = pl.ds(0, n * self.quarter)
+        for d in range(2):
+            totals = [(self.beside.at[:, span, :], self.cs.at[d]), (self.over.at[:, span, :], self.xs.at[d])]
+            totals += [(self.slots[e].at[d], self.ring_sems[e][0].at[d]) for e in range(2)]
+            for whole, sem in totals:
+                pltpu.make_async_copy(whole, whole, sem).wait()
+        if self.vec is not None:
+            lax.fori_loop(0, n - 1, lambda k, _: (self.vec_hop(k).wait_send(), 0)[1], 0)
 
 
 def hosted(
-    kernel, steps, args, in_specs, out_shapes, out_specs, scratch, name, carry=None, collective_id=None, done_by=None, ticks=1, vmem=58
+    kernel, steps, args, in_specs, out_shapes, out_specs, scratch, name, carry=None, collective_id=None, done_by=None, ticks=1, vmem=58,
+    late=(),
 ):
+    args, in_specs = list(args), list(in_specs)
+    stores = []
+    for at, _, lead in late:
+        in_specs[at] = HBM
+        stores.append(pltpu.VMEM(args[at].shape if lead is None else (lead,) + args[at].shape[1:], args[at].dtype))
+    scratch = list(scratch) + stores + ([pltpu.SemaphoreType.DMA((len(late),))] if late else [])
     counts = [len(args), len(out_shapes), len(scratch)]
     extra = [0, 0, 0]
     params = dict(vmem_limit_bytes=vmem * MIB)
@@ -541,10 +543,23 @@
             other.append(refs[first + count : first + count + more])
             first += count + more
         i = pl.program_id(0)
+        copies = []
+        if late:
+            *main, late_sems = main
+            kept = main[len(main) - len(late) :]
+            main = main[: len(main) - len(late)]
+            for m, (at, _, lead) in enumerate(late):
+                src = main[at] if lead is None else main[at].at[pl.ds(0, lead)]
+                copies.append(pltpu.make_async_copy(src, kept[m], late_sems.at[m]))
+                main[at] = kept[m]
 
         def tick(j):
             if carry is not None:
                 carry.step(i * ticks + j)
+            if j == 0 and late:
+                pl.when(i == 0)(lambda: [copy.start() for copy in copies] and None)
+                for copy, (_, step, _) in zip(copies, late):
+                    pl.when(i == step)(copy.wait)
 
         if carry is not None:
             carry.bind(*other)
@@ -777,7 +792,7 @@
         + [pl.BlockSpec((1, 8, rows), lambda i: (jnp.minimum(i, last), 0, 0)), fixed(states), fixed(weights), some],
         [square] * 3 + [jax.ShapeDtypeStruct((rows, width), f32)], [fixed(square)] * 3 + [some],
         [pltpu.VMEM((regions, size, size), f32), pltpu.VMEM((3, rows, width), bf16)],
-        "self_backward", carry, collective_id, vmem=60,
+        "self_backward", carry, collective_id, vmem=60, late=((7, pairs, None), (8, pairs + 3, None)),
     )
 
 
@@ -845,8 +860,8 @@
 
 def cross_backward_kernel(
     scale, pairs, parts, b2_ref, mixed_ref, low_ref, mixed_one_ref, q_ref, lse_ref, k_ref, v_ref, w_ref, vec_ref, g2_ref,
-    n1_ref, i1_ref, g_out_ref, g_query_ref, g_self_out_ref, gk_ref, gv_ref, g1_ref, gm_ref, sums_ref,
-    g_mixed, gq_all, b1_all,
+    n1_ref, i1_ref, w_out_ref, enc_ref, g_out_ref, g_query_ref, g_self_out_ref, g_key_ref, g_value_ref, g1_ref, gm_ref,
+    sums_ref, g_enc_ref, g_mixed, gq_all, b1_all, gk_all, gv_all,
 ):
     i = pl.program_id(0)
     rows, width = b2_ref.shape
@@ -854,7 +869,7 @@
     @pl.when(i == 0)
     def _():
         for span in slices(rows, 4):
-            g_mixed[span, :] = dot(b2_ref[span, :], w_ref[4], 1, 1).astype(bf16)
+            g_mixed[span, :] = dot(b2_ref[span, :], w_out_ref[0], 1, 1).astype(bf16)
         sums_ref[...] = jnp.zeros_like(sums_ref)
 
     j = i - 1
@@ -884,8 +899,8 @@
                 gks[h] = gks[h] + dot(grad_scores, q)
                 gqs.append(dot(grad_scores, k_ref[...], 0, 0))
             gq_all[span, cols] = jnp.where(low, *gqs).astype(bf16) * scale
-        gk_ref[...] = jnp.where(low, *gks).astype(bf16)
-        gv_ref[...] = jnp.where(low, *gvs).astype(bf16)
+        gk_all[:, cols] = jnp.where(low, *gks).astype(bf16)
+        gv_all[:, cols] = jnp.where(low, *gvs).astype(bf16)
 
     m = j - pairs
 
@@ -909,9 +924,16 @@
             for span in slices(width, 4):
                 out[span, :] = dot(left[:, span], right[...], 0, 0).astype(bf16)
 
+    @pl.when(m == parts + 3)
+    def _():
+        for span in slices(width, 2):
+            g_key_ref[span, :] = dot(enc_ref[:, span], gk_all[...], 0, 0).astype(bf16)
+            g_value_ref[span, :] = dot(enc_ref[:, span], gv_all[...], 0, 0).astype(bf16)
+        g_enc_ref[...] = dot(gk_all[...], w_ref[2], 1, 1) + dot(gv_all[...], w_ref[3], 1, 1)
+
 
 def cross_backward(
-    branch, mixed, low, mixed_one, grad, normed, inverse, q, lse, k, v, weights, vecs, scale, carry, collective_id
+    branch, mixed, low, mixed_one, grad, normed, inverse, q, lse, k, v, weights, vecs, encoded, scale, carry, collective_id
 ):
     rows, width = q.shape
     pairs, parts = width // (2 * HD), 4
@@ -919,17 +941,19 @@
     some = lambda cols: pl.BlockSpec((rows // parts, cols), lambda i: (jnp.clip(i - 1 - pairs, 0, parts - 1), 0))
     square = jax.ShapeDtypeStruct((width, width), bf16)
     outs = [
-        (square, fixed(square)), (square, fixed(square)), (square, fixed(square)), (k, column(k)), (v, column(v)),
-        (grad, some(width)), (q, some(width)), (vecs, fixed(vecs)),
+        *[(square, fixed(square))] * 5, (grad, some(width)), (q, some(width)), (vecs, fixed(vecs)),
+        (jax.ShapeDtypeStruct(k.shape, f32), fixed(k)),
     ]
-    args = [branch, mixed, low, mixed_one, q, lse, k, v, weights, vecs, grad, normed, inverse]
+    args = [branch, mixed, low, mixed_one, q, lse, k, v, weights, vecs, grad, normed, inverse, weights, encoded]
+    out_weight = pl.BlockSpec((1, width, width), lambda i: (4, 0, 0), pipeline_mode=pl.Buffered(1))
     lse_spec = pl.BlockSpec((8, rows), lambda i: (jnp.clip(i - 1, 0, pairs - 1), 0))
     return hosted(
-        functools.partial(cross_backward_kernel, scale, pairs, parts), 1 + pairs + parts + 3, args,
+        functools.partial(cross_backward_kernel, scale, pairs, parts), 1 + pairs + parts + 4, args,
         [fixed(a) for a in args[:4]] + [column(q), lse_spec, column(k), column(v), fixed(weights), fixed(vecs)]
-        + [some(width), some(width), some(1)],
+        + [some(width), some(width), some(1), out_weight, HBM],
         [jax.ShapeDtypeStruct(o.shape, o.dtype) for o, _ in outs], [spec for _, spec in outs],
-        [pltpu.VMEM((rows, width), bf16)] * 3, "cross_backward", carry, collective_id, vmem=60,
+        [pltpu.VMEM((rows, width), bf16)] * 3 + [pltpu.VMEM(k.shape, bf16)] * 2, "cross_backward", carry, collective_id, vmem=62,
+        late=((2, 1 + pairs, None), (3, 1 + pairs, None), (8, 1 + pairs, 4), (14, 1 + pairs, None)),
     )
 
 
@@ -1021,6 +1045,7 @@
             pltpu.VMEM((2,) + part, bf16), pltpu.SemaphoreType.DMA((2,)),
         ],
         "ffn_forward", carry, collective_id, done_by=blocks if carry else None, vmem=60,
+        late=((1, blocks, None), (2, 2 * blocks - 1, None)),
     )
 
 
@@ -1119,12 +1144,12 @@
     g_expand, grad_resid_two, branch_two, sums_two, *own_contract = ffn_backward(
         two_low, branch_three, grad_three, normed_two, inverse_two, vecs, w1, w2, slope, give([g_contract], 1), 4
     )
-    g_cross_out, g_cross_query, g_self_out, g_k, g_v, grad_resid_one, grad_mixed, sums_one, *own_expand = cross_backward(
+    (g_cross_out, g_cross_query, g_self_out, g_cross_key, g_cross_value, grad_resid_one, grad_mixed, sums_one, grad_encoded,
+     *own_expand) = cross_backward(
         branch_two, mixed_cross, one_low, mixed_self, grad_resid_two, normed_one, inverse_one, q_cross, lse_cross, k_cross,
-        v_cross, second, vecs, scale, give([g_expand], 1, start=1, every=2), 5
-    )
-    g_cross = [g_cross_query, dot(encoded, g_k, 0, 0).astype(bf16), dot(encoded, g_v, 0, 0).astype(bf16), g_cross_out]
-    grad_encoded = dot(g_k, second[2], 1, 1) + dot(g_v, second[3], 1, 1)
+        v_cross, second, vecs, encoded, scale, give([g_expand], 1, start=1, every=2), 5
+    )
+    g_cross = [g_cross_query, g_cross_key, g_cross_value, g_cross_out]
     g_query, g_key, g_value, grad_states, *own_middle = self_backward(
         q_self, k_self, v_self, grad_mixed, mixed_self, lse_self, starts, states, first, grad_resid_one, scale,
         give([*g_cross, g_self_out], 1), 6

time: 519 us -> 496 us (0.956)
  Pallas kernels: 481 us -> 466 us
  matrix products: 10.1 us -> 0 us
    pallas_call x7, Pallas kernels: 481 us -> 466 us  [hosted(): pl.pallas_call(whole, grid=(steps,), out_shape=list(out_shapes) + (carry....]
    dot_general x4 -> x0, matrix products: 10.1 us -> none  [dot(): lax.dot_general(a, b, (((ca,), (cb,)), ((), ())), preferred_element_type=...]
where the time goes in v4:
time: 496 us; the launch traced here: 487 us
  Pallas kernels  466 us (94%)
  local copies, waits for them, and re-layouts  13.4 us (3%)
  other arithmetic  6.6 us (1%)
    pallas_call x7, Pallas kernels, hosted(): pl.pallas_call(whole, grid=(steps,), out_shape=list(out_shapes) + (carry....  466 us

profile of v4, /device:TPU:0, one launch (start us, length us, event | category | flops | bytes accessed | tf_op | source)
XLA Modules:
  0.0 487.4 jit_solution(5998072576790416903)
XLA Ops:
  0.7 0.1 pad.12.clone
  0.7 0.8 stack.27
  1.5 0.6 scatter.4.refs_5_
  2.1 88.8 %self_forward.1 = (bf16[1024,1024]{1,0:T(8,128)(2,1)}, bf16[1024,1024]{1,0:T(8,128)(2,1)}, bf16[1024,1024]{1,0:T(8,128)(2,1)}, bf16[1024,1024]{1,0:T(8,128)(2,1)...) custom-call(s32[1,2]{1,0:T(1,128)} %refs_0_.5, ...), custom_call_target="tpu_custom_call" | custom-call | tf_op jit(solution)/shard_map/self_forward/pallas_call | solution.py:577
  90.9 0.7 slice_bitcast_fusion.4
  91.6 0.6 pad_convert_fusion.refs_4_.refs_3_.refs_2_.refs_9_
  92.2 50.4 %cross_forward.1 = (bf16[1024,1024]{1,0:T(8,128)(2,1)}, f32[1024,1024]{1,0:T(8,128)}, f32[1024,1]{1,0:T(8,128)}, bf16[1024,1024]{1,0:T(8,128)(2,1)}, bf16[256,10...) custom-call(bf16[1024,1024]{1,0:T(8,128)(2,1)} %refs_7_.3, ...), custom_call_target="tpu_custom_call" | custom-call | tf_op jit(solution)/shard_map/cross_forward/pallas_call | solution.py:577
  142.6 75.7 %ffn_forward.1 = (bf16[1024,1024]{1,0:T(8,128)(2,1)}, bf16[1024,1024]{1,0:T(8,128)(2,1)}, f32[1024,1024]{1,0:T(8,128)}, bf16[1024,4096]{1,0:T(8,128)(2,1)}, bf16...) custom-call(bf16[1024,1024]{1,0:T(8,128)(2,1)} %get-tuple-element.84.refs_0_, ...), custom_call_target="tpu_custom_call" | custom-call | tf_op jit(solution)/shard_map/ffn_forward/pallas_call | solution.py:577
  218.3 0.8 slice.85
  219.1 58.6 %ffn_backward.1 = (bf16[4,1024,1024]{2,1,0:T(8,128)(2,1)}, f32[1024,1024]{1,0:T(8,128)}, bf16[1024,1024]{1,0:T(8,128)(2,1)}, f32[8,1024]{1,0:T(8,128)}, bf16[4,128,1024]{2,1,0:T(8,128)(2,1)}) custom-call(bf16[1024,1024]{1,0:T(8,128)(2,1)} %get-tuple-element.84.refs_0_, bf16[1024,1024]{1,0:T(8,128)(2,1)} %get-tuple-element.91.refs_1_, ...), custom_call_target="tpu_custom_call" | custom-call | tf_op jit(solution)/shard_map/ffn_backward/pallas_call | solution.py:577
  277.7 72.4 %cross_backward.1 = (bf16[1024,1024]{1,0:T(8,128)(2,1)}, bf16[1024,1024]{1,0:T(8,128)(2,1)}, bf16[1024,1024]{1,0:T(8,128)(2,1)}, bf16[1024,1024]{1,0:T(8,128)(2,...) custom-call(bf16[1024,1024]{1,0:T(8,128)(2,1)} %get-tuple-element.98, ...), custom_call_target="tpu_custom_call" | custom-call | tf_op jit(solution)/shard_map/cross_backward/pallas_call | solution.py:577
  350.1 80.7 %self_backward.1 = (bf16[1024,1024]{1,0:T(8,128)(2,1)}, bf16[1024,1024]{1,0:T(8,128)(2,1)}, bf16[1024,1024]{1,0:T(8,128)(2,1)}, f32[1024,1024]{1,0:T(8,128)}, bf16[5,128,1024]{2,1,0:T(8,128)(2,1)}) custom-call(s32[1,2]{1,0:T(1,128)} %refs_0_.5, bf16[1024,1024]{1,0:T(8,128)(2,1)} %get-tuple-element.88.refs_1_, bf16[1024,1024]{1,0:T(8,128)(2,1)} %get-tuple-element.89.refs_2_, ...), custom_call_target="tpu_custom_call" | custom-call | tf_op jit(solution)/shard_map/self_backward/pallas_call | solution.py:577
  430.9 0.8 slice.83
  431.6 0.8 slice.84
  432.4 0.7 maximum_maximum_fusion.refs_3_
  433.1 39.7 %scatter_last.1 = (bf16[3,128,1024]{2,1,0:T(8,128)(2,1)}, f32[8,128]{1,0:T(8,128)}) custom-call(bf16[1024,1024]{1,0:T(8,128)(2,1)} %get-tuple-element.120.refs_0_, bf16[1024,1024]{1,0:T(8,128)(2,1)} %get-tuple-element.121.refs_1_, bf16[1024,1024]{1,0:T(8,128)(2,1)} %get-tuple-element.122.refs_2_, f32[8,1024]{1,0:T(8,128)} %maximum_maximum_fusion.refs_3_), custom_call_target="tpu_custom_call" | custom-call | tf_op jit(solution)/shard_map/scatter_last/pallas_call | solution.py:577
  472.8 1.4 slice_bitcast_fusion.5
  474.2 0.0 copy-done.5
  474.2 0.1 slice_bitcast_fusion.3
  474.3 0.0 copy-start.3
  474.3 1.5 maximum_convert_fusion
  475.9 0.0 copy-done.3
  475.9 1.6 bitcast_convert_fusion
  477.5 0.0 copy-done.2
  477.5 0.6 copy-done.6
  478.1 2.1 bitcast_convert_fusion.1
  480.3 0.9 copy-done.1
  481.1 1.3 copy.42
  482.4 1.6 copy-done
  484.1 2.0 copy.43
  486.1 0.0 copy-done.4
  486.1 1.0 copy.44
  (7 shorter events, 0.0 us)
Async XLA Ops:
  433.1 41.2 %copy-start.5 = (bf16[4,128,1024]{2,1,0:T(8,128)(2,1)S(1)}, bf16[4,128,1024]{2,1,0:T(8,128)(2,1)}, u32[]{:S(2)}) copy-start(bf16[4,128,1024]{2,1,0:T(8,128)(2,1)} %get-tuple-element.128) | copy-start | bytes 3145732
  474.3 1.5 copy-start.3
  475.9 1.6 copy-start.2
  475.9 2.3 copy-start.6
  478.1 3.0 copy-start.1
  481.1 2.9 copy-start
  484.1 2.0 copy-start.4

commit v5 on v4

--- a/solution.py
+++ b/solution.py
@@ -975,27 +975,29 @@
     j = i - blocks
 
     def fetch(block, slot):
-        return pltpu.make_async_copy(w2_ref.at[block], w2_buf.at[slot], sems.at[slot])
+        return pltpu.make_async_copy(w2_ref.at[pl.ds(block * 2, 2)], w2_buf.at[slot], sems.at[slot])
+
+    half = blocks // 2
 
     @pl.when(j == 0)
     def _():
         fetch(0, 0).start()
         acc[...] = two_ref[...]
 
-    @pl.when((j >= 0) & (j < blocks))
+    @pl.when((j >= 0) & (j < half))
     def _():
         slot = lax.rem(j + blocks * 2, 2)
 
-        @pl.when(j + 1 < blocks)
+        @pl.when(j + 1 < half)
         def _():
             fetch(j + 1, 1 - slot).start()
 
         fetch(j, slot).wait()
-        w2 = w2_buf[slot].reshape(-1, w2_buf.shape[-1])
+        w2 = [w2_buf[slot, m].reshape(-1, w2_buf.shape[-1]) for m in range(2)]
         for span in spans:
-            acc[span, :] += dot(acts[j, span, :], w2)
-
-    @pl.when(j == blocks - 1)
+            acc[span, :] += dot(acts[2 * j, span, :], w2[0]) + dot(acts[2 * j + 1, span, :], w2[1])
+
+    @pl.when(j == half - 1)
     def _():
         gain, shift = vec_ref[4:5, :], vec_ref[5:6, :]
         sums = [0.0, 0.0]
@@ -1007,12 +1009,12 @@
             branch_ref[span, :] = grad.astype(bf16)
             sums = [a + b for a, b in zip(sums, parts)]
         sums_ref[...] = jnp.zeros_like(sums_ref)
-        sums_ref[0:1, :] = sums[0]
-        sums_ref[1:2, :] = sums[1]
-
-    @pl.when(j >= blocks)
-    def _():
-        made = dot(acts[j - blocks], branch_ref[...], 0, 0).astype(bf16)
+        sums_ref[4:5, :] = sums[0]
+        sums_ref[5:6, :] = sums[1]
+
+    @pl.when(j >= half)
+    def _():
+        made = dot(acts[j - half], branch_ref[...], 0, 0).astype(bf16)
         g_contract_ref[0] = made.reshape(g_contract_ref.shape[1:])
 
 
@@ -1035,17 +1037,17 @@
     outs = [low, low, two, tall, jax.ShapeDtypeStruct((blocks,) + part, bf16), jax.ShapeDtypeStruct((8, width), f32)]
     out_specs = [fixed(a) for a in outs[:3]]
     out_specs.append(pl.BlockSpec((rows, size), lambda i: (0, jnp.minimum(i, last))))
-    out_specs.append(pl.BlockSpec((1,) + part, lambda i: (jnp.maximum(i - 2 * blocks, 0), 0, 0, 0)))
+    out_specs.append(pl.BlockSpec((1,) + part, lambda i: (jnp.maximum(i - blocks - blocks // 2, 0), 0, 0, 0)))
     out_specs.append(fixed(outs[5]))
     return hosted(
-        functools.partial(ffn_forward_kernel, blocks, carry), 3 * blocks, args, specs,
+        functools.partial(ffn_forward_kernel, blocks, carry), 2 * blocks + blocks // 2, args, specs,
         [jax.ShapeDtypeStruct(a.shape, a.dtype) for a in outs], out_specs,
         [
             pltpu.VMEM((blocks, rows, size), bf16), pltpu.VMEM((rows, width), f32),
-            pltpu.VMEM((2,) + part, bf16), pltpu.SemaphoreType.DMA((2,)),
+            pltpu.VMEM((2, 2) + part, bf16), pltpu.SemaphoreType.DMA((2,)),
         ],
         "ffn_forward", carry, collective_id, done_by=blocks if carry else None, vmem=60,
-        late=((1, blocks, None), (2, 2 * blocks - 1, None)),
+        late=((1, blocks, None), (2, blocks + blocks // 2 - 1, None)),
     )
 
 
@@ -1081,8 +1083,8 @@
         grad, g_gain, g_shift = norm_backward(acc[at, :], normed_ref[...], inverse_ref[...], vec_ref[2:3, :])
         grad_ref[...] = grad
         branch_two_ref[...] = grad.astype(bf16)
-        sums_ref[0:1, :] += g_gain
-        sums_ref[1:2, :] += g_shift
+        sums_ref[2:3, :] += g_gain
+        sums_ref[3:4, :] += g_shift
 
 
 def ffn_backward(low, branch, grad, normed, inverse, vecs, w1, w2, slope, carry, collective_id):
@@ -1155,7 +1157,7 @@
         give([*g_cross, g_self_out], 1), 6
     )
     g_self = [g_query, g_key, g_value]
-    grads_vec = jnp.concatenate([sums_one[:2], sums_two[:2], sums_three[:2], jnp.zeros((2, width), f32)])
+    grads_vec = sums_one + sums_two + sums_three
     if small:
         own_self, own_vec = hosted(None, n + 3, [], [], [], [], [], "scatter_last", give(g_self, 1, vec=grads_vec), 7)
         own_contract, own_expand, own_middle = own_contract[0], own_expand[0], own_middle[0]

time: 496 us -> 493 us (level)
  no operation moved by 1% of the time
where the time goes in v5:
time: 493 us; the launch traced here: 485 us
  Pallas kernels  465 us (94%)
  local copies, waits for them, and re-layouts  11 us (2%)
  other arithmetic  7.29 us (1%)
    pallas_call x7, Pallas kernels, hosted(): pl.pallas_call(whole, grid=(steps,), out_shape=list(out_shapes) + (carry....  465 us

profile of v5, /device:TPU:0, one launch (start us, length us, event | category | flops | bytes accessed | tf_op | source)
XLA Modules:
  0.0 484.9 jit_solution(5435764179478683033)
XLA Ops:
  0.7 0.8 stack.27
  1.4 0.6 scatter.4.refs_5_
  2.0 88.8 %self_forward.1 = (bf16[1024,1024]{1,0:T(8,128)(2,1)}, bf16[1024,1024]{1,0:T(8,128)(2,1)}, bf16[1024,1024]{1,0:T(8,128)(2,1)}, bf16[1024,1024]{1,0:T(8,128)(2,1)...) custom-call(s32[1,2]{1,0:T(1,128)} %refs_0_.5, ...), custom_call_target="tpu_custom_call" | custom-call | tf_op jit(solution)/shard_map/self_forward/pallas_call | solution.py:577
  90.8 0.7 slice_bitcast_fusion.4
  91.5 0.6 pad_convert_fusion.refs_4_.refs_3_.refs_2_.refs_9_
  92.2 50.2 %cross_forward.1 = (bf16[1024,1024]{1,0:T(8,128)(2,1)}, f32[1024,1024]{1,0:T(8,128)}, f32[1024,1]{1,0:T(8,128)}, bf16[1024,1024]{1,0:T(8,128)(2,1)}, bf16[256,10...) custom-call(bf16[1024,1024]{1,0:T(8,128)(2,1)} %refs_7_.3, ...), custom_call_target="tpu_custom_call" | custom-call | tf_op jit(solution)/shard_map/cross_forward/pallas_call | solution.py:577
  142.4 74.5 %ffn_forward.1 = (bf16[1024,1024]{1,0:T(8,128)(2,1)}, bf16[1024,1024]{1,0:T(8,128)(2,1)}, f32[1024,1024]{1,0:T(8,128)}, bf16[1024,4096]{1,0:T(8,128)(2,1)}, bf16...) custom-call(bf16[1024,1024]{1,0:T(8,128)(2,1)} %get-tuple-element.84.refs_0_, ...), custom_call_target="tpu_custom_call" | custom-call | tf_op jit(solution)/shard_map/ffn_forward/pallas_call | solution.py:577
  216.9 59.0 %ffn_backward.1 = (bf16[4,1024,1024]{2,1,0:T(8,128)(2,1)}, f32[1024,1024]{1,0:T(8,128)}, bf16[1024,1024]{1,0:T(8,128)(2,1)}, f32[8,1024]{1,0:T(8,128)}, bf16[4,128,1024]{2,1,0:T(8,128)(2,1)}) custom-call(bf16[1024,1024]{1,0:T(8,128)(2,1)} %get-tuple-element.84.refs_0_, bf16[1024,1024]{1,0:T(8,128)(2,1)} %get-tuple-element.91.refs_1_, ...), custom_call_target="tpu_custom_call" | custom-call | tf_op jit(solution)/shard_map/ffn_backward/pallas_call | solution.py:577
  275.9 0.0 copy-start.7
  275.9 0.0 copy-start.8
  275.9 72.5 %cross_backward.1 = (bf16[1024,1024]{1,0:T(8,128)(2,1)}, bf16[1024,1024]{1,0:T(8,128)(2,1)}, bf16[1024,1024]{1,0:T(8,128)(2,1)}, bf16[1024,1024]{1,0:T(8,128)(2,...) custom-call(bf16[1024,1024]{1,0:T(8,128)(2,1)} %get-tuple-element.98, ...), custom_call_target="tpu_custom_call" | custom-call | tf_op jit(solution)/shard_map/cross_backward/pallas_call | solution.py:577
  348.4 0.0 copy-done.7
  348.5 0.0 copy-done.8
  348.5 1.4 add_add_fusion.refs_3_
  349.8 80.7 %self_backward.1 = (bf16[1024,1024]{1,0:T(8,128)(2,1)}, bf16[1024,1024]{1,0:T(8,128)(2,1)}, bf16[1024,1024]{1,0:T(8,128)(2,1)}, f32[1024,1024]{1,0:T(8,128)}, bf16[5,128,1024]{2,1,0:T(8,128)(2,1)}) custom-call(s32[1,2]{1,0:T(1,128)} %refs_0_.5, bf16[1024,1024]{1,0:T(8,128)(2,1)} %get-tuple-element.88.refs_1_, bf16[1024,1024]{1,0:T(8,128)(2,1)} %get-tuple-element.89.refs_2_, ...), custom_call_target="tpu_custom_call" | custom-call | tf_op jit(solution)/shard_map/self_backward/pallas_call | solution.py:577
  430.6 0.0 copy-start.5
  430.6 39.7 %scatter_last.1 = (bf16[3,128,1024]{2,1,0:T(8,128)(2,1)}, f32[8,128]{1,0:T(8,128)}) custom-call(bf16[1024,1024]{1,0:T(8,128)(2,1)} %get-tuple-element.120.refs_0_, bf16[1024,1024]{1,0:T(8,128)(2,1)} %get-tuple-element.121.refs_1_, bf16[1024,1024]{1,0:T(8,128)(2,1)} %get-tuple-element.122.refs_2_, f32[8,1024]{1,0:T(8,128)} %add_add_fusion.refs_3_), custom_call_target="tpu_custom_call" | custom-call | tf_op jit(solution)/shard_map/scatter_last/pallas_call | solution.py:577
  470.3 1.4 slice_bitcast_fusion.5
  471.7 0.0 copy-done.5
  471.7 0.1 slice_bitcast_fusion.3
  471.8 0.0 copy-start.3
  471.8 1.5 maximum_convert_fusion
  473.4 0.0 copy-done.3
  473.4 1.6 bitcast_convert_fusion
  475.0 0.0 copy-done.2
  475.0 0.6 copy-done.6
  475.6 2.1 bitcast_convert_fusion.1
  477.8 0.9 copy-done.1
  478.6 1.3 copy.42
  479.9 1.6 copy-done
  481.6 2.0 copy.43
  483.6 1.0 copy.44
  (6 shorter events, 0.0 us)
Async XLA Ops:
  275.9 72.5 %copy-start.7 = (f32[8,1024]{1,0:T(8,128)S(1)}, f32[8,1024]{1,0:T(8,128)}, u32[]{:S(2)}) copy-start(f32[8,1024]{1,0:T(8,128)} %get-tuple-element.125) | copy-start | bytes 98308
  275.9 72.5 %copy-start.8 = (f32[8,1024]{1,0:T(8,128)S(1)}, f32[8,1024]{1,0:T(8,128)}, u32[]{:S(2)}) copy-start(f32[8,1024]{1,0:T(8,128)} %get-tuple-element.124) | copy-start | bytes 98308
  430.6 41.2 %copy-start.5 = (bf16[4,128,1024]{2,1,0:T(8,128)(2,1)S(1)}, bf16[4,128,1024]{2,1,0:T(8,128)(2,1)}, u32[]{:S(2)}) copy-start(bf16[4,128,1024]{2,1,0:T(8,128)(2,1)} %get-tuple-element.128) | copy-start | bytes 3145732
  471.8 1.5 copy-start.3
  473.4 1.6 copy-start.2
  473.4 2.3 copy-start.6
  475.6 3.0 copy-start.1
  478.6 2.9 copy-start
  481.6 2.0 copy-start.4
